TPU v7x, 32 devices: a whole 2x2x4 slice. The times are simulated.
32 devices in a mesh: dp: 8 (over y, x, core), seq: 4 (over z).
Axes of the slice: x: 2, y: 2, z: 4, core: 2. Of those that a mesh axis runs over, the one named last changes fastest.
Arguments:
- inputs: bfloat16 [8, 1024, 1024], P('dp', 'seq'), may hold values from -6 to 6
- lengths: int32 [8], P('dp'), may hold values from 640 to 1024, as said below
- token_mask: int32 [8, 1024], P('dp', 'seq'), may hold values from 0 to 1, as said below
- mask_vector: bfloat16 [1024], P(('dp', 'seq')), may hold values from -6 to 6
- gain_first: bfloat16 [1024], P(('dp', 'seq')), may hold values from 0.25 to 1.75
- first_up: bfloat16 [1024, 4096], P(('dp', 'seq')), may hold values from -0.1875 to 0.1875
- first_down: bfloat16 [4096, 1024], P(('dp', 'seq')), may hold values from -0.1875 to 0.1875
- gain_attend: bfloat16 [1024], P(('dp', 'seq')), may hold values from 0.25 to 1.75
- joint_proj: bfloat16 [1024, 3072], P(('dp', 'seq')), may hold values from -0.25 to 0.25
- attend_out: bfloat16 [1024, 1024], P(('dp', 'seq')), may hold values from -4 to 4
- gain_conv: bfloat16 [1024], P(('dp', 'seq')), may hold values from 0.25 to 1.75
- conv_pair: bfloat16 [1024, 2048], P(('dp', 'seq')), may hold values from -0.1875 to 0.1875
- conv_taps: bfloat16 [1024, 31], P(('dp', 'seq')), may hold values from -1 to 1
- batch_scale: bfloat16 [1024], P(('dp', 'seq')), may hold values from 0.25 to 1.75
- batch_shift: bfloat16 [1024], P(('dp', 'seq')), may hold values from -3 to 3
- conv_out: bfloat16 [1024, 1024], P(('dp', 'seq')), may hold values from -0.25 to 0.25
- gain_second: bfloat16 [1024], P(('dp', 'seq')), may hold values from 0.25 to 1.75
- second_up: bfloat16 [1024, 4096], P(('dp', 'seq')), may hold values from -0.1875 to 0.1875
- second_down: bfloat16 [4096, 1024], P(('dp', 'seq')), may hold values from -0.1875 to 0.1875
- gain_final: bfloat16 [1024], P(('dp', 'seq')), may hold values from 0.25 to 1.75
- cotangent: bfloat16 [8, 1024, 1024], P('dp', 'seq'), may hold values from -6 to 6
Outputs:
- output: bfloat16 [8, 1024, 1024], P('dp', 'seq')
- input_grad: float32 [8, 1024, 1024], P('dp', 'seq')
- mask_vector_grad: float32 [1024], P(('dp', 'seq'))
- gain_first_grad: float32 [1024], P(('dp', 'seq'))
- first_up_grad: float32 [1024, 4096], P(('dp', 'seq'))
- first_down_grad: float32 [4096, 1024], P(('dp', 'seq'))
- gain_attend_grad: float32 [1024], P(('dp', 'seq'))
- joint_proj_grad: float32 [1024, 3072], P(('dp', 'seq'))
- attend_out_grad: float32 [1024, 1024], P(('dp', 'seq'))
- gain_conv_grad: float32 [1024], P(('dp', 'seq'))
- conv_pair_grad: float32 [1024, 2048], P(('dp', 'seq'))
- conv_taps_grad: float32 [1024, 31], P(('dp', 'seq'))
- batch_scale_grad: float32 [1024], P(('dp', 'seq'))
- batch_shift_grad: float32 [1024], P(('dp', 'seq'))
- conv_out_grad: float32 [1024, 1024], P(('dp', 'seq'))
- gain_second_grad: float32 [1024], P(('dp', 'seq'))
- second_up_grad: float32 [1024, 4096], P(('dp', 'seq'))
- second_down_grad: float32 [4096, 1024], P(('dp', 'seq'))
- gain_final_grad: float32 [1024], P(('dp', 'seq'))
- moment_mean: float32 [1024], replicated
- moment_var: float32 [1024], replicated
Inputs may be any that keep to these rules, and one draw needn't show every extreme that they name: `lengths`: valid frames of each item, which come first; one item has exactly 1024 and one exactly 640. `token_mask`: 1 marks a frame whose input is replaced by the mask vector.
All inputs are finite; a program needn't handle non-finite values.
Results may differ from a plain program's by a relative error of at most 0.025.
Values may be sent and summed in bfloat16 or wider, within the bound.
No kernel may reach another device: no remote copies, remote signals or barrier semaphores. Data moves between devices by JAX's collectives and lax.ppermute only.
A program may use at most 384 MiB of HBM per device.

v0:
```python
import math

import jax
import jax.numpy as jnp
from jax import lax
from jax.sharding import PartitionSpec as P

HEADS = 16
HEAD_DIM = 64


epsilon = 1e-05


def shortened(shard):

    def short(part):
        return part.astype(jnp.bfloat16) if part.dtype == jnp.float32 else part

    return jax.tree.map(short, shard)


def with_halo(shard, sides, width):
    for axis, dim in sides:
        size, length = (lax.axis_size(axis), shard.shape[dim])
        up = [(i, (i + 1) % size) for i in range(size - 1)]
        down = [(j, i) for i, j in up]
        last = lax.slice_in_dim(shard, length - width, length, axis=dim)
        first = lax.slice_in_dim(shard, 0, width, axis=dim)
        before = lax.ppermute(last, axis, up)
        after = lax.ppermute(first, axis, down)
        shard = jnp.concatenate([before, shard, after], axis=dim)
    return shard


def product(left_side, right_side):
    return jnp.dot(left_side, right_side, preferred_element_type=jnp.float32)


def product_lead(left_side, right_side):
    return lax.dot_general(
        left_side, right_side, (((0,), (0,)), ((), ())), preferred_element_type=jnp.float32
    )


def product_tail(left_side, right_side):
    return lax.dot_general(
        left_side, right_side, (((1,), (1,)), ((), ())), preferred_element_type=jnp.float32
    )


def norm_forward(values, norm_gain):
    centered = values - jnp.mean(values, axis=-1, keepdims=True)
    inverse = lax.rsqrt(jnp.mean(centered * centered, axis=-1, keepdims=True) + epsilon)
    normal = centered * inverse
    return (normal * norm_gain, normal, inverse)


def norm_backward(grad_out, norm_gain, normal, inverse):
    scaled = grad_out * norm_gain
    grad_in = inverse * (
        scaled
        - jnp.mean(scaled, axis=-1, keepdims=True)
        - normal * jnp.mean(scaled * normal, axis=-1, keepdims=True)
    )
    return (grad_in, jnp.sum(grad_out * normal, axis=0))


def silu_slope(hidden):
    sigmoid_rows = jax.nn.sigmoid(hidden)
    return sigmoid_rows * (1.0 + hidden * (1.0 - sigmoid_rows))


def fetch_weights(members):
    return jax.tree.map(
        lambda part, own: part.astype(own.dtype),
        lax.all_gather(shortened(members), ("dp", "seq"), axis=0, tiled=True),
        members,
    )


def fetch_again(members):
    return jax.tree.map(
        lambda part, own: part.astype(own.dtype),
        lax.all_gather(shortened(members), ("dp", "seq"), axis=0, tiled=True),
        members,
    )


def return_grads(members):
    return lax.psum_scatter(members, ("dp", "seq"), scatter_dimension=0, tiled=True)


def ffn_forward(values, norm_gain, upward, downward):
    normed, normal, inverse = norm_forward(values, norm_gain.astype(jnp.float32))
    normed_low = normed.astype(jnp.bfloat16)
    hidden = product(normed_low, upward)
    active = jax.nn.silu(hidden).astype(jnp.bfloat16)
    return (values + 0.5 * product(active, downward), (normed_low, normal, inverse, hidden, active))


def ffn_backward(grad_rows, norm_gain, upward, downward, stored):
    normed_low, normal, inverse, hidden, active = stored
    grad_branch = (0.5 * grad_rows).astype(jnp.bfloat16)
    grad_down = product_lead(active, grad_branch)
    grad_hidden = (product_tail(grad_branch, downward) * silu_slope(hidden)).astype(jnp.bfloat16)
    grad_up = product_lead(normed_low, grad_hidden)
    grad_in, grad_gain = norm_backward(
        product_tail(grad_hidden, upward), norm_gain.astype(jnp.float32), normal, inverse
    )
    return (grad_rows + grad_in, grad_gain, grad_up, grad_down)


def attention_forward(values, length, norm_gain, joint_proj, attend_out):
    normed, normal, inverse = norm_forward(values, norm_gain.astype(jnp.float32))
    normed_low = normed.astype(jnp.bfloat16)
    joined = product(normed_low, joint_proj).astype(jnp.bfloat16)
    model_width = joined.shape[1] // 3
    frames = joined.shape[0]
    key_rows, value_rows = (
        lax.all_gather(joined[:, model_width : 2 * model_width], "seq", axis=0, tiled=True),
        lax.all_gather(joined[:, 2 * model_width :], "seq", axis=0, tiled=True),
    )
    key_valid = jnp.arange(key_rows.shape[0]) < length
    score_scale = 1.0 / math.sqrt(HEAD_DIM)

    def one_head(head_index, carried):
        mixture, log_totals = carried
        column = head_index * HEAD_DIM
        query_rows = lax.dynamic_slice_in_dim(joined, column, HEAD_DIM, 1)
        key_block = lax.dynamic_slice_in_dim(key_rows, column, HEAD_DIM, 1)
        value_block = lax.dynamic_slice_in_dim(value_rows, column, HEAD_DIM, 1)
        scores = jnp.where(
            key_valid[None, :], product_tail(query_rows, key_block) * score_scale, -1e30
        )
        largest = jnp.max(scores, axis=-1, keepdims=True)
        exponent = jnp.exp(scores - largest)
        totals = jnp.sum(exponent, axis=-1, keepdims=True)
        weights = (exponent / totals).astype(jnp.bfloat16)
        mixture = lax.dynamic_update_slice_in_dim(mixture, product(weights, value_block), column, 1)
        log_totals = lax.dynamic_update_slice_in_dim(
            log_totals, largest + jnp.log(totals), head_index, 1
        )
        return (mixture, log_totals)

    mixture, log_totals = lax.fori_loop(
        0,
        HEADS,
        one_head,
        (jnp.zeros((frames, model_width), jnp.float32), jnp.zeros((frames, HEADS), jnp.float32)),
    )
    mixed_low = mixture.astype(jnp.bfloat16)
    output = values + product(mixed_low, attend_out)
    return (
        output,
        (
            normed_low,
            normal,
            inverse,
            joined,
            key_rows,
            value_rows,
            key_valid,
            log_totals,
            mixed_low,
        ),
    )


def attention_backward(grad_rows, norm_gain, joint_proj, attend_out, stored):
    normed_low, normal, inverse, joined, key_rows, value_rows, key_valid, log_totals, mixed_low = (
        stored
    )
    grad_branch = grad_rows.astype(jnp.bfloat16)
    grad_out = product_lead(mixed_low, grad_branch)
    grad_mixed = product_tail(grad_branch, attend_out).astype(jnp.bfloat16)
    frames, model_width = grad_mixed.shape
    score_scale = 1.0 / math.sqrt(HEAD_DIM)

    def one_head(head_index, carried):
        grad_query, grad_key, grad_value = carried
        column = head_index * HEAD_DIM
        query_rows = lax.dynamic_slice_in_dim(joined, column, HEAD_DIM, 1)
        key_block = lax.dynamic_slice_in_dim(key_rows, column, HEAD_DIM, 1)
        value_block = lax.dynamic_slice_in_dim(value_rows, column, HEAD_DIM, 1)
        grad_block = lax.dynamic_slice_in_dim(grad_mixed, column, HEAD_DIM, 1)
        scores = jnp.where(
            key_valid[None, :], product_tail(query_rows, key_block) * score_scale, -1e30
        )
        weights = jnp.exp(scores - lax.dynamic_slice_in_dim(log_totals, head_index, 1, 1))
        grad_weights = product_tail(grad_block, value_block)
        grad_scores = (
            weights * (grad_weights - jnp.sum(weights * grad_weights, axis=-1, keepdims=True))
        ).astype(jnp.bfloat16)
        grad_query = lax.dynamic_update_slice_in_dim(
            grad_query, product(grad_scores, key_block) * score_scale, column, 1
        )
        grad_key = lax.dynamic_update_slice_in_dim(
            grad_key, product_lead(grad_scores, query_rows) * score_scale, column, 1
        )
        grad_value = lax.dynamic_update_slice_in_dim(
            grad_value, product_lead(weights.astype(jnp.bfloat16), grad_block), column, 1
        )
        return (grad_query, grad_key, grad_value)

    key_count = key_rows.shape[0]
    grad_query, grad_key, grad_value = lax.fori_loop(
        0,
        HEADS,
        one_head,
        (
            jnp.zeros((frames, model_width), jnp.float32),
            jnp.zeros((key_count, model_width), jnp.float32),
            jnp.zeros((key_count, model_width), jnp.float32),
        ),
    )
    grad_key, grad_value = (
        lax.psum_scatter(
            grad_key.astype(jnp.bfloat16), "seq", scatter_dimension=0, tiled=True
        ).astype(jnp.float32),
        lax.psum_scatter(
            grad_value.astype(jnp.bfloat16), "seq", scatter_dimension=0, tiled=True
        ).astype(jnp.float32),
    )
    grad_joined = jnp.concatenate([grad_query, grad_key, grad_value], axis=1).astype(jnp.bfloat16)
    grad_joint = product_lead(normed_low, grad_joined)
    grad_in, grad_gain = norm_backward(
        product_tail(grad_joined, joint_proj), norm_gain.astype(jnp.float32), normal, inverse
    )
    return (grad_rows + grad_in, grad_gain, grad_joint, grad_out)


def conv_forward(
    values, valid_rows, norm_gain, conv_pair, conv_taps, batch_scale, batch_shift, conv_out
):
    normed, normal, inverse = norm_forward(values, norm_gain.astype(jnp.float32))
    normed_low = normed.astype(jnp.bfloat16)
    paired = product(normed_low, conv_pair)
    model_width = paired.shape[1] // 2
    frames = paired.shape[0]
    sigmoid_rows = jax.nn.sigmoid(paired[:, model_width:])
    gated_rows = (paired[:, :model_width] * sigmoid_rows * valid_rows).astype(jnp.bfloat16)
    half_width = conv_taps.shape[1] // 2
    widened = with_halo(gated_rows, (("seq", 0),), half_width)
    taps_float = conv_taps.astype(jnp.float32)
    mixture = jnp.zeros((frames, model_width), jnp.float32)
    for offset in range(conv_taps.shape[1]):
        mixture = mixture + widened[offset : offset + frames] * taps_float[:, offset]
    sum_rows, frame_count = lax.psum(
        (jnp.sum(mixture * valid_rows, axis=0), jnp.sum(valid_rows)), ("dp", "seq")
    )
    batch_mean = sum_rows / frame_count
    deviation = (mixture - batch_mean) * valid_rows
    batch_var = lax.psum(jnp.sum(deviation * deviation, axis=0), ("dp", "seq")) / frame_count
    inverse_std = lax.rsqrt(batch_var + epsilon)
    normal_batch = (mixture - batch_mean) * inverse_std
    shaped = normal_batch * batch_scale.astype(jnp.float32) + batch_shift.astype(jnp.float32)
    active = jax.nn.silu(shaped).astype(jnp.bfloat16)
    output = values + product(active, conv_out)
    stored = (
        normed_low,
        normal,
        inverse,
        paired,
        sigmoid_rows,
        widened,
        normal_batch,
        inverse_std,
        shaped,
        active,
    )
    return (output, stored, (batch_mean, batch_var, frame_count))


def conv_backward(
    grad_rows,
    valid_rows,
    norm_gain,
    conv_pair,
    conv_taps,
    batch_scale,
    conv_out,
    stored,
    frame_count,
):
    (
        normed_low,
        normal,
        inverse,
        paired,
        sigmoid_rows,
        widened,
        normal_batch,
        inverse_std,
        shaped,
        active,
    ) = stored
    grad_branch = grad_rows.astype(jnp.bfloat16)
    grad_out = product_lead(active, grad_branch)
    grad_shaped = product_tail(grad_branch, conv_out) * silu_slope(shaped) * valid_rows
    total_shift, total_scale = lax.psum(
        (jnp.sum(grad_shaped, axis=0), jnp.sum(grad_shaped * normal_batch, axis=0)), ("dp", "seq")
    )
    scale_float = batch_scale.astype(jnp.float32)
    grad_mixture = (
        inverse_std
        * valid_rows
        * (
            grad_shaped * scale_float
            - scale_float * (total_shift + normal_batch * total_scale) / frame_count
        )
    ).astype(jnp.bfloat16)
    half_width = conv_taps.shape[1] // 2
    grad_rims = with_halo(grad_mixture, (("seq", 0),), half_width)
    taps_float = conv_taps.astype(jnp.float32)
    frames, model_width = grad_mixture.shape
    widened_float = widened.astype(jnp.float32)
    grad_float = grad_mixture.astype(jnp.float32)
    grad_gated = jnp.zeros((frames, model_width), jnp.float32)
    tap_grads = []
    for offset in range(conv_taps.shape[1]):
        lower_edge = 2 * half_width - offset
        grad_gated = (
            grad_gated + grad_rims[lower_edge : lower_edge + frames] * taps_float[:, offset]
        )
        tap_grads.append(jnp.sum(widened_float[offset : offset + frames] * grad_float, axis=0))
    grad_taps = jnp.stack(tap_grads, axis=1)
    grad_left = grad_gated * sigmoid_rows * valid_rows
    grad_right = (
        grad_gated * paired[:, :model_width] * sigmoid_rows * (1.0 - sigmoid_rows) * valid_rows
    )
    grad_paired = jnp.concatenate([grad_left, grad_right], axis=1).astype(jnp.bfloat16)
    grad_pair = product_lead(normed_low, grad_paired)
    grad_in, grad_gain = norm_backward(
        product_tail(grad_paired, conv_pair), norm_gain.astype(jnp.float32), normal, inverse
    )
    return (
        grad_rows + grad_in,
        grad_gain,
        grad_pair,
        grad_taps,
        grad_out,
        total_scale,
        total_shift,
    )


def per_device(
    inputs,
    lengths,
    token_mask,
    mask_vector,
    gain_first,
    first_up,
    first_down,
    gain_attend,
    joint_proj,
    attend_out,
    gain_conv,
    conv_pair,
    conv_taps,
    batch_scale,
    batch_shift,
    conv_out,
    gain_second,
    second_up,
    second_down,
    gain_final,
    cotangent,
):
    frames = inputs.shape[1]
    model_width = inputs.shape[2]
    length = lengths[0]
    positions = lax.axis_index("seq") * frames + jnp.arange(frames)
    valid_rows = (positions < length).astype(jnp.float32)[:, None]
    masked_float = (token_mask[0] > 0).astype(jnp.float32)[:, None]
    front_set = fetch_weights(
        (mask_vector, gain_first, first_up, first_down, gain_attend, joint_proj, attend_out)
    )
    start_rows = jnp.where(
        masked_float > 0.0, front_set[0].astype(jnp.float32)[None, :], inputs[0].astype(jnp.float32)
    )
    values, first_stored = ffn_forward(start_rows, front_set[1], front_set[2], front_set[3])
    values, attend_stored = attention_forward(
        values, length, front_set[4], front_set[5], front_set[6]
    )
    back_set = fetch_weights(
        (
            gain_conv,
            conv_pair,
            conv_taps,
            batch_scale,
            batch_shift,
            conv_out,
            gain_second,
            second_up,
            second_down,
            gain_final,
        )
    )
    values, conv_stored, batch_stats = conv_forward(
        values,
        valid_rows,
        back_set[0],
        back_set[1],
        back_set[2],
        back_set[3],
        back_set[4],
        back_set[5],
    )
    values, second_stored = ffn_forward(values, back_set[6], back_set[7], back_set[8])
    final_gain = back_set[9].astype(jnp.float32)
    normed, normal, inverse = norm_forward(values, final_gain)
    output = (normed * valid_rows).astype(jnp.bfloat16)
    back_needs = (
        back_set[0],
        back_set[1],
        back_set[2],
        back_set[3],
        back_set[5],
        back_set[6],
        back_set[7],
        back_set[8],
    )
    front_needs = (
        front_set[1],
        front_set[2],
        front_set[3],
        front_set[4],
        front_set[5],
        front_set[6],
    )
    grad_rows, grad_final = norm_backward(
        cotangent[0].astype(jnp.float32) * valid_rows, final_gain, normal, inverse
    )
    back_needs = fetch_again(
        (
            gain_conv,
            conv_pair,
            conv_taps,
            batch_scale,
            conv_out,
            gain_second,
            second_up,
            second_down,
        )
    )
    grad_rows, grad_gain_two, grad_up_two, grad_down_two = ffn_backward(
        grad_rows, back_needs[5], back_needs[6], back_needs[7], second_stored
    )
    grad_rows, grad_gain_conv, grad_pair, grad_taps, grad_conv_out, total_scale, total_shift = (
        conv_backward(
            grad_rows,
            valid_rows,
            back_needs[0],
            back_needs[1],
            back_needs[2],
            back_needs[3],
            back_needs[4],
            conv_stored,
            batch_stats[2],
        )
    )
    back_grads = return_grads(
        (
            grad_gain_conv,
            grad_pair,
            grad_taps,
            grad_conv_out,
            grad_gain_two,
            grad_up_two,
            grad_down_two,
            grad_final,
        )
    )
    front_needs = fetch_again(
        (gain_first, first_up, first_down, gain_attend, joint_proj, attend_out)
    )
    grad_rows, grad_gain_attend, grad_joint, grad_attend_out = attention_backward(
        grad_rows, front_needs[3], front_needs[4], front_needs[5], attend_stored
    )
    grad_rows, grad_gain_one, grad_up_one, grad_down_one = ffn_backward(
        grad_rows, front_needs[0], front_needs[1], front_needs[2], first_stored
    )
    input_grad = grad_rows * (1.0 - masked_float)
    mask_grad = jnp.sum(grad_rows * masked_float, axis=0)
    front_grads = return_grads(
        (
            mask_grad,
            grad_gain_one,
            grad_up_one,
            grad_down_one,
            grad_gain_attend,
            grad_joint,
            grad_attend_out,
        )
    )
    shards = lax.axis_size(("dp", "seq"))
    own_rows = model_width // shards
    own_start = lax.axis_index(("dp", "seq")) * own_rows
    scale_grad = lax.dynamic_slice_in_dim(total_scale, own_start, own_rows)
    shift_grad = lax.dynamic_slice_in_dim(total_shift, own_start, own_rows)
    batch_mean, batch_var, frame_count = batch_stats
    moment_var = batch_var * frame_count / (frame_count - 1.0)
    return (
        output[None],
        input_grad[None],
        front_grads[0],
        front_grads[1],
        front_grads[2],
        front_grads[3],
        front_grads[4],
        front_grads[5],
        front_grads[6],
        back_grads[0],
        back_grads[1],
        back_grads[2],
        scale_grad,
        shift_grad,
        back_grads[3],
        back_grads[4],
        back_grads[5],
        back_grads[6],
        back_grads[7],
        batch_mean,
        moment_var,
    )


def solution(mesh):
    in_specs = (
        P("dp", "seq", None),
        P("dp"),
        P("dp", "seq"),
        P(("dp", "seq")),
        P(("dp", "seq")),
        P(("dp", "seq"), None),
        P(("dp", "seq"), None),
        P(("dp", "seq")),
        P(("dp", "seq"), None),
        P(("dp", "seq"), None),
        P(("dp", "seq")),
        P(("dp", "seq"), None),
        P(("dp", "seq"), None),
        P(("dp", "seq")),
        P(("dp", "seq")),
        P(("dp", "seq"), None),
        P(("dp", "seq")),
        P(("dp", "seq"), None),
        P(("dp", "seq"), None),
        P(("dp", "seq")),
        P("dp", "seq", None),
    )
    out_specs = (
        P("dp", "seq", None),
        P("dp", "seq", None),
        P(("dp", "seq")),
        P(("dp", "seq")),
        P(("dp", "seq"), None),
        P(("dp", "seq"), None),
        P(("dp", "seq")),
        P(("dp", "seq"), None),
        P(("dp", "seq"), None),
        P(("dp", "seq")),
        P(("dp", "seq"), None),
        P(("dp", "seq"), None),
        P(("dp", "seq")),
        P(("dp", "seq")),
        P(("dp", "seq"), None),
        P(("dp", "seq")),
        P(("dp", "seq"), None),
        P(("dp", "seq"), None),
        P(("dp", "seq")),
        P(),
        P(),
    )
    return jax.shard_map(
        per_device, mesh=mesh, in_specs=in_specs, out_specs=out_specs, check_vma=False
    )
```

profile of v0, /device:TPU:0, one launch (start us, length us, event | category | flops | bytes accessed | tf_op | source)
XLA Modules:
  0.0 3291.2 jit_solution(7819539050051754860)
XLA Ops:
  16.2 42.5 %all-reduce.17 = (bf16[1024]{0:T(1024)(128)(2,1)S(1)}, bf16[1024]{0:T(1024)(128)(2,1)S(1)}, bf16[1024]{0:T(1024)(128)(2,1)S(1)}, bf16[1024]{0:T(1024)(128)(2,1)S...) all-reduce(bf16[1024]{0:T(1024)(128)(2,1)S(1)} %dynamic-update-slic, ...), channel_id=1, replica_groups=mesh['dp'=8,'seq'=4] {'dp','seq'}, use_global_device_ids=true, to_apply=%add | all-reduce | flops 8192 | bytes 32768
  62.8 28.5 all-gather.11.cloned.1.call-done
  99.4 70.9 %all-gather.13.cloned.1.call-done = bf16[4096,1024]{1,0:T(8,128)(2,1)} async-done(((bf16[128,1024]{1,0:T(8,128)(2,1)}), bf16[4096,1024]{1,0:T(8,128)(2,1)}) %all-gather.13.cloned.1.call-update) | async-done | bytes 8388624 | tf_op jit(solution)/shard_map/all_gather | solution.py:77
  177.7 63.6 %all-gather.15.cloned.1.call-done = bf16[1024,3072]{1,0:T(8,128)(2,1)} async-done(((bf16[32,3072]{1,0:T(8,128)(2,1)}), bf16[1024,3072]{1,0:T(8,128)(2,1)}) %all-gather.15.cloned.1.call-update) | async-done | bytes 6291472 | tf_op jit(solution)/shard_map/all_gather | solution.py:77
  252.9 72.1 %all_gather.82 = bf16[1024,31]{1,0:T(8,128)(2,1)S(1)} all-gather(bf16[32,31]{1,0:T(8,128)(2,1)S(1)} %copy-done.62), channel_id=1, replica_groups=mesh['dp'=8,'seq'=4] {'dp','seq'}, dimensions={0}, use_global_device_ids=true | all-gather | bytes 65472 | tf_op jit(solution)/shard_map/all_gather | solution.py:77
  343.5 83.4 %while.34 = (s32[]{:T(128)}, bf16[256,1024]{0,1:T(8,128)(2,1)S(1)}, f32[256,16]{0,1:T(8,128)}, bf16[256,3072]{1,0:T(8,128)(2,1)}, bf16[1024,1024]{1,0:T(8,128)(2...) while((s32[]{:T(128)}, bf16[256,1024]{0,1:T(8,128)(2,1)S(1)}, ...), condition=%wide.region_7.8_spmd.clone, body=%wide.region_4.7_spmd.clone.sunk | while | flops 69206792 | bytes 3814612 | solution.py:146
  429.7 36.0 %all-gather.23.cloned.1.call-done = bf16[1024,2048]{1,0:T(8,128)(2,1)} async-done(((bf16[32,2048]{1,0:T(8,128)(2,1)}), bf16[1024,2048]{1,0:T(8,128)(2,1)}) %all-gather.23.cloned.1.call-update) | async-done | bytes 4194320 | tf_op jit(solution)/shard_map/all_gather | solution.py:77
  485.7 39.6 %all-reduce.16 = (f32[1024]{0:T(1024)S(1)}, f32[]{:T(128)}) all-reduce(f32[1024]{0:T(1024)S(1)} %get-tuple-element.540, f32[]{:T(128)} %fusion.190), channel_id=1, replica_groups=mesh['dp'=8,'seq'=4] {'dp','seq'}, use_global_device_ids=true, to_apply=%region_11.12 | all-reduce | flops 1025 | bytes 8200 | tf_op jit(solution)/shard_map/psum | solution.py:249
  526.8 40.8 %psum.37 = f32[1024]{0:T(1024)S(1)} all-reduce(f32[1024]{0:T(1024)S(1)} %multiply_reduce_fusion.11), channel_id=1, replica_groups=mesh['dp'=8,'seq'=4] {'dp','seq'}, use_global_device_ids=true, to_apply=%region_15.16 | all-reduce | flops 1024 | bytes 8192 | tf_op jit(solution)/shard_map/psum | solution.py:254
  571.7 31.4 all-gather.27.cloned.1.call-done
  610.8 71.1 %all-gather.29.cloned.1.call-done = bf16[4096,1024]{1,0:T(8,128)(2,1)} async-done(((bf16[128,1024]{1,0:T(8,128)(2,1)}), bf16[4096,1024]{1,0:T(8,128)(2,1)}) %all-gather.29.cloned.1.call-update) | async-done | bytes 8388624 | tf_op jit(solution)/shard_map/all_gather | solution.py:77
  707.8 39.3 %all-reduce.15 = (f32[1024]{0:T(1024)}, f32[1024]{0:T(1024)}) all-reduce(f32[1024]{0:T(1024)S(1)} %get-tuple-element.450, f32[1024]{0:T(1024)S(1)} %get-tuple-element.449), channel_id=1, replica_groups=mesh['dp'=8,'seq'=4] {'dp','seq'}, use_global_device_ids=true, to_apply=%region_27.28 | all-reduce | flops 2048 | bytes 16384 | tf_op jit(solution)/shard_map/psum | solution.py:301
  789.7 161.9 %while.35 = (s32[]{:T(128)}, bf16[256,1024]{0,1:T(8,128)(2,1)}, bf16[1024,1024]{0,1:T(8,128)(2,1)}, bf16[1024,1024]{0,1:T(8,128)(2,1)}, bf16[256,3072]{1,0:T(8,1...) while((s32[]{:T(128)}, bf16[256,1024]{0,1:T(8,128)(2,1)}, ...), condition=%wide.region_32.33_spmd.clone, body=%wide.region_30.32_spmd.clone.sunk | while | flops 170214144 | bytes 9513204 | solution.py:207
  970.7 25.7 reduce-scatter.16.cloned.1.call-done
  996.4 45.5 %reduce-scatter.14.cloned.1.call-done = bf16[256,1024]{0,1:T(8,128)(2,1)} async-done(((bf16[1024,1024]{0,1:T(8,128)(2,1)}), bf16[256,1024]{0,1:T(8,128)(2,1)}) %reduce-scatter.14.cloned.1.call-update) | async-done | bytes 524304 | tf_op jit(solution)/shard_map/reduce_scatter | solution.py:218
  1118.5 40.0 %all-reduce.14 = (f32[1024]{0:T(1024)S(1)}, f32[1024]{0:T(1024)S(1)}, f32[1024]{0:T(1024)S(1)}, f32[1024]{0:T(1024)S(1)}, f32[1024]{0:T(1024)S(1)}, /*index=5*/f32[1024]{0:T(1024)S(1)}) all-reduce(f32[1024]{0:T(1024)S(1)} %get-tuple-element.536, ...), channel_id=4, replica_groups=mesh['dp'=8,'seq'=4] {'dp','seq'}, use_global_device_ids=true, to_apply=%region_40.41.clone | all-reduce | flops 6144 | bytes 49152
  1178.1 147.3 %reduce-scatter.28.cloned.1.call-done = f32[32,1024]{1,0:T(8,128)} async-done(((f32[1024,1024]{1,0:T(8,128)}), f32[32,1024]{1,0:T(8,128)}) %reduce-scatter.28.cloned.1.call-update) | async-done | bytes 131088 | tf_op jit(solution)/shard_map/reduce_scatter | solution.py:91
  1325.4 149.7 %reduce-scatter.24.cloned.1.call-done = f32[32,1024]{1,0:T(8,128)} async-done(((f32[1024,1024]{1,0:T(8,128)}), f32[32,1024]{1,0:T(8,128)}) %reduce-scatter.24.cloned.1.call-update) | async-done | bytes 131088 | tf_op jit(solution)/shard_map/reduce_scatter | solution.py:91
  1475.1 187.4 %reduce-scatter.26.cloned.1.call-done = f32[32,2048]{1,0:T(8,128)} async-done(((f32[1024,2048]{1,0:T(8,128)}), f32[32,2048]{1,0:T(8,128)}) %reduce-scatter.26.cloned.1.call-update) | async-done | bytes 262160 | tf_op jit(solution)/shard_map/reduce_scatter | solution.py:91
  1662.5 160.5 %reduce-scatter.22.cloned.1.call-done = f32[32,3072]{1,0:T(8,128)} async-done(((f32[1024,3072]{1,0:T(8,128)}), f32[32,3072]{1,0:T(8,128)}) %reduce-scatter.22.cloned.1.call-update) | async-done | bytes 393232 | tf_op jit(solution)/shard_map/reduce_scatter | solution.py:91
  1823.0 366.1 %reduce-scatter.30.cloned.1.call-done = f32[32,4096]{1,0:T(8,128)} async-done(((f32[1024,4096]{1,0:T(8,128)}), f32[32,4096]{1,0:T(8,128)}) %reduce-scatter.30.cloned.1.call-update) | async-done | bytes 524304 | tf_op jit(solution)/shard_map/reduce_scatter | solution.py:91
  2189.1 365.1 %reduce-scatter.32.cloned.1.call-done = f32[128,1024]{1,0:T(8,128)} async-done(((f32[4096,1024]{1,0:T(8,128)}), f32[128,1024]{1,0:T(8,128)}) %reduce-scatter.32.cloned.1.call-update) | async-done | bytes 524304 | tf_op jit(solution)/shard_map/reduce_scatter | solution.py:91
  2554.1 364.9 %reduce-scatter.18.cloned.1.call-done = f32[32,4096]{1,0:T(8,128)} async-done(((f32[1024,4096]{1,0:T(8,128)}), f32[32,4096]{1,0:T(8,128)}) %reduce-scatter.18.cloned.1.call-update) | async-done | bytes 524304 | tf_op jit(solution)/shard_map/reduce_scatter | solution.py:91
  2919.0 365.1 %reduce-scatter.20.cloned.1.call-done = f32[128,1024]{1,0:T(8,128)} async-done(((f32[4096,1024]{1,0:T(8,128)}), f32[128,1024]{1,0:T(8,128)}) %reduce-scatter.20.cloned.1.call-update) | async-done | bytes 524304 | tf_op jit(solution)/shard_map/reduce_scatter | solution.py:91
  (545 shorter events, 520.8 us)
Async XLA Ops:
  7.2 84.1 %all-gather.11.cloned.1.call-start = ((), (), s32[]{:S(2)}) async-start(), calls=%async_computation.11 | async-start | bytes 8650752 | tf_op jit(solution)/shard_map/all_gather | solution.py:77
  7.9 162.4 %all-gather.13.cloned.1.call-start = ((), (), s32[]{:S(2)}) async-start(), calls=%async_computation.12 | async-start | bytes 8650752 | tf_op jit(solution)/shard_map/all_gather | solution.py:77
  8.7 232.7 %all-gather.15.cloned.1.call-start = ((), (), s32[]{:S(2)}) async-start(), calls=%async_computation.13 | async-start | bytes 6488064 | tf_op jit(solution)/shard_map/all_gather | solution.py:77
  9.4 320.8 %all-gather.17.cloned.1.call-start = ((), (), s32[]{:S(2)}) async-start(), calls=%async_computation.14 | async-start | bytes 2621440 | tf_op jit(solution)/shard_map/all_gather | solution.py:121
  248.2 95.2 %all-gather.19.cloned.1.call-start = ((), (), s32[]{:S(2)}) async-start(), calls=%async_computation.15 | async-start | bytes 2621440 | tf_op jit(solution)/shard_map/all_gather | solution.py:122
  248.8 178.0 %all-gather.21.cloned.1.call-start = ((), (), s32[]{:S(2)}) async-start(), calls=%async_computation.16 | async-start | bytes 2162688 | tf_op jit(solution)/shard_map/all_gather | solution.py:77
  249.4 216.3 %all-gather.23.cloned.1.call-start = ((), (), s32[]{:S(2)}) async-start(), calls=%async_computation.17 | async-start | bytes 4325376 | tf_op jit(solution)/shard_map/all_gather | solution.py:77
  250.1 318.7 %all-gather.25.cloned.1.call-start = ((), (), s32[]{:S(2)}) async-start(), calls=%async_computation.18 | async-start | bytes 2162688 | tf_op jit(solution)/shard_map/all_gather | solution.py:77
  250.9 352.2 %all-gather.27.cloned.1.call-start = ((), (), s32[]{:S(2)}) async-start(), calls=%async_computation.19 | async-start | bytes 8650752 | tf_op jit(solution)/shard_map/all_gather | solution.py:77
  251.6 430.2 %all-gather.29.cloned.1.call-start = ((), (), s32[]{:S(2)}) async-start(), calls=%async_computation.20 | async-start | bytes 8650752 | tf_op jit(solution)/shard_map/all_gather | solution.py:77
  252.2 744.1 %reduce-scatter.16.cloned.1.call-start = ((), (), s32[]{:S(2)}) async-start(), calls=%async_computation.22 | async-start | bytes 2621440 | tf_op jit(solution)/shard_map/reduce_scatter | solution.py:221
  470.9 10.0 collective-permute-start.1
  472.2 8.7 collective-permute-start
  757.0 5.8 collective-permute-start.2
  951.7 90.1 %reduce-scatter.14.cloned.1.call-start = ((), (), s32[]{:S(2)}) async-start(), calls=%async_computation.21 | async-start | bytes 2621440 | tf_op jit(solution)/shard_map/reduce_scatter | solution.py:218
  952.5 225.7 %reduce-scatter.34.cloned.1.call-start = ((), (), s32[]{:S(2)}) async-start(), calls=%async_computation.31 | async-start | bytes 540672
  956.7 368.7 %reduce-scatter.28.cloned.1.call-start = ((), (), s32[]{:S(2)}) async-start(), calls=%async_computation.28 | async-start | bytes 4325376 | tf_op jit(solution)/shard_map/reduce_scatter | solution.py:91
  961.0 514.1 %reduce-scatter.24.cloned.1.call-start = ((), (), s32[]{:S(2)}) async-start(), calls=%async_computation.26 | async-start | bytes 4325376 | tf_op jit(solution)/shard_map/reduce_scatter | solution.py:91
  964.8 697.7 %reduce-scatter.26.cloned.1.call-start = ((), (), s32[]{:S(2)}) async-start(), calls=%async_computation.27 | async-start | bytes 8650752 | tf_op jit(solution)/shard_map/reduce_scatter | solution.py:91
  970.5 852.5 %reduce-scatter.22.cloned.1.call-start = ((), (), s32[]{:S(2)}) async-start(), calls=%async_computation.25 | async-start | bytes 12976128 | tf_op jit(solution)/shard_map/reduce_scatter | solution.py:91
  1049.5 1139.5 %reduce-scatter.30.cloned.1.call-start = ((), (), s32[]{:S(2)}) async-start(), calls=%async_computation.29 | async-start | bytes 17301504 | tf_op jit(solution)/shard_map/reduce_scatter | solution.py:91
  1060.6 1493.6 %reduce-scatter.32.cloned.1.call-start = ((), (), s32[]{:S(2)}) async-start(), calls=%async_computation.30 | async-start | bytes 17301504 | tf_op jit(solution)/shard_map/reduce_scatter | solution.py:91
  1072.8 1846.3 %reduce-scatter.18.cloned.1.call-start = ((), (), s32[]{:S(2)}) async-start(), calls=%async_computation.23 | async-start | bytes 17301504 | tf_op jit(solution)/shard_map/reduce_scatter | solution.py:91
  1097.3 2186.8 %reduce-scatter.20.cloned.1.call-start = ((), (), s32[]{:S(2)}) async-start(), calls=%async_computation.24 | async-start | bytes 17301504 | tf_op jit(solution)/shard_map/reduce_scatter | solution.py:91
  (76 other events, 2711.2 us)
Sparse Core Ops, SparseCore 0:
  11.0 80.3 all-gather.10
  94.2 76.0 all-gather.12
  173.2 68.1 all-gather.14
  248.3 47.5 all-gather.16
  297.9 45.4 all-gather.18
  346.2 55.4 all-gather.20
  404.7 60.9 all-gather.22
  468.6 55.1 all-gather.24
  526.8 76.2 all-gather.26
  605.8 75.9 all-gather.28
  951.8 44.4 reduce-scatter.15
  998.6 43.1 reduce-scatter.13
  1044.6 133.4 reduce-scatter.33
  1180.9 144.4 reduce-scatter.27
  1328.2 146.8 reduce-scatter.23
  1477.9 184.4 reduce-scatter.25
  1670.0 152.9 reduce-scatter.21
  1825.7 363.2 reduce-scatter.29
  2191.9 362.1 reduce-scatter.31
  2556.8 362.1 reduce-scatter.17
  2921.9 362.1 reduce-scatter.19
where the time goes:
time: 3300 us; the launch traced here: 3290 us
  waiting for transfers between devices  2520 us (76%)
  matrix products  323 us (10%)
  blocking collectives  274 us (8%)
  local copies, waits for them, and re-layouts  74 us (2%)
  other arithmetic  73 us (2%)
    reduce_scatter x8, waiting for transfers between devices, return_grads(): lax.psum_scatter(members, ('dp', 'seq'), scatter_dimension=0, tiled=True)  2110 us
    all_gather x8, waiting for transfers between devices, fetch_weights(): lax.all_gather(shortened(members), ('dp', 'seq'), axis=0, tiled=True)  301 us
    dot_general x40, matrix products, product_lead(): lax.dot_general(left_side, right_side, (((0,), (0,)), ((), ())), preferre...  116 us
    dot_general x56, matrix products, product_tail(): lax.dot_general(left_side, right_side, (((1,), (1,)), ((), ())), preferre...  108 us
    dot_general x40, matrix products, product(): return jnp.dot(left_side, right_side, preferred_element_type=jnp.float32)  98.7 us
    unnamed x2, blocking collectives  82.5 us
    all_gather x1, blocking collectives, fetch_weights(): lax.all_gather(shortened(members), ('dp', 'seq'), axis=0, tiled=True)  72.1 us
  transfers between devices with their start and end apart: 25, of which 20 were waited for; matrix products, arithmetic and copies ran while one was open for 7% of the time, Pallas kernels for 0%

commit v1 on v0

v1 whole, which is shorter than its diff:
```python
import functools

import jax
import jax.numpy as jnp
from jax import lax
from jax.experimental import pallas as pl
from jax.experimental.pallas import tpu as pltpu
from jax.sharding import PartitionSpec as P

HEADS = 16
HEAD_DIM = 64
epsilon = 1e-05
f32 = jnp.float32
bf16 = jnp.bfloat16


def product(left_side, right_side):
    return jnp.dot(left_side, right_side, preferred_element_type=f32)


def product_lead(left_side, right_side):
    return lax.dot_general(
        left_side, right_side, (((0,), (0,)), ((), ())), preferred_element_type=f32
    )


def product_tail(left_side, right_side):
    return lax.dot_general(
        left_side, right_side, (((1,), (1,)), ((), ())), preferred_element_type=f32
    )


def axis_bits(axis):
    size = lax.axis_size(axis)
    return [1 << i for i in range(size.bit_length() - 1)]


def swap(values, axis, bit):
    return lax.ppermute(values, axis, [(i, i ^ bit) for i in range(lax.axis_size(axis))])


def bit_of(axis, bit):
    return (lax.axis_index(axis) & bit) // bit


def all_bits():
    return [("dp", b) for b in axis_bits("dp")] + [("seq", b) for b in axis_bits("seq")]


def pick(array, axis, index):
    return lax.dynamic_index_in_dim(array, index, axis, keepdims=False)


def gather_small(part):
    whole = part
    for axis, bit in [("seq", b) for b in axis_bits("seq")] + [("dp", b) for b in axis_bits("dp")]:
        other = swap(whole, axis, bit)
        upper = bit_of(axis, bit) > 0
        whole = jnp.concatenate(
            [jnp.where(upper, other, whole), jnp.where(upper, whole, other)], axis=0
        )
    return whole


def sum_small(values):
    for axis, bit in all_bits():
        values = values + swap(values, axis, bit)
    return values


def scatter_small(values):
    for axis, bit in [("dp", b) for b in axis_bits("dp")[::-1]] + [
        ("seq", b) for b in axis_bits("seq")[::-1]
    ]:
        view = values.reshape((2, values.shape[0] // 2) + values.shape[1:])
        mine = bit_of(axis, bit)
        values = pick(view, 0, mine) + swap(pick(view, 0, 1 - mine), axis, bit)
    return values


def merge_moments(count, mean, square):
    packed = jnp.stack([jnp.broadcast_to(count, mean.shape), mean, square])
    for axis, bit in all_bits():
        other = swap(packed, axis, bit)
        upper = bit_of(axis, bit) > 0
        low = jnp.where(upper, other, packed)
        high = jnp.where(upper, packed, other)
        total = low[0] + high[0]
        share = high[0] / jnp.maximum(total, 1.0)
        delta = high[1] - low[1]
        packed = jnp.stack(
            [
                total,
                low[1] + delta * share,
                low[2] + high[2] + delta * delta * (low[0] * share),
            ]
        )
    return packed[0, 0], packed[1], packed[2]


def group_bits():
    return axis_bits("dp")[1:]


def owner_columns(rows_of_lhs):
    tokens, rows = rows_of_lhs.shape
    groups = lax.axis_size("dp") // 2
    return rows_of_lhs.reshape(tokens, groups, 2, rows // (2 * groups))


def grad_job(lhs, rhs, share_rows):
    core = bit_of("dp", 1)
    cols = owner_columns(lhs)
    mine, other = pick(cols, 2, core), pick(cols, 2, 1 - core)
    if share_rows:
        lhs_all = jnp.concatenate([mine, swap(other, "dp", 1)], axis=0)
        rhs_all = jnp.concatenate([rhs, swap(rhs, "dp", 1)], axis=0)
        return lhs_all, rhs_all
    return mine, other, rhs


def rows_product(cols, rhs):
    return product_lead(cols.reshape(cols.shape[0], -1), rhs).astype(bf16)


def split_bit(array, axis, size, bit):
    shape = array.shape
    return array.reshape(shape[:axis] + (size // (2 * bit), 2, bit) + shape[axis + 1 :])


def halve_cols(cols, bit, groups):
    view = split_bit(cols, 1, groups, bit)
    mine = bit_of("dp", 2 * bit)
    flat = lambda a: a.reshape((a.shape[0], groups // 2) + cols.shape[2:])
    return flat(pick(view, 2, mine)), flat(pick(view, 2, 1 - mine))


def add_pair(keep, other, dtype=bf16):
    return (keep.astype(f32) + other.astype(f32)).astype(dtype)


def remaining_position(done, bit):
    return bit >> sum(1 for d in done if d < bit)


def scatter_job(job, rows):
    groups = lax.axis_size("dp") // 2
    seq = lax.axis_size("seq")
    bits = [b // 2 for b in group_bits()]
    halves = []
    shared = len(job) == 2
    rhs = job[-1]
    width = rhs.shape[1] // 2
    for half in range(2):
        order = bits if half == 0 else bits[::-1]
        part = rhs[:, half * width : (half + 1) * width]
        if shared:
            first, rest = order[0], order[1:]
            mine, other = halve_cols(job[0], first, groups)
            got = swap(rows_product(other, part), "dp", 2 * first)
            keep = rows_product(mine, part)
            done = [first]
        else:
            got = swap(rows_product(job[1], part), "dp", 1)
            keep = rows_product(job[0], part)
            rest, done = order, []
        size = groups >> len(done)
        keep, got = (a.reshape(size, -1, width) for a in (keep, got))
        for bit in rest:
            place = remaining_position(done, bit)
            view_keep = split_bit(keep, 0, size, place)
            view_got = split_bit(got, 0, size, place)
            mine = bit_of("dp", 2 * bit)
            send = add_pair(pick(view_keep, 1, 1 - mine), pick(view_got, 1, 1 - mine))
            keep = add_pair(pick(view_keep, 1, mine), pick(view_got, 1, mine))
            size //= 2
            got = swap(send, "dp", 2 * bit).reshape(size, -1, width)
            keep = keep.reshape(size, -1, width)
            done.append(bit)
        halves.append((keep.reshape(seq, rows, width), got.reshape(seq, rows, width)))
    keep = got = None
    size = seq
    done = []
    for bit in axis_bits("seq"):
        place = remaining_position(done, bit)
        mine = bit_of("seq", bit)

        def side(which):
            if keep is None:
                return jnp.concatenate(
                    [
                        add_pair(
                            pick(split_bit(a, 0, size, place), 1, which),
                            pick(split_bit(b, 0, size, place), 1, which),
                        )
                        for a, b in halves
                    ],
                    axis=-1,
                )
            return add_pair(
                pick(split_bit(keep, 0, size, place), 1, which),
                pick(split_bit(got, 0, size, place), 1, which),
            )

        send, kept = side(1 - mine), side(mine)
        size //= 2
        got = swap(send, "seq", bit).reshape(size, rows, -1)
        keep = kept.reshape(size, rows, -1)
        done.append(bit)
    return add_pair(keep[0], got[0], f32)


def gather_line(own):
    seq = lax.axis_size("seq")
    ups, downs = [own], [own]
    for step in range(seq - 1):
        ups.append(lax.ppermute(ups[-1], "seq", [(i, i + 1) for i in range(seq - 1)]))
        downs.append(lax.ppermute(downs[-1], "seq", [(i + 1, i) for i in range(seq - 1)]))
    me = lax.axis_index("seq")
    blocks = [own]
    for r in range(1, seq):
        blocks.append(jnp.where(me + r < seq, downs[r], ups[seq - r]))
    return jnp.stack(blocks)


def scatter_line(blocks):
    seq = lax.axis_size("seq")
    up = down = None
    for step in range(seq - 1, 0, -1):
        message_up, message_down = blocks[step], blocks[seq - step]
        if up is not None:
            message_up = add_pair(message_up, up)
            message_down = add_pair(message_down, down)
        up = lax.ppermute(message_up, "seq", [(i, i + 1) for i in range(seq - 1)])
        down = lax.ppermute(message_down, "seq", [(i + 1, i) for i in range(seq - 1)])
    total = blocks[0].astype(f32)
    if up is not None:
        total = total + up.astype(f32) + down.astype(f32)
    return total


def with_halo(shard, width):
    size, length = lax.axis_size("seq"), shard.shape[0]
    up = [(i, i + 1) for i in range(size - 1)]
    down = [(i + 1, i) for i in range(size - 1)]
    before = lax.ppermute(shard[length - width :], "seq", up)
    after = lax.ppermute(shard[:width], "seq", down)
    return jnp.concatenate([before, shard, after], axis=0)


def norm_forward(values, norm_gain):
    centered = values - jnp.mean(values, axis=-1, keepdims=True)
    inverse = lax.rsqrt(jnp.mean(centered * centered, axis=-1, keepdims=True) + epsilon)
    normal = centered * inverse
    return (normal * norm_gain, normal, inverse)


def norm_backward(grad_out, norm_gain, normal, inverse):
    scaled = grad_out * norm_gain
    grad_in = inverse * (
        scaled
        - jnp.mean(scaled, axis=-1, keepdims=True)
        - normal * jnp.mean(scaled * normal, axis=-1, keepdims=True)
    )
    return (grad_in, jnp.sum(grad_out * normal, axis=0))


def silu_slope(hidden):
    sigmoid_rows = jax.nn.sigmoid(hidden)
    return sigmoid_rows * (1.0 + hidden * (1.0 - sigmoid_rows))


def ffn_forward(values, norm_gain, upward, downward):
    normed, normal, inverse = norm_forward(values, norm_gain)
    normed_low = normed.astype(bf16)
    hidden = product(normed_low, upward)
    active = jax.nn.silu(hidden).astype(bf16)
    return (values + 0.5 * product(active, downward), (normed_low, normal, inverse, hidden, active))


def ffn_backward(grad_rows, norm_gain, upward, downward, stored):
    normed_low, normal, inverse, hidden, active = stored
    grad_branch = (0.5 * grad_rows).astype(bf16)
    grad_hidden = (product_tail(grad_branch, downward) * silu_slope(hidden)).astype(bf16)
    grad_in, grad_gain = norm_backward(
        product_tail(grad_hidden, upward), norm_gain, normal, inverse
    )
    rows = upward.shape[0] // (lax.axis_size("dp") * lax.axis_size("seq"))
    rows_down = downward.shape[0] // (lax.axis_size("dp") * lax.axis_size("seq"))
    grad_down = scatter_job(grad_job(active, grad_branch, True), rows_down)
    grad_up = scatter_job(grad_job(normed_low, grad_hidden, True), rows)
    return (grad_rows + grad_in, grad_gain, grad_up, grad_down)


def key_valid(offsets_ref, rows, keys):
    count = keys // rows
    spots = []
    for block in range(count):
        spots.append(offsets_ref[block] + lax.broadcasted_iota(jnp.int32, (rows, 1), 0))
    return jnp.concatenate(spots, axis=0) < offsets_ref[count]


def head_mask(block, head):
    lanes = lax.broadcasted_iota(jnp.int32, block.shape, 1)
    inside = (lanes < HEAD_DIM) if head == 0 else (lanes >= HEAD_DIM)
    return jnp.where(inside, block, jnp.zeros_like(block))


def attend_kernel(rows, offsets_ref, query_ref, key_ref, value_ref, mixture_ref, total_ref):
    keys = key_ref[...]
    values = value_ref[...]
    query = query_ref[...] * jnp.asarray(HEAD_DIM**-0.5, bf16)
    valid = key_valid(offsets_ref, rows, keys.shape[0])
    halves = []
    for head in range(2):
        scores = product_tail(keys, head_mask(query, head))
        scores = jnp.where(valid, scores, -1e30)
        largest = jnp.max(scores, axis=0, keepdims=True)
        exponent = jnp.exp(scores - largest)
        totals = jnp.sum(exponent, axis=0, keepdims=True)
        weights = (exponent * (1.0 / totals)).astype(bf16)
        mixed = product_lead(values, weights)
        halves.append(mixed[head * HEAD_DIM : (head + 1) * HEAD_DIM])
        total_ref[0, head : head + 1, :] = largest + jnp.log(totals)
    mixture_ref[...] = jnp.concatenate(halves, axis=0).T.astype(bf16)


def attend_back_kernel(
    rows,
    offsets_ref,
    query_ref,
    key_ref,
    value_ref,
    total_ref,
    grad_ref,
    query_grad_ref,
    key_grad_ref,
    value_grad_ref,
):
    keys = key_ref[...]
    values = value_ref[...]
    grad = grad_ref[...]
    query = query_ref[...] * jnp.asarray(HEAD_DIM**-0.5, bf16)
    valid = key_valid(offsets_ref, rows, keys.shape[0])
    halves = []
    key_grad = value_grad = None
    for head in range(2):
        query_head = head_mask(query, head)
        grad_head = head_mask(grad, head)
        scores = product_tail(keys, query_head)
        scores = jnp.where(valid, scores, -1e30)
        weights = jnp.exp(scores - total_ref[0, head : head + 1, :])
        grad_weights = product_tail(values, grad_head)
        inner = jnp.sum(weights * grad_weights, axis=0, keepdims=True)
        grad_scores = (weights * (grad_weights - inner)).astype(bf16)
        key_part = product(grad_scores, query_head)
        value_part = product(weights.astype(bf16), grad_head)
        key_grad = key_part if key_grad is None else key_grad + key_part
        value_grad = value_part if value_grad is None else value_grad + value_part
        query_part = product_lead(keys, grad_scores)
        halves.append(query_part[head * HEAD_DIM : (head + 1) * HEAD_DIM])
    query_grad = jnp.concatenate(halves, axis=0).T * HEAD_DIM**-0.5
    query_grad_ref[...] = query_grad.astype(bf16)
    key_grad_ref[...] = key_grad.astype(bf16)
    value_grad_ref[...] = value_grad.astype(bf16)


def attend(offsets, query, key_value):
    rows, width = query.shape
    keys = key_value.shape[0]
    pairs = width // 128
    return pl.pallas_call(
        functools.partial(attend_kernel, rows),
        grid_spec=pltpu.PrefetchScalarGridSpec(
            num_scalar_prefetch=1,
            grid=(pairs,),
            in_specs=[
                pl.BlockSpec((rows, 128), lambda i, o: (0, i)),
                pl.BlockSpec((keys, 128), lambda i, o: (0, i)),
                pl.BlockSpec((keys, 128), lambda i, o: (0, i + pairs)),
            ],
            out_specs=[
                pl.BlockSpec((rows, 128), lambda i, o: (0, i)),
                pl.BlockSpec((1, 2, rows), lambda i, o: (i, 0, 0)),
            ],
        ),
        out_shape=[
            jax.ShapeDtypeStruct((rows, width), bf16),
            jax.ShapeDtypeStruct((pairs, 2, rows), f32),
        ],
        compiler_params=pltpu.CompilerParams(vmem_limit_bytes=48 << 20),
        name="attend",
    )(offsets, query, key_value, key_value)


def attend_back(offsets, query, key_value, totals, grad):
    rows, width = query.shape
    keys = key_value.shape[0]
    pairs = width // 128
    row_spec = pl.BlockSpec((rows, 128), lambda i, o: (0, i))
    key_spec = pl.BlockSpec((keys, 128), lambda i, o: (0, i))
    return pl.pallas_call(
        functools.partial(attend_back_kernel, rows),
        grid_spec=pltpu.PrefetchScalarGridSpec(
            num_scalar_prefetch=1,
            grid=(pairs,),
            in_specs=[
                row_spec,
                key_spec,
                pl.BlockSpec((keys, 128), lambda i, o: (0, i + pairs)),
                pl.BlockSpec((1, 2, rows), lambda i, o: (i, 0, 0)),
                row_spec,
            ],
            out_specs=[row_spec, key_spec, key_spec],
        ),
        out_shape=[
            jax.ShapeDtypeStruct((rows, width), bf16),
            jax.ShapeDtypeStruct((keys, width), bf16),
            jax.ShapeDtypeStruct((keys, width), bf16),
        ],
        compiler_params=pltpu.CompilerParams(vmem_limit_bytes=48 << 20),
        name="attend_back",
    )(offsets, query, key_value, key_value, totals, grad)


def attention_forward(values, length, norm_gain, joint_proj, attend_out):
    normed, normal, inverse = norm_forward(values, norm_gain)
    normed_low = normed.astype(bf16)
    frames, model_width = normed_low.shape
    seq = lax.axis_size("seq")
    normed_all = gather_line(normed_low).reshape(seq * frames, model_width)
    query = product(normed_low, joint_proj[:, :model_width]).astype(bf16)
    key_value = product(normed_all, joint_proj[:, model_width:]).astype(bf16)
    starts = ((lax.axis_index("seq") + jnp.arange(seq)) % seq) * frames
    offsets = jnp.concatenate([starts, length[None]]).astype(jnp.int32)
    mixed_low, totals = attend(offsets, query, key_value)
    output = values + product(mixed_low, attend_out)
    stored = (normed_low, normal, inverse, normed_all, query, key_value, offsets, totals, mixed_low)
    return (output, stored)


def attention_backward(grad_rows, norm_gain, joint_proj, attend_out, stored):
    normed_low, normal, inverse, normed_all, query, key_value, offsets, totals, mixed_low = stored
    frames, model_width = normed_low.shape
    shards = lax.axis_size("dp") * lax.axis_size("seq")
    rows = model_width // shards
    grad_branch = grad_rows.astype(bf16)
    grad_mixed = product_tail(grad_branch, attend_out).astype(bf16)
    grad_query, grad_key, grad_value = attend_back(offsets, query, key_value, totals, grad_mixed)
    part = product_tail(grad_key, joint_proj[:, model_width : 2 * model_width]) + product_tail(
        grad_value, joint_proj[:, 2 * model_width :]
    )
    blocks = part.astype(bf16).reshape(-1, frames, model_width)
    grad_normed = scatter_line(blocks) + product_tail(grad_query, joint_proj[:, :model_width])
    grad_in, grad_gain = norm_backward(grad_normed, norm_gain, normal, inverse)
    grad_out = scatter_job(grad_job(mixed_low, grad_branch, True), rows)
    grad_joint = [
        scatter_job(grad_job(normed_low, grad_query, True), rows),
        scatter_job(grad_job(normed_all, grad_key, False), rows),
        scatter_job(grad_job(normed_all, grad_value, False), rows),
    ]
    return (grad_rows + grad_in, grad_gain, jnp.concatenate(grad_joint, axis=1), grad_out)


def conv_forward(
    values, valid_rows, norm_gain, conv_pair, taps_float, batch_scale, batch_shift, conv_out
):
    normed, normal, inverse = norm_forward(values, norm_gain)
    normed_low = normed.astype(bf16)
    paired = product(normed_low, conv_pair)
    model_width = paired.shape[1] // 2
    frames = paired.shape[0]
    sigmoid_rows = jax.nn.sigmoid(paired[:, model_width:])
    gated_rows = (paired[:, :model_width] * sigmoid_rows * valid_rows).astype(bf16)
    half_width = taps_float.shape[1] // 2
    widened = with_halo(gated_rows, half_width)
    mixture = jnp.zeros((frames, model_width), f32)
    for offset in range(taps_float.shape[1]):
        mixture = mixture + widened[offset : offset + frames] * taps_float[:, offset]
    own_count = jnp.sum(valid_rows)
    own_mean = jnp.sum(mixture * valid_rows, axis=0) / jnp.maximum(own_count, 1.0)
    own_dev = (mixture - own_mean) * valid_rows
    frame_count, batch_mean, square = merge_moments(
        own_count, own_mean, jnp.sum(own_dev * own_dev, axis=0)
    )
    batch_var = square / frame_count
    inverse_std = lax.rsqrt(batch_var + epsilon)
    normal_batch = (mixture - batch_mean) * inverse_std
    shaped = normal_batch * batch_scale + batch_shift
    active = jax.nn.silu(shaped).astype(bf16)
    output = values + product(active, conv_out)
    stored = (
        normed_low,
        normal,
        inverse,
        paired,
        sigmoid_rows,
        widened,
        normal_batch,
        inverse_std,
        shaped,
        active,
    )
    return (output, stored, (batch_mean, batch_var, frame_count))


def conv_backward(
    grad_rows,
    valid_rows,
    norm_gain,
    conv_pair,
    taps_float,
    scale_float,
    conv_out,
    stored,
    frame_count,
):
    (
        normed_low,
        normal,
        inverse,
        paired,
        sigmoid_rows,
        widened,
        normal_batch,
        inverse_std,
        shaped,
        active,
    ) = stored
    grad_branch = grad_rows.astype(bf16)
    grad_shaped = product_tail(grad_branch, conv_out) * silu_slope(shaped) * valid_rows
    total_shift, total_scale = sum_small(
        jnp.stack([jnp.sum(grad_shaped, axis=0), jnp.sum(grad_shaped * normal_batch, axis=0)])
    )
    grad_mixture = (
        inverse_std
        * valid_rows
        * (
            grad_shaped * scale_float
            - scale_float * (total_shift + normal_batch * total_scale) / frame_count
        )
    ).astype(bf16)
    taps = taps_float.shape[1]
    half_width = taps // 2
    grad_rims = with_halo(grad_mixture, half_width)
    frames, model_width = grad_mixture.shape
    widened_float = widened.astype(f32)
    grad_float = grad_mixture.astype(f32)
    grad_gated = jnp.zeros((frames, model_width), f32)
    tap_grads = []
    for offset in range(taps):
        lower_edge = 2 * half_width - offset
        grad_gated = (
            grad_gated + grad_rims[lower_edge : lower_edge + frames] * taps_float[:, offset]
        )
        tap_grads.append(jnp.sum(widened_float[offset : offset + frames] * grad_float, axis=0))
    grad_taps = jnp.stack(tap_grads, axis=1)
    grad_left = grad_gated * sigmoid_rows * valid_rows
    grad_right = (
        grad_gated * paired[:, :model_width] * sigmoid_rows * (1.0 - sigmoid_rows) * valid_rows
    )
    grad_paired = jnp.concatenate([grad_left, grad_right], axis=1).astype(bf16)
    grad_in, grad_gain = norm_backward(
        product_tail(grad_paired, conv_pair), norm_gain, normal, inverse
    )
    rows = model_width // (lax.axis_size("dp") * lax.axis_size("seq"))
    grad_out = scatter_job(grad_job(active, grad_branch, True), rows)
    grad_pair = scatter_job(grad_job(normed_low, grad_paired, True), rows)
    return (
        grad_rows + grad_in,
        grad_gain,
        grad_pair,
        grad_taps,
        grad_out,
        total_scale,
        total_shift,
    )


def fetch_weight(part):
    return lax.all_gather(part, ("dp", "seq"), axis=0, tiled=True)


def per_device(
    inputs,
    lengths,
    token_mask,
    mask_vector,
    gain_first,
    first_up,
    first_down,
    gain_attend,
    joint_proj,
    attend_out,
    gain_conv,
    conv_pair,
    conv_taps,
    batch_scale,
    batch_shift,
    conv_out,
    gain_second,
    second_up,
    second_down,
    gain_final,
    cotangent,
):
    frames = inputs.shape[1]
    model_width = inputs.shape[2]
    taps = conv_taps.shape[1]
    length = lengths[0]
    positions = lax.axis_index("seq") * frames + jnp.arange(frames)
    valid_rows = (positions < length).astype(f32)[:, None]
    masked_float = (token_mask[0] > 0).astype(f32)[:, None]

    vectors = (
        mask_vector,
        gain_first,
        gain_attend,
        gain_conv,
        gain_second,
        gain_final,
        batch_scale,
        batch_shift,
    )
    own_small = jnp.concatenate([jnp.stack(vectors, axis=0), conv_taps.T], axis=0)
    count = own_small.shape[0]
    small = gather_small(own_small[None])
    small = jnp.transpose(small, (1, 0, 2)).reshape(count, model_width).astype(f32)
    vector_mask, g_first, g_attend, g_conv, g_second, g_final, scale_float, shift_float = (
        small[i] for i in range(8)
    )
    taps_float = small[8:].T

    start_rows = jnp.where(masked_float > 0.0, vector_mask[None, :], inputs[0].astype(f32))
    up_one, down_one = fetch_weight(first_up), fetch_weight(first_down)
    values, first_stored = ffn_forward(start_rows, g_first, up_one, down_one)
    joint_all, outward_all = fetch_weight(joint_proj), fetch_weight(attend_out)
    values, attend_stored = attention_forward(values, length, g_attend, joint_all, outward_all)
    pair_all, conv_out_all = fetch_weight(conv_pair), fetch_weight(conv_out)
    values, conv_stored, batch_stats = conv_forward(
        values, valid_rows, g_conv, pair_all, taps_float, scale_float, shift_float, conv_out_all
    )
    up_two, down_two = fetch_weight(second_up), fetch_weight(second_down)
    values, second_stored = ffn_forward(values, g_second, up_two, down_two)
    normed, normal, inverse = norm_forward(values, g_final)
    output = (normed * valid_rows).astype(bf16)

    grad_rows, grad_final = norm_backward(
        cotangent[0].astype(f32) * valid_rows, g_final, normal, inverse
    )
    grad_rows, grad_gain_two, grad_up_two, grad_down_two = ffn_backward(
        grad_rows, g_second, up_two, down_two, second_stored
    )
    grad_rows, grad_gain_conv, grad_pair, grad_taps, grad_conv_out, total_scale, total_shift = (
        conv_backward(
            grad_rows,
            valid_rows,
            g_conv,
            pair_all,
            taps_float,
            scale_float,
            conv_out_all,
            conv_stored,
            batch_stats[2],
        )
    )
    grad_rows, grad_gain_attend, grad_joint, grad_attend_out = attention_backward(
        grad_rows, g_attend, joint_all, outward_all, attend_stored
    )
    grad_rows, grad_gain_one, grad_up_one, grad_down_one = ffn_backward(
        grad_rows, g_first, up_one, down_one, first_stored
    )
    input_grad = grad_rows * (1.0 - masked_float)
    mask_grad = jnp.sum(grad_rows * masked_float, axis=0)

    shards = lax.axis_size("dp") * lax.axis_size("seq")
    own_rows = model_width // shards
    sums = jnp.concatenate(
        [
            jnp.stack(
                [
                    mask_grad,
                    grad_gain_one,
                    grad_gain_attend,
                    grad_gain_conv,
                    grad_gain_two,
                    grad_final,
                ]
            ),
            grad_taps.T,
        ],
        axis=0,
    )
    sums = jnp.transpose(sums.reshape(-1, shards, own_rows), (1, 0, 2))
    sums = scatter_small(sums)[0]
    own_start = (lax.axis_index("dp") * lax.axis_size("seq") + lax.axis_index("seq")) * own_rows
    scale_grad = lax.dynamic_slice_in_dim(total_scale, own_start, own_rows)
    shift_grad = lax.dynamic_slice_in_dim(total_shift, own_start, own_rows)
    batch_mean, batch_var, frame_count = batch_stats
    moment_var = batch_var * frame_count / (frame_count - 1.0)
    return (
        output[None],
        input_grad[None],
        sums[0],
        sums[1],
        grad_up_one,
        grad_down_one,
        sums[2],
        grad_joint,
        grad_attend_out,
        sums[3],
        grad_pair,
        sums[6 : 6 + taps].T,
        scale_grad,
        shift_grad,
        grad_conv_out,
        sums[4],
        grad_up_two,
        grad_down_two,
        sums[5],
        batch_mean,
        moment_var,
    )


def solution(mesh):
    both = P(("dp", "seq"))
    rows = P(("dp", "seq"), None)
    frames = P("dp", "seq", None)
    in_specs = (
        frames,
        P("dp"),
        P("dp", "seq"),
        both,
        both,
        rows,
        rows,
        both,
        rows,
        rows,
        both,
        rows,
        rows,
        both,
        both,
        rows,
        both,
        rows,
        rows,
        both,
        frames,
    )
    out_specs = (
        frames,
        frames,
        both,
        both,
        rows,
        rows,
        both,
        rows,
        rows,
        both,
        rows,
        rows,
        both,
        both,
        rows,
        both,
        rows,
        rows,
        both,
        P(),
        P(),
    )
    return jax.shard_map(
        per_device, mesh=mesh, in_specs=in_specs, out_specs=out_specs, check_vma=False
    )
```

time: 3300 us -> 1180 us (0.36)
  waiting for transfers between devices: 2520 us -> 574 us
  blocking collectives: 274 us -> 0 us
  matrix products: 323 us -> 131 us
  starting transfers between devices: 11.2 us -> 134 us
  local copies, waits for them, and re-layouts: 74 us -> 177 us
  Pallas kernels: 0 us -> 37.2 us
    reduce_scatter x10 -> x0, waiting for transfers between devices: 2180 us -> none  [the longest x8 2110 us: return_grads(): lax.psum_scatter(members, ('dp', 'seq'), scatter_dimension=0, tiled=True)]
    ppermute x4 -> x116, waiting for transfers between devices: 4.49 us -> 229 us  [the longest x100 205 us: swap(): lax.ppermute(values, axis, [(i, i ^ bit) for i in range(lax.axis_size(axi...]
    ppermute x4 -> x116, starting transfers between devices: 9.76 us -> 134 us  [the longest x100 85.3 us: swap(): lax.ppermute(values, axis, [(i, i ^ bit) for i in range(lax.axis_size(axi...]
    psum x3 -> x0, blocking collectives: 120 us -> none  [the longest x1 40.8 us: conv_forward(): lax.psum(jnp.sum(deviation * deviation, axis=0), ('dp', 'seq'))]
    unnamed x2 -> x0, blocking collectives: 82.5 us -> none
    dynamic_slice x16 -> x43, local copies, waits for them, and re-layouts: 11.3 us -> 86.2 us  [pick(): return lax.dynamic_index_in_dim(array, index, axis, keepdims=False)]
    dot_general x56 -> x10, matrix products: 108 us -> 35 us  [product_tail(): lax.dot_general(left_side, right_side, (((1,), (1,)), ((), ())), preferre...]
    all_gather x1 -> x0, blocking collectives: 72.1 us -> none  [fetch_weights(): lax.all_gather(shortened(members), ('dp', 'seq'), axis=0, tiled=True)]
  transfers between devices with their start and end apart: 25 -> 124, of which waited for: 20 -> 61; matrix products, arithmetic and copies ran while one was open for 7% -> 34% of each run, Pallas kernels for 0% -> 3%
where the time goes in v1:
time: 1180 us; the launch traced here: 1170 us
  waiting for transfers between devices  574 us (49%)
  local copies, waits for them, and re-layouts  177 us (15%)
  starting transfers between devices  134 us (11%)
  matrix products  131 us (11%)
  other arithmetic  94.4 us (8%)
  Pallas kernels  37.2 us (3%)
  between operations  20 us (2%)
    all_gather x8, waiting for transfers between devices, fetch_weight(): return lax.all_gather(part, ('dp', 'seq'), axis=0, tiled=True)  341 us
    ppermute x100, waiting for transfers between devices, swap(): lax.ppermute(values, axis, [(i, i ^ bit) for i in range(lax.axis_size(axi...  205 us
    dynamic_slice x43, local copies, waits for them, and re-layouts, pick(): return lax.dynamic_index_in_dim(array, index, axis, keepdims=False)  86.2 us
    ppermute x100, starting transfers between devices, swap(): lax.ppermute(values, axis, [(i, i ^ bit) for i in range(lax.axis_size(axi...  85.3 us
    dot_general x40, matrix products, product_lead(): lax.dot_general(left_side, right_side, (((0,), (0,)), ((), ())), preferre...  50.2 us
    dot_general x9, matrix products, product(): return jnp.dot(left_side, right_side, preferred_element_type=f32)  45.9 us
    unnamed x401, local copies, waits for them, and re-layouts  42.1 us
    dot_general x10, matrix products, product_tail(): lax.dot_general(left_side, right_side, (((1,), (1,)), ((), ())), preferre...  35 us
  transfers between devices with their start and end apart: 124, of which 61 were waited for; matrix products, arithmetic and copies ran while one was open for 34% of the time, Pallas kernels for 3%

profile of v1, /device:TPU:0, one launch (start us, length us, event | category | flops | bytes accessed | tf_op | source)
XLA Modules:
  0.0 1168.3 jit_solution(9388212513935338304)
XLA Ops:
  43.1 48.3 %all-gather.9.cloned.1.call-done = bf16[1024,4096]{1,0:T(8,128)(2,1)} async-done(((bf16[32,4096]{1,0:T(8,128)(2,1)}), bf16[1024,4096]{1,0:T(8,128)(2,1)}) %all-gather.9.cloned.1.call-update) | async-done | bytes 8388624 | tf_op jit(solution)/shard_map/all_gather | solution.py:581
  91.4 8.9 multiply_convert_fusion.1
  100.3 70.1 %all-gather.11.cloned.1.call-done = bf16[4096,1024]{1,0:T(8,128)(2,1)} async-done(((bf16[128,1024]{1,0:T(8,128)(2,1)}), bf16[4096,1024]{1,0:T(8,128)(2,1)}) %all-gather.11.cloned.1.call-update) | async-done | bytes 8388624 | tf_op jit(solution)/shard_map/all_gather | solution.py:581
  188.0 9.6 collective-permute-done.5
  213.1 35.3 %all-gather.13.cloned.1.call-done = bf16[1024,3072]{1,0:T(8,128)(2,1)} async-done(((bf16[32,3072]{1,0:T(8,128)(2,1)}), bf16[1024,3072]{1,0:T(8,128)(2,1)}) %all-gather.13.cloned.1.call-update) | async-done | bytes 6291472 | tf_op jit(solution)/shard_map/all_gather | solution.py:581
  258.3 9.9 collective-permute-done.10
  276.4 16.9 %attend.1 = (bf16[256,1024]{1,0:T(8,128)(2,1)S(1)}, f32[8,2,256]{2,1,0:T(2,128)S(1)}) custom-call(s32[5]{0:T(128)S(1)} %pad_add_fusion.offsets_ref, bf16[256,1024]{1,0:T(8,128)(2,1)S(1)} %fusion.22.query_ref, bf16[1024,2048]{1,0:T(8,128)(2,1)S(1)} %fusion.4.key_ref.value_ref, bf16[1024,2048]{1,0:T(8,128)(2,1)S(1)} %fusion.4.key_ref.value_ref), custom_call_target="tpu_custom_call" | custom-call | tf_op jit(solution)/shard_map/attend/pallas_call | solution.py:372
  295.3 11.4 all-gather.15.cloned.1.call-done
  309.7 60.9 %all-gather.17.cloned.1.call-done = bf16[1024,2048]{1,0:T(8,128)(2,1)} async-done(((bf16[32,2048]{1,0:T(8,128)(2,1)}), bf16[1024,2048]{1,0:T(8,128)(2,1)}) %all-gather.17.cloned.1.call-update) | async-done | bytes 4194320 | tf_op jit(solution)/shard_map/all_gather | solution.py:581
  420.4 8.6 constant_dynamic-slice_fusion.52
  463.2 44.7 %all-gather.21.cloned.1.call-done = bf16[1024,4096]{1,0:T(8,128)(2,1)} async-done(((bf16[32,4096]{1,0:T(8,128)(2,1)}), bf16[1024,4096]{1,0:T(8,128)(2,1)}) %all-gather.21.cloned.1.call-update) | async-done | bytes 8388624 | tf_op jit(solution)/shard_map/all_gather | solution.py:581
  507.9 8.4 multiply_convert_fusion
  516.3 70.5 %all-gather.23.cloned.1.call-done = bf16[4096,1024]{1,0:T(8,128)(2,1)} async-done(((bf16[128,1024]{1,0:T(8,128)(2,1)}), bf16[4096,1024]{1,0:T(8,128)(2,1)}) %all-gather.23.cloned.1.call-update) | async-done | bytes 8388624 | tf_op jit(solution)/shard_map/all_gather | solution.py:581
  595.5 6.8 fusion
  616.3 8.6 constant_dynamic-slice_fusion.49
  678.1 20.3 %attend_back.1 = (bf16[256,1024]{1,0:T(8,128)(2,1)S(1)}, bf16[1024,1024]{1,0:T(8,128)(2,1)S(1)}, bf16[1024,1024]{1,0:T(8,128)(2,1)S(1)}) custom-call(s32[5]{0:T(128)S(1)} %pad_add_fusion.offsets_ref, bf16[256,1024]{1,0:T(8,128)(2,1)S(1)} %fusion.22.query_ref, bf16[1024,2048]{1,0:T(8,128)(2,1)} %copy-done, bf16[1024,2048]{1,0:T(8,128)(2,1)} %copy-done, ...), custom_call_target="tpu_custom_call" | custom-call | tf_op jit(solution)/shard_map/attend_back/pallas_call | solution.py:402
  906.0 9.6 collective-permute-done.75
  980.8 7.8 collective-permute-done.88
  1021.7 19.7 %collective-permute-done.113 = bf16[1,1,512,512]{3,2,1,0:T(8,128)(2,1)S(1)} collective-permute-done((bf16[1,1,512,512]{3,2,1,0:T(8,128)(2,1)S(1)}, bf16[1,1,512,512]{3,2,1,0:T(8,128)(2,1)S(1)}, u32[]{:S(2)}, u32[]{:S(2)}) %collective-permute-start.113) | collective-permute-done | bytes 524320 | tf_op jit(solution)/shard_map/ppermute | solution.py:39
  1056.9 9.8 collective-permute-done.114
  1095.1 16.3 %collective-permute-done.40 = bf16[256,2048]{1,0:T(8,128)(2,1)S(1)} collective-permute-done((bf16[256,2048]{1,0:T(8,128)(2,1)S(1)}, bf16[256,2048]{1,0:T(8,128)(2,1)S(1)}, u32[]{:S(2)}, u32[]{:S(2)}) %collective-permute-start.40) | collective-permute-done | bytes 1048608 | tf_op jit(solution)/shard_map/ppermute | solution.py:39
  1125.2 10.6 collective-permute-done.50
  1136.0 7.7 collective-permute-done.42
  1144.7 12.7 %collective-permute-done.51 = bf16[1,1,128,1024]{3,2,0,1:T(8,128)(2,1)S(1)} collective-permute-done((bf16[1,1,128,1024]{3,2,0,1:T(8,128)(2,1)S(1)}, bf16[1,1,128,1024]{3,2,0,1:T(8,128)(2,1)S(1)}, u32[]{:S(2)}, u32[]{:S(2)}) %collective-permute-start.51) | collective-permute-done | bytes 262176 | tf_op jit(solution)/shard_map/ppermute | solution.py:39
  (996 shorter events, 615.1 us)
Async XLA Ops:
  7.2 84.2 %all-gather.9.cloned.1.call-start = ((), (), s32[]{:S(2)}) async-start(), calls=%async_computation | async-start | bytes 8650752 | tf_op jit(solution)/shard_map/all_gather | solution.py:581
  7.9 162.4 %all-gather.11.cloned.1.call-start = ((), (), s32[]{:S(2)}) async-start(), calls=%async_computation.1 | async-start | bytes 8650752 | tf_op jit(solution)/shard_map/all_gather | solution.py:581
  8.7 239.8 %all-gather.13.cloned.1.call-start = ((), (), s32[]{:S(2)}) async-start(), calls=%async_computation.2 | async-start | bytes 6488064 | tf_op jit(solution)/shard_map/all_gather | solution.py:581
  9.4 297.3 %all-gather.15.cloned.1.call-start = ((), (), s32[]{:S(2)}) async-start(), calls=%async_computation.3 | async-start | bytes 2162688 | tf_op jit(solution)/shard_map/all_gather | solution.py:581
  10.0 360.5 %all-gather.17.cloned.1.call-start = ((), (), s32[]{:S(2)}) async-start(), calls=%async_computation.4 | async-start | bytes 4325376 | tf_op jit(solution)/shard_map/all_gather | solution.py:581
  10.6 449.5 %all-gather.19.cloned.1.call-start = ((), (), s32[]{:S(2)}) async-start(), calls=%async_computation.5 | async-start | bytes 2162688 | tf_op jit(solution)/shard_map/all_gather | solution.py:581
  11.2 496.7 %all-gather.21.cloned.1.call-start = ((), (), s32[]{:S(2)}) async-start(), calls=%async_computation.6 | async-start | bytes 8650752 | tf_op jit(solution)/shard_map/all_gather | solution.py:581
  11.9 574.9 %all-gather.23.cloned.1.call-start = ((), (), s32[]{:S(2)}) async-start(), calls=%async_computation.7 | async-start | bytes 8650752 | tf_op jit(solution)/shard_map/all_gather | solution.py:581
  197.6 53.3 %collective-permute-start.9 = (bf16[256,1024]{1,0:T(8,128)(2,1)}, bf16[256,1024]{1,0:T(8,128)(2,1)}, u32[]{:S(2)}, u32[]{:S(2)}) collective-permute-start(bf16[256,1024]{1,0:T(8,128)(2,1)} %collective-permute-done.5), channel_id=1, source_target_pairs={{1,0},{2,1},{3,2},{5,4},{6,5},{7,6},{9,8},{10,9},{11,10},{13,12},{... | collective-permute-start | bytes 1572872 | tf_op jit(solution)/shard_map/ppermute | solution.py:218
  199.8 194.8 %collective-permute-start.36 = (bf16[256,4,128]{2,0,1:T(8,128)(2,1)}, bf16[256,4,128]{2,0,1:T(8,128)(2,1)}, u32[]{:S(2)}, u32[]{:S(2)}) collective-permute-start(bf16[256,4,128]{2,0,1:T(8,128)(2,1)} %get-tuple-element.234), channel_id=1, source_target_pairs={{0,4},{4,0},{8,12},{12,8},{16,20},{20,16},{24,28},{28,24},{1,5},{5... | collective-permute-start | bytes 786440 | tf_op jit(solution)/shard_map/ppermute | solution.py:39
  207.3 187.3 %collective-permute-start.52 = (bf16[256,4,128]{2,0,1:T(8,128)(2,1)}, bf16[256,4,128]{2,0,1:T(8,128)(2,1)}, u32[]{:S(2)}, u32[]{:S(2)}) collective-permute-start(bf16[256,4,128]{2,0,1:T(8,128)(2,1)} %bitcast.954), channel_id=1, source_target_pairs={{0,4},{4,0},{8,12},{12,8},{16,20},{20,16},{24,28},{28,24},{1,5},{5... | collective-permute-start | bytes 786440 | tf_op jit(solution)/shard_map/ppermute | solution.py:39
  386.6 452.2 %collective-permute-start.44 = (bf16[256,4,512]{2,0,1:T(8,128)(2,1)}, bf16[256,4,512]{2,0,1:T(8,128)(2,1)}, u32[]{:S(2)}, u32[]{:S(2)}) collective-permute-start(bf16[256,4,512]{2,0,1:T(8,128)(2,1)} %bitcast.949), channel_id=1, source_target_pairs={{0,4},{4,0},{8,12},{12,8},{16,20},{20,16},{24,28},{28,24},{1,5},{5... | collective-permute-start | bytes 3145736 | tf_op jit(solution)/shard_map/ppermute | solution.py:39
  452.7 272.7 %collective-permute-start.84 = (bf16[256,4,128]{2,0,1:T(8,128)(2,1)}, bf16[256,4,128]{2,0,1:T(8,128)(2,1)}, u32[]{:S(2)}, u32[]{:S(2)}) collective-permute-start(bf16[256,4,128]{2,0,1:T(8,128)(2,1)} %bitcast.952), channel_id=1, source_target_pairs={{0,4},{4,0},{8,12},{12,8},{16,20},{20,16},{24,28},{28,24},{1,5},{5... | collective-permute-start | bytes 786440 | tf_op jit(solution)/shard_map/ppermute | solution.py:39
  454.9 270.5 %collective-permute-start.76 = (bf16[256,4,128]{2,0,1:T(8,128)(2,1)}, bf16[256,4,128]{2,0,1:T(8,128)(2,1)}, u32[]{:S(2)}, u32[]{:S(2)}) collective-permute-start(bf16[256,4,128]{2,0,1:T(8,128)(2,1)} %bitcast.953), channel_id=1, source_target_pairs={{0,4},{4,0},{8,12},{12,8},{16,20},{20,16},{24,28},{28,24},{1,5},{5... | collective-permute-start | bytes 786440 | tf_op jit(solution)/shard_map/ppermute | solution.py:39
  666.2 90.2 %collective-permute-start.93 = (bf16[256,1024]{1,0:T(8,128)(2,1)}, bf16[256,1024]{1,0:T(8,128)(2,1)}, u32[]{:S(2)}, u32[]{:S(2)}) collective-permute-start(bf16[256,1024]{1,0:T(8,128)(2,1)} %copy-done.23), channel_id=1, source_target_pairs={{0,4},{4,0},{8,12},{12,8},{16,20},{20,16},{24,28},{28,24},{1,5},{5... | collective-permute-start | bytes 1572872 | tf_op jit(solution)/shard_map/ppermute | solution.py:39
  666.2 69.1 %collective-permute-start.100 = (bf16[256,4,128]{2,0,1:T(8,128)(2,1)}, bf16[256,4,128]{2,0,1:T(8,128)(2,1)}, u32[]{:S(2)}, u32[]{:S(2)}) collective-permute-start(bf16[256,4,128]{2,0,1:T(8,128)(2,1)} %bitcast.1082), channel_id=1, source_target_pairs={{0,4},{4,0},{8,12},{12,8},{16,20},{20,16},{24,28},{28,24},{1,5},{5... | collective-permute-start | bytes 786440 | tf_op jit(solution)/shard_map/ppermute | solution.py:39
  769.5 232.5 %collective-permute-start.101 = (bf16[256,4096]{1,0:T(8,128)(2,1)S(1)}, bf16[256,4096]{1,0:T(8,128)(2,1)}, u32[]{:S(2)}, u32[]{:S(2)}) collective-permute-start(bf16[256,4096]{1,0:T(8,128)(2,1)S(1)} %copy-done.15), channel_id=1, source_target_pairs={{0,4},{4,0},{8,12},{12,8},{16,20},{20,16},{24,28},{28,24},{1,5},{5... | collective-permute-start | bytes 6291464 | tf_op jit(solution)/shard_map/ppermute | solution.py:39
  838.0 48.5 %collective-permute-start.85 = (bf16[256,2048]{1,0:T(8,128)(2,1)}, bf16[256,2048]{1,0:T(8,128)(2,1)}, u32[]{:S(2)}, u32[]{:S(2)}) collective-permute-start(bf16[256,2048]{1,0:T(8,128)(2,1)} %pad_maximum_fusion.4), channel_id=1, source_target_pairs={{0,4},{4,0},{8,12},{12,8},{16,20},{20,16},{24,28},{28,24},{1,5},{5... | collective-permute-start | bytes 3145736 | tf_op jit(solution)/shard_map/ppermute | solution.py:39
  838.8 54.9 %collective-permute-start.26 = (bf16[256,1024]{1,0:T(8,128)(2,1)}, bf16[256,1024]{1,0:T(8,128)(2,1)}, u32[]{:S(2)}, u32[]{:S(2)}) collective-permute-start(bf16[256,1024]{1,0:T(8,128)(2,1)} %get-tuple-element.155), channel_id=1, source_target_pairs={{0,1},{1,2},{2,3},{4,5},{5,6},{6,7},{8,9},{9,10},{10,11},{12,13},{... | collective-permute-start | bytes 1572872 | tf_op jit(solution)/shard_map/ppermute | solution.py:234
  898.7 112.0 %collective-permute-start.110 = (bf16[1024,512]{1,0:T(8,128)(2,1)}, bf16[1024,512]{1,0:T(8,128)(2,1)}, u32[]{:S(2)}, u32[]{:S(2)}) collective-permute-start(bf16[1024,512]{1,0:T(8,128)(2,1)} %convolution_convert_fusion.10), channel_id=1, source_target_pairs={{0,8},{4,12},{8,0},{12,4},{16,24},{20,28},{24,16},{28,20},{1,9},{5... | collective-permute-start | bytes 3145736 | tf_op jit(solution)/shard_map/ppermute | solution.py:39
  926.8 87.2 %collective-permute-start.112 = (bf16[1024,512]{1,0:T(8,128)(2,1)}, bf16[1024,512]{1,0:T(8,128)(2,1)}, u32[]{:S(2)}, u32[]{:S(2)}) collective-permute-start(bf16[1024,512]{1,0:T(8,128)(2,1)} %convolution_convert_fusion.8), channel_id=1, source_target_pairs={{0,16},{4,20},{8,24},{12,28},{16,0},{20,4},{24,8},{28,12},{1,17},{... | collective-permute-start | bytes 3145736 | tf_op jit(solution)/shard_map/ppermute | solution.py:39
  1004.0 52.4 %collective-permute-start.102 = (bf16[256,2048]{1,0:T(8,128)(2,1)S(1)}, bf16[256,2048]{1,0:T(8,128)(2,1)S(1)}, u32[]{:S(2)}, u32[]{:S(2)}) collective-permute-start(bf16[256,2048]{1,0:T(8,128)(2,1)S(1)} %convolution_convert_fusion.2), channel_id=1, source_target_pairs={{0,8},{4,12},{8,0},{12,4},{16,24},{20,28},{24,16},{28,20},{1,9},{5... | collective-permute-start | bytes 3145736 | tf_op jit(solution)/shard_map/ppermute | solution.py:39
  1010.7 58.4 %collective-permute-start.104 = (bf16[256,2048]{1,0:T(8,128)(2,1)S(1)}, bf16[256,2048]{1,0:T(8,128)(2,1)S(1)}, u32[]{:S(2)}, u32[]{:S(2)}) collective-permute-start(bf16[256,2048]{1,0:T(8,128)(2,1)S(1)} %convolution_convert_fusion), channel_id=1, source_target_pairs={{0,16},{4,20},{8,24},{12,28},{16,0},{20,4},{24,8},{28,12},{1,17},{... | collective-permute-start | bytes 3145736 | tf_op jit(solution)/shard_map/ppermute | solution.py:39
  1021.2 48.5 %collective-permute-start.46 = (bf16[1024,512]{1,0:T(8,128)(2,1)S(1)}, bf16[1024,512]{1,0:T(8,128)(2,1)S(1)}, u32[]{:S(2)}, u32[]{:S(2)}) collective-permute-start(bf16[1024,512]{1,0:T(8,128)(2,1)S(1)} %convolution_convert_fusion.14), channel_id=1, source_target_pairs={{0,8},{4,12},{8,0},{12,4},{16,24},{20,28},{24,16},{28,20},{1,9},{5... | collective-permute-start | bytes 3145736 | tf_op jit(solution)/shard_map/ppermute | solution.py:39
  (289 other events, 5229.5 us)
Sparse Core Ops, SparseCore 0:
  11.0 80.3 all-gather.8
  94.3 75.9 all-gather.10
  173.2 75.1 all-gather.12
  251.2 55.4 all-gather.14
  309.6 60.9 all-gather.16
  373.3 55.0 all-gather.18
  431.3 76.4 all-gather.20
  510.8 75.9 all-gather.22

commit v2 on v1

--- a/solution.py
+++ b/solution.py
@@ -28,6 +28,10 @@
     return lax.dot_general(
         left_side, right_side, (((1,), (1,)), ((), ())), preferred_element_type=f32
     )
+
+
+def tie(*values):
+    return lax.optimization_barrier(values)
 
 
 def axis_bits(axis):
@@ -210,6 +214,399 @@
     return add_pair(keep[0], got[0], f32)
 
 
+def in_steps(model_width):
+    return lax.axis_size("dp") == 8 and lax.axis_size("seq") == 4 and model_width == 1024
+
+
+BLOCK = 512
+
+
+def terms_of(refs, pairs, half, rows, blocks, seq):
+    own, got = (jnp.concatenate([refs[2 * i][...], refs[2 * i + 1][...]], axis=1) for i in (0, 1))
+    rhs = refs[4:]
+    if pairs:
+        rhs = rhs[2 * half : 2 * half + 2]
+    total = product_lead(own, rhs[0][...]) + product_lead(got, rhs[1][...])
+    for block in range(2):
+        for z in range(seq):
+            for j in range(blocks):
+                start = (block * seq + z) * rows
+                yield block, z, j, total[start : start + rows, j * BLOCK : (j + 1) * BLOCK]
+
+
+def job_refs(refs, shape):
+    at = start = 0
+    for rows, blocks, pairs in shape:
+        count = 8 if pairs else 6
+        yield refs[at : at + count], pairs, rows, blocks, start
+        at += count
+        start += rows * blocks
+
+
+def send_kernel(shape, seq, table_ref, *refs):
+    del table_ref
+    outs = refs[-2:]
+    for half in range(2):
+
+        @pl.when(pl.program_id(0) == half)
+        def _():
+            for part, pairs, rows, blocks, start in job_refs(refs, shape):
+                for block, z, j, piece in terms_of(part, pairs, half, rows, blocks, seq):
+                    at = start + j * rows
+                    outs[half][block, z, at : at + rows, :] = piece.astype(bf16)
+
+
+def fold_kernel(shape, seq, table_ref, *refs):
+    del table_ref
+    gots, (sends, keep) = refs[-7:-3], (refs[-3:-1], refs[-1])
+    for half in range(2):
+
+        @pl.when(pl.program_id(0) == half)
+        def _():
+            for part, pairs, rows, blocks, start in job_refs(refs, shape):
+                for block, z, j, piece in terms_of(part, pairs, half, rows, blocks, seq):
+                    at = slice(start + j * rows, start + (j + 1) * rows)
+                    piece = (piece + gots[2 * half + block][0, z, at, :].astype(f32)).astype(bf16)
+                    if block == 0:
+                        sends[half][z, at, :] = piece
+                    else:
+                        keep[0, z, at, :] = piece
+
+
+def split_kernel(bits, bit_ref, keep_ref, *refs):
+    gots, (send_ref, left_ref) = refs[:-2], refs[-2:]
+    mine = bit_ref[0]
+    for half in range(2):
+        for entry in range(send_ref.shape[1]):
+            for ref, side in ((send_ref, 1 - mine), (left_ref, mine)):
+                at = 2 * entry + side if bits == 2 else side
+                if len(gots) == 2:
+                    got = gots[half][at]
+                else:
+                    got = gots[0][half, at]
+                total = keep_ref[half, at].astype(f32) + got.astype(f32)
+                ref[half, entry] = total.astype(bf16)
+
+
+def finish_kernel(shape, keep_ref, got_ref, *outs):
+    start = 0
+    for out, (rows, blocks, _) in zip(outs, shape):
+        for half in range(2):
+            for j in range(blocks):
+                at = slice(start + j * rows, start + (j + 1) * rows)
+                columns = slice((half * blocks + j) * BLOCK, (half * blocks + j + 1) * BLOCK)
+                out[:, columns] = keep_ref[half, 0, at, :].astype(f32) + got_ref[
+                    half, 0, at, :
+                ].astype(f32)
+        start += rows * blocks
+
+
+LIMIT = pltpu.CompilerParams(vmem_limit_bytes=56 << 20)
+
+
+def whole_call(kernel, name, bits, inputs, outs):
+    spec = lambda x: pl.BlockSpec(x.shape, lambda i, *t: (0,) * len(x.shape))
+    size = sum(x.size * x.dtype.itemsize for x in list(inputs) + list(outs))
+    return pl.pallas_call(
+        kernel,
+        grid_spec=pltpu.PrefetchScalarGridSpec(
+            num_scalar_prefetch=len(bits),
+            grid=(1,),
+            in_specs=[spec(x) for x in inputs],
+            out_specs=[spec(o) for o in outs],
+        ),
+        out_shape=outs,
+        compiler_params=LIMIT,
+        cost_estimate=pl.CostEstimate(flops=0, transcendentals=0, bytes_accessed=size),
+        name=name,
+    )(*bits, *inputs)
+
+
+class SmallScatter:
+    def __init__(self, values):
+        self.keep = values
+        self.bits = [("dp", b) for b in axis_bits("dp")[::-1]]
+        self.bits += [("seq", b) for b in axis_bits("seq")[::-1]]
+        self.got = None
+
+    def step(self):
+        if self.got is not None:
+            self.keep = self.keep + self.got
+        if not self.bits:
+            return
+        axis, bit = self.bits.pop(0)
+        view = self.keep.reshape((2, self.keep.shape[0] // 2) + self.keep.shape[1:])
+        mine = bit_of(axis, bit)
+        self.keep, sent = pick(view, 0, mine), pick(view, 0, 1 - mine)
+        self.got = swap(sent, axis, bit)
+
+
+class ModuleScatter:
+    def __init__(self, jobs, name):
+        self.jobs = jobs
+        self.name = name
+        self.shape = tuple((j[4], j[5] // BLOCK, j[3][0] is not j[3][1]) for j in jobs)
+        self.rows = sum(rows * blocks for rows, blocks, _ in self.shape)
+
+    def share(self):
+        self.others = {}
+        for lhs, rhs in ((j[0], j[3]) for j in self.jobs):
+            for array in (lhs, *rhs):
+                if id(array) not in self.others:
+                    self.others[id(array)] = swap(array, "dp", 1)
+
+    def operands(self):
+        specs, args = [], []
+        for lhs, _, tokens, rhs, rows, width in self.jobs:
+            wide = 4 * rows
+            for array in (lhs, self.others[id(lhs)]):
+                for block in range(2):
+                    spec = lambda h, t, block=block: (0, t[h, block])
+                    specs.append(pl.BlockSpec((tokens, wide), spec))
+                    args.append(array)
+            if rhs[0] is rhs[1]:
+                for array in (rhs[0], self.others[id(rhs[0])]):
+                    specs.append(pl.BlockSpec((tokens, width), lambda h, t: (0, h)))
+                    args.append(array)
+            else:
+                for half in rhs:
+                    for array in (half, self.others[id(half)]):
+                        specs.append(pl.BlockSpec((tokens, width), lambda h, t: (0, 0)))
+                        args.append(array)
+        return specs, args
+
+    def call(self, kernel, name, table, more, more_specs, outs, out_specs):
+        specs, args = self.operands()
+        flops = sum(16 * j[2] * 4 * j[4] * j[5] for j in self.jobs)
+        moved = sum(4 * j[2] * (4 * j[4] * 2 + 2 * j[5]) for j in self.jobs)
+        moved += 2 * sum(x.size for x in list(more) + list(outs))
+        return pl.pallas_call(
+            functools.partial(kernel, self.shape, 4),
+            grid_spec=pltpu.PrefetchScalarGridSpec(
+                num_scalar_prefetch=1,
+                grid=(2,),
+                in_specs=specs + more_specs,
+                out_specs=out_specs,
+            ),
+            out_shape=outs,
+            compiler_params=LIMIT,
+            cost_estimate=pl.CostEstimate(flops=flops, transcendentals=0, bytes_accessed=moved),
+            name=self.name + name,
+        )(table, *args, *more)
+
+    def first_send(self):
+        core, x, y = (bit_of("dp", b) for b in (1, 2, 4))
+        table = [
+            [core + 2 * (1 - x) + 4 * i for i in range(2)],
+            [core + 2 * i + 4 * (1 - y) for i in range(2)],
+        ]
+        table = jnp.stack([jnp.stack(row) for row in table]).astype(jnp.int32)
+        out = jax.ShapeDtypeStruct((2, 4, self.rows, BLOCK), bf16)
+        spec = pl.BlockSpec(out.shape, lambda h, t: (0, 0, 0, 0))
+        self.sends = self.call(send_kernel, "_send", table, [], [], [out, out], [spec, spec])
+
+    def first_swap(self):
+        self.got = [swap(s, "dp", b) for s, b in zip(self.sends, (2, 4))]
+        self.sends = None
+
+    def second_send(self):
+        core, x, y = (bit_of("dp", b) for b in (1, 2, 4))
+        table = [
+            [core + 2 * x + 4 * side for side in (1 - y, y)] + [1 - y, y],
+            [core + 2 * side + 4 * y for side in (1 - x, x)] + [1 - x, x],
+        ]
+        table = jnp.stack([jnp.stack(row) for row in table]).astype(jnp.int32)
+        piece = (4, self.rows, BLOCK)
+        more, more_specs = [], []
+        for half in range(2):
+            for block in range(2):
+                spec = lambda h, t, half=half, block=block: (t[half, 2 + block], 0, 0, 0)
+                more.append(self.got[half])
+                more_specs.append(pl.BlockSpec((1,) + piece, spec))
+        outs = [jax.ShapeDtypeStruct(s, bf16) for s in (piece, piece, (2,) + piece)]
+        spec = pl.BlockSpec(piece, lambda h, t: (0, 0, 0))
+        keep_spec = pl.BlockSpec((1,) + piece, lambda h, t: (h, 0, 0, 0))
+        *self.sends, self.keep = self.call(
+            fold_kernel, "_fold", table, more, more_specs, outs, [spec, spec, keep_spec]
+        )
+        self.got = None
+
+    def second_swap(self):
+        self.got = [swap(s, "dp", b) for s, b in zip(self.sends, (4, 2))]
+        self.sends = None
+
+    def z_send(self, bit):
+        entries = 2 if bit == 1 else 1
+        out = jax.ShapeDtypeStruct((2, entries, self.rows, BLOCK), bf16)
+        gots = self.got if bit == 1 else [self.got]
+        mine = bit_of("seq", bit)[None].astype(jnp.int32)
+        self.sends, self.keep = whole_call(
+            functools.partial(split_kernel, entries),
+            f"{self.name}_z{bit}",
+            [mine],
+            [self.keep, *gots],
+            [out, out],
+        )
+        self.got = None
+
+    def z_swap(self, bit):
+        self.got = swap(self.sends, "seq", bit)
+        self.sends = None
+
+    def finish(self):
+        outs = [jax.ShapeDtypeStruct((j[4], 2 * j[5]), f32) for j in self.jobs]
+        return whole_call(
+            functools.partial(finish_kernel, self.shape),
+            self.name + "_finish",
+            [],
+            [self.keep, self.got],
+            outs,
+        )
+
+
+def scatter_module(jobs):
+    outs = []
+    for lhs, start, tokens, rhs, rows, columns in jobs:
+        whole = rhs[0] if rhs[0] is rhs[1] else jnp.concatenate(rhs, axis=1)
+        outs.append(scatter_job(grad_job(lhs[start : start + tokens], whole, True), rows))
+    return outs
+
+
+def one(rhs):
+    return (rhs, rhs)
+
+
+FIELDS = ("got", "keep", "sends")
+
+
+def fence(things, *extras):
+    fields = [{k: v for k, v in vars(t).items() if k in FIELDS} for t in things]
+    fields, extras = lax.optimization_barrier((fields, extras))
+    for thing, values in zip(things, fields):
+        vars(thing).update(values)
+    return extras
+
+
+def fetch_weight(part):
+    return lax.all_gather(part, ("dp", "seq"), axis=0, tiled=True)
+
+
+def pack_kernel(*refs):
+    shards, out = refs[:-1], refs[-1]
+    width = out.shape[1]
+    at = 0
+    for shard in shards:
+        rows = shard.shape[0]
+        for j in range(shard.shape[1] // width):
+            out[at : at + rows, :] = shard[:, j * width : (j + 1) * width]
+            at += rows
+
+
+def fetch_packed(shards, name):
+    width = shards[-1].shape[1]
+    rows = sum(s.shape[0] * s.shape[1] // width for s in shards)
+    out = jax.ShapeDtypeStruct((rows, width), bf16)
+    (packed,) = whole_call(pack_kernel, name, [], shards, [out])
+    return lax.all_gather(packed, ("dp", "seq"), axis=0)
+
+
+def packed_block(packed, start, rows):
+    return packed[:, start : start + rows].reshape(-1, packed.shape[2])
+
+
+def up_kernel(normed_ref, weight_ref, active_ref, slope_ref):
+    width = normed_ref.shape[1]
+    for half in range(2):
+        columns = slice(half * width // 2, (half + 1) * width // 2)
+        block = weight_ref[:, :, columns].reshape(width, width // 2)
+        hidden = product(normed_ref[...], block)
+        sigmoid = 1.0 / (1.0 + jnp.exp(-hidden))
+        active_ref[:, columns] = (hidden * sigmoid).astype(bf16)
+        slope_ref[:, columns] = (sigmoid * (1.0 + hidden * (1.0 - sigmoid))).astype(bf16)
+
+
+def up_back_kernel(grad_ref, weight_ref, out_ref):
+    width = out_ref.shape[1]
+    part = product_tail(grad_ref[...], weight_ref[...].reshape(width, -1))
+    out_ref[...] = jnp.where(pl.program_id(0) == 0, part, out_ref[...] + part)
+
+
+def down_kernel(values_ref, active_ref, weight_ref, out_ref, total_ref):
+    width = out_ref.shape[1]
+    part = product(active_ref[...], weight_ref[...].reshape(-1, width))
+    total_ref[...] = jnp.where(pl.program_id(0) == 0, part, total_ref[...] + part)
+
+    @pl.when(pl.program_id(0) == pl.num_programs(0) - 1)
+    def _():
+        out_ref[...] = values_ref[...] + 0.5 * total_ref[...]
+
+
+def down_back_kernel(branch_ref, slope_ref, weight_ref, out_ref):
+    width = branch_ref.shape[1]
+    part = product_tail(branch_ref[...], weight_ref[...].reshape(-1, width))
+    out_ref[...] = (part * slope_ref[...].astype(f32)).astype(bf16)
+
+
+def ffn_call(kernel, name, packed, part, inputs, outs, scratch=()):
+    owners, _, width = packed.shape
+    steps = 4
+    rows = width // owners
+    if part == "up":
+        weight = pl.BlockSpec((owners, rows, width), lambda i: (0, i, 0))
+    else:
+        weight = pl.BlockSpec((owners // steps, rows * steps, width), lambda i: (i, 1, 0))
+
+    def spec(x):
+        tokens, columns = x.shape
+        return pl.BlockSpec((tokens, width), (lambda i: (0, i)) if columns > width else (lambda i: (0, 0)))
+
+    numbers = lambda things: sum(t.size * t.dtype.itemsize for t in things)
+    tokens = inputs[0].shape[0]
+    inner = steps * width
+    return pl.pallas_call(
+        kernel,
+        grid=(steps,),
+        in_specs=[spec(x) for x in inputs] + [weight],
+        out_specs=[spec(o) for o in outs],
+        out_shape=outs,
+        scratch_shapes=list(scratch),
+        compiler_params=pltpu.CompilerParams(vmem_limit_bytes=56 << 20),
+        cost_estimate=pl.CostEstimate(
+            flops=2 * tokens * width * inner,
+            transcendentals=0,
+            bytes_accessed=2 * width * inner + numbers(inputs) + numbers(outs),
+        ),
+        name=name,
+    )(*inputs, packed)
+
+
+class Packed:
+    def __init__(self, array):
+        self.array = array
+
+
+def ffn_up(normed, packed, name):
+    tokens, width = normed.shape
+    out = jax.ShapeDtypeStruct((tokens, 4 * width), bf16)
+    return ffn_call(up_kernel, name, packed.array, "up", [normed], [out, out])
+
+
+def ffn_up_back(grad_hidden, packed, name):
+    out = jax.ShapeDtypeStruct((grad_hidden.shape[0], packed.array.shape[2]), f32)
+    return ffn_call(up_back_kernel, name, packed.array, "up", [grad_hidden], [out])[0]
+
+
+def ffn_down(values, active, packed, name):
+    out = jax.ShapeDtypeStruct(values.shape, f32)
+    scratch = [pltpu.VMEM(values.shape, f32)]
+    return ffn_call(down_kernel, name, packed.array, "down", [values, active], [out], scratch)[0]
+
+
+def ffn_down_back(branch, slope, packed, name):
+    out = jax.ShapeDtypeStruct(slope.shape, bf16)
+    return ffn_call(down_back_kernel, name, packed.array, "down", [branch, slope], [out])[0]
+
+
 def gather_line(own):
     seq = lax.axis_size("seq")
     ups, downs = [own], [own]
@@ -223,9 +620,10 @@
     return jnp.stack(blocks)
 
 
-def scatter_line(blocks):
+def scatter_line(blocks, between=()):
     seq = lax.axis_size("seq")
     up = down = None
+    between = iter(between)
     for step in range(seq - 1, 0, -1):
         message_up, message_down = blocks[step], blocks[seq - step]
         if up is not None:
@@ -233,6 +631,9 @@
             message_down = add_pair(message_down, down)
         up = lax.ppermute(message_up, "seq", [(i, i + 1) for i in range(seq - 1)])
         down = lax.ppermute(message_down, "seq", [(i + 1, i) for i in range(seq - 1)])
+        meanwhile = next(between, None)
+        if meanwhile is not None:
+            up, down = meanwhile(up, down)
     total = blocks[0].astype(f32)
     if up is not None:
         total = total + up.astype(f32) + down.astype(f32)
@@ -270,26 +671,46 @@
     return sigmoid_rows * (1.0 + hidden * (1.0 - sigmoid_rows))
 
 
-def ffn_forward(values, norm_gain, upward, downward):
+def ffn_forward(values, norm_gain, upward, downward, name):
     normed, normal, inverse = norm_forward(values, norm_gain)
     normed_low = normed.astype(bf16)
-    hidden = product(normed_low, upward)
-    active = jax.nn.silu(hidden).astype(bf16)
-    return (values + 0.5 * product(active, downward), (normed_low, normal, inverse, hidden, active))
-
-
-def ffn_backward(grad_rows, norm_gain, upward, downward, stored):
-    normed_low, normal, inverse, hidden, active = stored
-    grad_branch = (0.5 * grad_rows).astype(bf16)
-    grad_hidden = (product_tail(grad_branch, downward) * silu_slope(hidden)).astype(bf16)
-    grad_in, grad_gain = norm_backward(
-        product_tail(grad_hidden, upward), norm_gain, normal, inverse
-    )
-    rows = upward.shape[0] // (lax.axis_size("dp") * lax.axis_size("seq"))
-    rows_down = downward.shape[0] // (lax.axis_size("dp") * lax.axis_size("seq"))
-    grad_down = scatter_job(grad_job(active, grad_branch, True), rows_down)
-    grad_up = scatter_job(grad_job(normed_low, grad_hidden, True), rows)
-    return (grad_rows + grad_in, grad_gain, grad_up, grad_down)
+    if isinstance(upward, Packed):
+        active, slope = ffn_up(normed_low, upward, name + "_up")
+        out = ffn_down(values, active, downward, name + "_down")
+    else:
+        hidden = product(normed_low, upward)
+        active, slope = jax.nn.silu(hidden).astype(bf16), silu_slope(hidden)
+        out = values + 0.5 * product(active, downward)
+    return out, (normed_low, normal, inverse, slope, active)
+
+
+def owner_rows(rows):
+    return rows // (lax.axis_size("dp") * lax.axis_size("seq"))
+
+
+def ffn_hidden_grad(grad_branch, downward, stored, name):
+    if isinstance(downward, Packed):
+        return ffn_down_back(grad_branch, stored[3], downward, name + "_down_back")
+    return (product_tail(grad_branch, downward) * stored[3]).astype(bf16)
+
+
+def ffn_input_grad(grad_rows, grad_hidden, norm_gain, upward, stored, name):
+    if isinstance(upward, Packed):
+        grad_normed = ffn_up_back(grad_hidden, upward, name + "_up_back")
+    else:
+        grad_normed = product_tail(grad_hidden, upward)
+    grad_in, grad_gain = norm_backward(grad_normed, norm_gain, stored[1], stored[2])
+    return grad_rows + grad_in, grad_gain
+
+
+def ffn_jobs(grad_branch, grad_hidden, stored):
+    normed_low, active = stored[0], stored[4]
+    tokens, width = normed_low.shape
+    inner = active.shape[1]
+    return [
+        (normed_low, 0, tokens, one(grad_hidden), owner_rows(width), inner // 2),
+        (active, 0, tokens, one(grad_branch), owner_rows(inner), width // 2),
+    ]
 
 
 def key_valid(offsets_ref, rows, keys):
@@ -365,9 +786,9 @@
     value_grad_ref[...] = value_grad.astype(bf16)
 
 
-def attend(offsets, query, key_value):
+def attend(offsets, query, key, value):
     rows, width = query.shape
-    keys = key_value.shape[0]
+    keys = key.shape[0]
     pairs = width // 128
     return pl.pallas_call(
         functools.partial(attend_kernel, rows),
@@ -377,7 +798,7 @@
             in_specs=[
                 pl.BlockSpec((rows, 128), lambda i, o: (0, i)),
                 pl.BlockSpec((keys, 128), lambda i, o: (0, i)),
-                pl.BlockSpec((keys, 128), lambda i, o: (0, i + pairs)),
+                pl.BlockSpec((keys, 128), lambda i, o: (0, i)),
             ],
             out_specs=[
                 pl.BlockSpec((rows, 128), lambda i, o: (0, i)),
@@ -390,12 +811,13 @@
         ],
         compiler_params=pltpu.CompilerParams(vmem_limit_bytes=48 << 20),
         name="attend",
-    )(offsets, query, key_value, key_value)
+    )(offsets, query, key, value)
 
 
 def attend_back(offsets, query, key_value, totals, grad):
     rows, width = query.shape
-    keys = key_value.shape[0]
+    key, value = key_value
+    keys = key.shape[0]
     pairs = width // 128
     row_spec = pl.BlockSpec((rows, 128), lambda i, o: (0, i))
     key_spec = pl.BlockSpec((keys, 128), lambda i, o: (0, i))
@@ -407,7 +829,7 @@
             in_specs=[
                 row_spec,
                 key_spec,
-                pl.BlockSpec((keys, 128), lambda i, o: (0, i + pairs)),
+                pl.BlockSpec((keys, 128), lambda i, o: (0, i)),
                 pl.BlockSpec((1, 2, rows), lambda i, o: (i, 0, 0)),
                 row_spec,
             ],
@@ -420,46 +842,54 @@
         ],
         compiler_params=pltpu.CompilerParams(vmem_limit_bytes=48 << 20),
         name="attend_back",
-    )(offsets, query, key_value, key_value, totals, grad)
-
-
-def attention_forward(values, length, norm_gain, joint_proj, attend_out):
+    )(offsets, query, key, value, totals, grad)
+
+
+def attention_forward(values, length, norm_gain, joint_proj, attend_out, gathered):
     normed, normal, inverse = norm_forward(values, norm_gain)
     normed_low = normed.astype(bf16)
     frames, model_width = normed_low.shape
     seq = lax.axis_size("seq")
-    normed_all = gather_line(normed_low).reshape(seq * frames, model_width)
-    query = product(normed_low, joint_proj[:, :model_width]).astype(bf16)
-    key_value = product(normed_all, joint_proj[:, model_width:]).astype(bf16)
+    normed_all = gathered(gather_line(normed_low)).reshape(seq * frames, model_width)
+    query = product(normed_low, joint_proj[0]).astype(bf16)
+    key = product(normed_all, joint_proj[1]).astype(bf16)
+    value = product(normed_all, joint_proj[2]).astype(bf16)
     starts = ((lax.axis_index("seq") + jnp.arange(seq)) % seq) * frames
     offsets = jnp.concatenate([starts, length[None]]).astype(jnp.int32)
-    mixed_low, totals = attend(offsets, query, key_value)
+    mixed_low, totals = attend(offsets, query, key, value)
     output = values + product(mixed_low, attend_out)
-    stored = (normed_low, normal, inverse, normed_all, query, key_value, offsets, totals, mixed_low)
+    stored = (normed_low, normal, inverse, normed_all, query, (key, value), offsets, totals, mixed_low)
     return (output, stored)
 
 
-def attention_backward(grad_rows, norm_gain, joint_proj, attend_out, stored):
+def attention_parts_grad(grad_rows, attend_out, stored):
     normed_low, normal, inverse, normed_all, query, key_value, offsets, totals, mixed_low = stored
-    frames, model_width = normed_low.shape
-    shards = lax.axis_size("dp") * lax.axis_size("seq")
-    rows = model_width // shards
     grad_branch = grad_rows.astype(bf16)
     grad_mixed = product_tail(grad_branch, attend_out).astype(bf16)
-    grad_query, grad_key, grad_value = attend_back(offsets, query, key_value, totals, grad_mixed)
-    part = product_tail(grad_key, joint_proj[:, model_width : 2 * model_width]) + product_tail(
-        grad_value, joint_proj[:, 2 * model_width :]
-    )
-    blocks = part.astype(bf16).reshape(-1, frames, model_width)
-    grad_normed = scatter_line(blocks) + product_tail(grad_query, joint_proj[:, :model_width])
-    grad_in, grad_gain = norm_backward(grad_normed, norm_gain, normal, inverse)
-    grad_out = scatter_job(grad_job(mixed_low, grad_branch, True), rows)
-    grad_joint = [
-        scatter_job(grad_job(normed_low, grad_query, True), rows),
-        scatter_job(grad_job(normed_all, grad_key, False), rows),
-        scatter_job(grad_job(normed_all, grad_value, False), rows),
+    return (grad_branch,) + tuple(attend_back(offsets, query, key_value, totals, grad_mixed))
+
+
+def attention_blocks_grad(grad_key, grad_value, joint_proj, frames):
+    width = grad_key.shape[1]
+    part = product_tail(grad_key, joint_proj[1]) + product_tail(grad_value, joint_proj[2])
+    return part.astype(bf16).reshape(-1, frames, width)
+
+
+def attention_input_grad(grad_rows, grad_normed, grad_query, norm_gain, joint_proj, stored):
+    grad_normed = grad_normed + product_tail(grad_query, joint_proj[0])
+    grad_in, grad_gain = norm_backward(grad_normed, norm_gain, stored[1], stored[2])
+    return grad_rows + grad_in, grad_gain
+
+
+def attention_jobs(grad_branch, grad_query, grad_key, grad_value, stored):
+    normed_all, mixed_low = stored[3], stored[8]
+    frames, width = grad_query.shape
+    rows = owner_rows(width)
+    return [
+        (normed_all, 0, frames, one(grad_query), rows, width // 2),
+        (normed_all, 0, normed_all.shape[0], (grad_key, grad_value), rows, width),
+        (mixed_low, 0, frames, one(grad_branch), rows, width // 2),
     ]
-    return (grad_rows + grad_in, grad_gain, jnp.concatenate(grad_joint, axis=1), grad_out)
 
 
 def conv_forward(
@@ -467,11 +897,10 @@
 ):
     normed, normal, inverse = norm_forward(values, norm_gain)
     normed_low = normed.astype(bf16)
-    paired = product(normed_low, conv_pair)
-    model_width = paired.shape[1] // 2
-    frames = paired.shape[0]
-    sigmoid_rows = jax.nn.sigmoid(paired[:, model_width:])
-    gated_rows = (paired[:, :model_width] * sigmoid_rows * valid_rows).astype(bf16)
+    paired = product(normed_low, conv_pair[0])
+    frames, model_width = paired.shape
+    sigmoid_rows = jax.nn.sigmoid(product(normed_low, conv_pair[1]))
+    gated_rows = (paired * sigmoid_rows * valid_rows).astype(bf16)
     half_width = taps_float.shape[1] // 2
     widened = with_halo(gated_rows, half_width)
     mixture = jnp.zeros((frames, model_width), f32)
@@ -504,34 +933,17 @@
     return (output, stored, (batch_mean, batch_var, frame_count))
 
 
-def conv_backward(
-    grad_rows,
-    valid_rows,
-    norm_gain,
-    conv_pair,
-    taps_float,
-    scale_float,
-    conv_out,
-    stored,
-    frame_count,
-):
-    (
-        normed_low,
-        normal,
-        inverse,
-        paired,
-        sigmoid_rows,
-        widened,
-        normal_batch,
-        inverse_std,
-        shaped,
-        active,
-    ) = stored
+def conv_shaped_grad(grad_rows, valid_rows, conv_out, stored):
+    normal_batch, shaped = stored[6], stored[8]
     grad_branch = grad_rows.astype(bf16)
     grad_shaped = product_tail(grad_branch, conv_out) * silu_slope(shaped) * valid_rows
-    total_shift, total_scale = sum_small(
-        jnp.stack([jnp.sum(grad_shaped, axis=0), jnp.sum(grad_shaped * normal_batch, axis=0)])
-    )
+    sums = jnp.stack([jnp.sum(grad_shaped, axis=0), jnp.sum(grad_shaped * normal_batch, axis=0)])
+    return grad_branch, grad_shaped, sums
+
+
+def conv_paired_grad(grad_shaped, totals, valid_rows, taps_float, scale_float, frame_count, stored):
+    paired, sigmoid_rows, widened, normal_batch, inverse_std = (stored[i] for i in (3, 4, 5, 6, 7))
+    total_shift, total_scale = totals
     grad_mixture = (
         inverse_std
         * valid_rows
@@ -554,31 +966,27 @@
             grad_gated + grad_rims[lower_edge : lower_edge + frames] * taps_float[:, offset]
         )
         tap_grads.append(jnp.sum(widened_float[offset : offset + frames] * grad_float, axis=0))
-    grad_taps = jnp.stack(tap_grads, axis=1)
     grad_left = grad_gated * sigmoid_rows * valid_rows
-    grad_right = (
-        grad_gated * paired[:, :model_width] * sigmoid_rows * (1.0 - sigmoid_rows) * valid_rows
-    )
-    grad_paired = jnp.concatenate([grad_left, grad_right], axis=1).astype(bf16)
-    grad_in, grad_gain = norm_backward(
-        product_tail(grad_paired, conv_pair), norm_gain, normal, inverse
-    )
-    rows = model_width // (lax.axis_size("dp") * lax.axis_size("seq"))
-    grad_out = scatter_job(grad_job(active, grad_branch, True), rows)
-    grad_pair = scatter_job(grad_job(normed_low, grad_paired, True), rows)
-    return (
-        grad_rows + grad_in,
-        grad_gain,
-        grad_pair,
-        grad_taps,
-        grad_out,
-        total_scale,
-        total_shift,
-    )
-
-
-def fetch_weight(part):
-    return lax.all_gather(part, ("dp", "seq"), axis=0, tiled=True)
+    grad_right = grad_gated * paired * sigmoid_rows * (1.0 - sigmoid_rows) * valid_rows
+    return (grad_left.astype(bf16), grad_right.astype(bf16)), jnp.stack(tap_grads)
+
+
+def conv_input_grad(grad_rows, grad_paired, norm_gain, conv_pair, stored):
+    grad_normed = product_tail(grad_paired[0], conv_pair[0]) + product_tail(
+        grad_paired[1], conv_pair[1]
+    )
+    grad_in, grad_gain = norm_backward(grad_normed, norm_gain, stored[1], stored[2])
+    return grad_rows + grad_in, grad_gain
+
+
+def conv_jobs(grad_branch, grad_paired, stored):
+    normed_low, active = stored[0], stored[9]
+    frames, width = normed_low.shape
+    rows = owner_rows(width)
+    return [
+        (normed_low, 0, frames, grad_paired, rows, width),
+        (active, 0, frames, one(grad_branch), rows, width // 2),
+    ]
 
 
 def per_device(
@@ -624,6 +1032,30 @@
     )
     own_small = jnp.concatenate([jnp.stack(vectors, axis=0), conv_taps.T], axis=0)
     count = own_small.shape[0]
+    shards = lax.axis_size("dp") * lax.axis_size("seq")
+    own_rows = model_width // shards
+    if in_steps(model_width):
+        front = fetch_packed((first_up, first_down), "pack_first")
+        middle_shards = tie(front, joint_proj, attend_out, conv_pair, conv_out)[1:]
+        middle = fetch_packed(middle_shards, "pack_middle")
+        up_one = down_one = Packed(front)
+        squares = [packed_block(middle, i * own_rows, own_rows) for i in range(7)]
+        joint_all, outward_all = squares[:3], squares[3]
+        pair_all, conv_out_all = squares[4:6], squares[6]
+    else:
+        up_one, down_one, joint_all, outward_all, pair_all, conv_out_all = (
+            fetch_weight(part)
+            for part in (
+                first_up,
+                first_down,
+                joint_proj,
+                attend_out,
+                conv_pair,
+                conv_out,
+            )
+        )
+        joint_all = jnp.split(joint_all, 3, axis=1)
+        pair_all = jnp.split(pair_all, 2, axis=1)
     small = gather_small(own_small[None])
     small = jnp.transpose(small, (1, 0, 2)).reshape(count, model_width).astype(f32)
     vector_mask, g_first, g_attend, g_conv, g_second, g_final, scale_float, shift_float = (
@@ -632,49 +1064,131 @@
     taps_float = small[8:].T
 
     start_rows = jnp.where(masked_float > 0.0, vector_mask[None, :], inputs[0].astype(f32))
-    up_one, down_one = fetch_weight(first_up), fetch_weight(first_down)
-    values, first_stored = ffn_forward(start_rows, g_first, up_one, down_one)
-    joint_all, outward_all = fetch_weight(joint_proj), fetch_weight(attend_out)
-    values, attend_stored = attention_forward(values, length, g_attend, joint_all, outward_all)
-    pair_all, conv_out_all = fetch_weight(conv_pair), fetch_weight(conv_out)
+    values, first_stored = ffn_forward(start_rows, g_first, up_one, down_one, "first")
+    second_weights = []
+
+    def gathered(rows):
+        if not in_steps(model_width):
+            second_weights.extend([fetch_weight(second_up), fetch_weight(second_down)])
+            return rows
+        rows, _, up_shard, down_shard = tie(rows, middle, second_up, second_down)
+        back = Packed(fetch_packed((up_shard, down_shard), "pack_second"))
+        second_weights.extend([back, back])
+        return rows
+
+    values, attend_stored = attention_forward(
+        values, length, g_attend, joint_all, outward_all, gathered
+    )
+    up_two, down_two = second_weights
     values, conv_stored, batch_stats = conv_forward(
         values, valid_rows, g_conv, pair_all, taps_float, scale_float, shift_float, conv_out_all
     )
-    up_two, down_two = fetch_weight(second_up), fetch_weight(second_down)
-    values, second_stored = ffn_forward(values, g_second, up_two, down_two)
+    values, second_stored = ffn_forward(values, g_second, up_two, down_two, "second")
     normed, normal, inverse = norm_forward(values, g_final)
     output = (normed * valid_rows).astype(bf16)
 
     grad_rows, grad_final = norm_backward(
         cotangent[0].astype(f32) * valid_rows, g_final, normal, inverse
     )
-    grad_rows, grad_gain_two, grad_up_two, grad_down_two = ffn_backward(
-        grad_rows, g_second, up_two, down_two, second_stored
-    )
-    grad_rows, grad_gain_conv, grad_pair, grad_taps, grad_conv_out, total_scale, total_shift = (
-        conv_backward(
-            grad_rows,
-            valid_rows,
-            g_conv,
-            pair_all,
-            taps_float,
-            scale_float,
-            conv_out_all,
-            conv_stored,
-            batch_stats[2],
-        )
-    )
-    grad_rows, grad_gain_attend, grad_joint, grad_attend_out = attention_backward(
-        grad_rows, g_attend, joint_all, outward_all, attend_stored
-    )
-    grad_rows, grad_gain_one, grad_up_one, grad_down_one = ffn_backward(
-        grad_rows, g_first, up_one, down_one, first_stored
+    steps = in_steps(model_width)
+    frame_count = batch_stats[2]
+    branch_two = (0.5 * grad_rows).astype(bf16)
+    hidden_two = ffn_hidden_grad(branch_two, down_two, second_stored, "second")
+    jobs_two = ffn_jobs(branch_two, hidden_two, second_stored)
+    if steps:
+        two = ModuleScatter(jobs_two, "second_terms")
+        two.share()
+        two.first_send()
+    grad_rows, grad_gain_two = ffn_input_grad(
+        grad_rows, hidden_two, g_second, up_two, second_stored, "second"
+    )
+    if steps:
+        (grad_rows,) = fence([two], grad_rows)
+        two.first_swap()
+
+    branch_conv, grad_shaped, sums = conv_shaped_grad(
+        grad_rows, valid_rows, conv_out_all, conv_stored
+    )
+    totals = sum_small(sums)
+    total_shift, total_scale = totals
+    grad_paired, grad_taps = conv_paired_grad(
+        grad_shaped, totals, valid_rows, taps_float, scale_float, frame_count, conv_stored
+    )
+    jobs_conv = conv_jobs(branch_conv, grad_paired, conv_stored)
+    if steps:
+        conv = ModuleScatter(jobs_conv, "conv_terms")
+        conv.share()
+        conv.first_send()
+    grad_rows, grad_gain_conv = conv_input_grad(
+        grad_rows, grad_paired, g_conv, pair_all, conv_stored
+    )
+    if steps:
+        (grad_rows,) = fence([two, conv], grad_rows)
+        conv.first_swap()
+        two.second_send()
+        (grad_rows,) = fence([two], grad_rows)
+        two.second_swap()
+
+    branch_attend, grad_query, grad_key, grad_value = attention_parts_grad(
+        grad_rows, outward_all, attend_stored
+    )
+    jobs_attend = attention_jobs(branch_attend, grad_query, grad_key, grad_value, attend_stored)
+    blocks = attention_blocks_grad(grad_key, grad_value, joint_all, frames)
+    between = ()
+    if steps:
+        attend_sum = ModuleScatter(jobs_attend, "attend_terms")
+        attend_sum.share()
+
+        def fold_conv(up, down):
+            up, down = fence([conv], up, down)
+            conv.second_send()
+            up, down = fence([conv], up, down)
+            conv.second_swap()
+            return up, down
+
+        def send_attend(up, down):
+            attend_sum.first_send()
+            return fence([attend_sum], up, down)
+
+        def send_two(up, down):
+            attend_sum.first_swap()
+            up, down = fence([two], up, down)
+            two.z_send(1)
+            return fence([two], up, down)
+
+        between = (fold_conv, send_attend, send_two)
+    grad_normed = scatter_line(blocks, between)
+    if steps:
+        two.z_swap(1)
+    grad_rows, grad_gain_attend = attention_input_grad(
+        grad_rows, grad_normed, grad_query, g_attend, joint_all, attend_stored
+    )
+    branch_one = (0.5 * grad_rows).astype(bf16)
+    if steps:
+        down_sum = ModuleScatter(ffn_jobs(branch_one, None, first_stored)[1:], "down_terms")
+        down_sum.share()
+        down_sum.first_send()
+        branch_one, grad_rows = fence([down_sum], branch_one, grad_rows)
+        down_sum.first_swap()
+    hidden_one = ffn_hidden_grad(branch_one, down_one, first_stored, "first")
+    jobs_one = ffn_jobs(branch_one, hidden_one, first_stored)
+    if steps:
+        hidden_one, grad_rows = fence([two, attend_sum], hidden_one, grad_rows)
+        two.z_send(2)
+        two.z_swap(2)
+        attend_sum.second_send()
+        up_sum = ModuleScatter([(jobs_one[0][0], 0, frames, one(hidden_one)) + jobs_one[0][4:]], "up_terms")
+        up_sum.share()
+        up_sum.first_send()
+        hidden_one, grad_rows = fence([attend_sum, up_sum], hidden_one, grad_rows)
+        attend_sum.second_swap()
+        up_sum.first_swap()
+    grad_rows, grad_gain_one = ffn_input_grad(
+        grad_rows, hidden_one, g_first, up_one, first_stored, "first"
     )
     input_grad = grad_rows * (1.0 - masked_float)
     mask_grad = jnp.sum(grad_rows * masked_float, axis=0)
 
-    shards = lax.axis_size("dp") * lax.axis_size("seq")
-    own_rows = model_width // shards
     sums = jnp.concatenate(
         [
             jnp.stack(
@@ -687,16 +1201,63 @@
                     grad_final,
                 ]
             ),
-            grad_taps.T,
+            grad_taps,
         ],
         axis=0,
     )
     sums = jnp.transpose(sums.reshape(-1, shards, own_rows), (1, 0, 2))
-    sums = scatter_small(sums)[0]
+    if steps:
+        few = SmallScatter(sums)
+        fence([two, conv, down_sum, few])
+        conv.z_send(1)
+        conv.z_swap(1)
+        down_sum.second_send()
+        down_sum.second_swap()
+        few.step()
+        fence([attend_sum, conv, few])
+        conv.z_send(2)
+        conv.z_swap(2)
+        attend_sum.z_send(1)
+        attend_sum.z_swap(1)
+        few.step()
+        fence([up_sum, attend_sum, conv, few])
+        up_sum.second_send()
+        up_sum.second_swap()
+        attend_sum.z_send(2)
+        attend_sum.z_swap(2)
+        few.step()
+        fence([down_sum, attend_sum, few])
+        down_sum.z_send(1)
+        down_sum.z_swap(1)
+        few.step()
+        fence([down_sum, up_sum, few])
+        down_sum.z_send(2)
+        down_sum.z_swap(2)
+        up_sum.z_send(1)
+        up_sum.z_swap(1)
+        few.step()
+        fence([down_sum, up_sum, few])
+        up_sum.z_send(2)
+        up_sum.z_swap(2)
+        few.step()
+        sums = few.keep[0]
+        grad_up_two, grad_down_two = two.finish()
+        grad_pair, grad_conv_out = conv.finish()
+        attend_grads = attend_sum.finish()
+        (grad_up_one,) = up_sum.finish()
+        (grad_down_one,) = down_sum.finish()
+    else:
+        sums = scatter_small(sums)[0]
+        grad_up_two, grad_down_two = scatter_module(jobs_two)
+        grad_pair, grad_conv_out = scatter_module(jobs_conv)
+        attend_grads = scatter_module(jobs_attend)
+        grad_up_one, grad_down_one = scatter_module(jobs_one)
+    grad_joint = jnp.concatenate(list(attend_grads[:2]), axis=1)
+    grad_attend_out = attend_grads[2]
     own_start = (lax.axis_index("dp") * lax.axis_size("seq") + lax.axis_index("seq")) * own_rows
     scale_grad = lax.dynamic_slice_in_dim(total_scale, own_start, own_rows)
     shift_grad = lax.dynamic_slice_in_dim(total_shift, own_start, own_rows)
-    batch_mean, batch_var, frame_count = batch_stats
+    batch_mean, batch_var, _ = batch_stats
     moment_var = batch_var * frame_count / (frame_count - 1.0)
     return (
         output[None],

time: 1180 us -> 884 us (0.75)
  Pallas kernels: 37.2 us -> 208 us
  waiting for transfers between devices: 574 us -> 421 us
  local copies, waits for them, and re-layouts: 177 us -> 47.1 us
  matrix products: 131 us -> 23.5 us
  other arithmetic: 94.4 us -> 54.8 us
  starting transfers between devices: 134 us -> 103 us
    all_gather x8 -> x3, waiting for transfers between devices: 341 us -> 160 us  [fetch_packed(): return lax.all_gather(packed, ('dp', 'seq'), axis=0)]
    pallas_call x0 -> x36, Pallas kernels: none -> 171 us  [the longest x10 69.6 us: call(): pl.pallas_call(functools.partial(kernel, self.shape, 4), grid_spec=pltpu....]
    dynamic_slice x43 -> x1, local copies, waits for them, and re-layouts: 86.2 us -> 1.92 us  [pick(): return lax.dynamic_index_in_dim(array, index, axis, keepdims=False)]
    dot_general x40 -> x0, matrix products: 50.2 us -> none  [product_lead(): lax.dot_general(left_side, right_side, (((0,), (0,)), ((), ())), preferre...]
    ppermute x3, waiting for transfers between devices: 19.5 us -> 64.7 us  [gather_line(): lax.ppermute(downs[-1], 'seq', [(i + 1, i) for i in range(seq - 1)])]
    dot_general x9 -> x7, matrix products: 45.9 us -> 11.3 us  [product(): return jnp.dot(left_side, right_side, preferred_element_type=f32)]
    ppermute x100 -> x69, waiting for transfers between devices: 205 us -> 172 us  [swap(): lax.ppermute(values, axis, [(i, i ^ bit) for i in range(lax.axis_size(axi...]
    ppermute x100 -> x69, starting transfers between devices: 85.3 us -> 58.7 us  [swap(): lax.ppermute(values, axis, [(i, i ^ bit) for i in range(lax.axis_size(axi...]
  transfers between devices with their start and end apart: 124 -> 88, of which waited for: 61 -> 47; matrix products, arithmetic and copies ran while one was open for 34% -> 11% of each run, Pallas kernels for 3% -> 16%
where the time goes in v2:
time: 884 us; the launch traced here: 877 us
  waiting for transfers between devices  421 us (48%)
  Pallas kernels  208 us (24%)
  starting transfers between devices  103 us (12%)
  other arithmetic  54.8 us (6%)
  local copies, waits for them, and re-layouts  47.1 us (5%)
  matrix products  23.5 us (3%)
  between operations  18.9 us (2%)
    ppermute x69, waiting for transfers between devices, swap(): lax.ppermute(values, axis, [(i, i ^ bit) for i in range(lax.axis_size(axi...  172 us
    all_gather x3, waiting for transfers between devices, fetch_packed(): return lax.all_gather(packed, ('dp', 'seq'), axis=0)  160 us
    pallas_call x10, Pallas kernels, call(): pl.pallas_call(functools.partial(kernel, self.shape, 4), grid_spec=pltpu....  69.6 us
    ppermute x3, waiting for transfers between devices, gather_line(): lax.ppermute(downs[-1], 'seq', [(i + 1, i) for i in range(seq - 1)])  64.7 us
    pallas_call x8, Pallas kernels, ffn_call(): pl.pallas_call(kernel, grid=(steps,), in_specs=[spec(x) for x in inputs]...  59.9 us
    ppermute x69, starting transfers between devices, swap(): lax.ppermute(values, axis, [(i, i ^ bit) for i in range(lax.axis_size(axi...  58.7 us
    pallas_call x18, Pallas kernels, whole_call(): pl.pallas_call(kernel, grid_spec=pltpu.PrefetchScalarGridSpec(num_scalar_...  41.5 us
    pallas_call x1, Pallas kernels, attend_back(): pl.pallas_call(functools.partial(attend_back_kernel, rows), grid_spec=plt...  20.3 us
  transfers between devices with their start and end apart: 88, of which 47 were waited for; matrix products, arithmetic and copies ran while one was open for 11% of the time, Pallas kernels for 16%

profile of v2, /device:TPU:0, one launch (start us, length us, event | category | flops | bytes accessed | tf_op | source)
XLA Modules:
  0.0 876.9 jit_solution(5839035843782354341)
XLA Ops:
  9.3 120.0 %all-gather.7.cloned.1.call-done = bf16[8192,1024]{1,0:T(8,128)(2,1)} async-done(((bf16[256,1024]{1,0:T(8,128)(2,1)}), bf16[8192,1024]{1,0:T(8,128)(2,1)}) %all-gather.7.cloned.1.call-update) | async-done | bytes 16777232 | tf_op jit(solution)/shard_map/all_gather | solution.py:510
  156.8 8.3 first_up.1
  165.1 7.4 first_down.1
  181.6 14.3 %collective-permute-done.5 = bf16[256,1024]{1,0:T(8,128)(2,1)S(1)} collective-permute-done((bf16[256,1024]{1,0:T(8,128)(2,1)S(1)}, bf16[256,1024]{1,0:T(8,128)(2,1)S(1)}, u32[]{:S(2)}, u32[]{:S(2)}) %collective-permute-start.5) | collective-permute-done | bytes 524320 | tf_op jit(solution)/shard_map/ppermute | solution.py:615
  201.8 33.3 %collective-permute-done.9 = bf16[256,1024]{1,0:T(8,128)(2,1)} collective-permute-done((bf16[256,1024]{1,0:T(8,128)(2,1)S(1)}, bf16[256,1024]{1,0:T(8,128)(2,1)}, u32[]{:S(2)}, u32[]{:S(2)}) %collective-permute-start.9) | collective-permute-done | bytes 524320 | tf_op jit(solution)/shard_map/ppermute | solution.py:615
  242.9 17.0 %collective-permute-done.10 = bf16[256,1024]{1,0:T(8,128)(2,1)S(1)} collective-permute-done((bf16[256,1024]{1,0:T(8,128)(2,1)}, bf16[256,1024]{1,0:T(8,128)(2,1)S(1)}, u32[]{:S(2)}, u32[]{:S(2)}) %collective-permute-start.10) | collective-permute-done | bytes 524320 | tf_op jit(solution)/shard_map/ppermute | solution.py:615
  266.3 7.8 fusion.132
  280.3 16.9 %attend.1 = (bf16[256,1024]{1,0:T(8,128)(2,1)S(1)}, f32[8,2,256]{2,1,0:T(2,128)S(1)}) custom-call(s32[5]{0:T(128)S(1)} %pad_add_fusion.2.offsets_ref, bf16[256,1024]{1,0:T(8,128)(2,1)S(1)} %convolution_convert_fusion.3.query_ref, bf16[1024,1024]{1,0:T(8,128)(2,1)S(1)} %convolution_convert_fusion.1.key_ref, ...), custom_call_target="tpu_custom_call" | custom-call | tf_op jit(solution)/shard_map/attend/pallas_call | solution.py:793
  341.1 39.9 %all-gather.11.cloned.1.call-done = bf16[8192,1024]{1,0:T(8,128)(2,1)} async-done(((bf16[256,1024]{1,0:T(8,128)(2,1)}), bf16[8192,1024]{1,0:T(8,128)(2,1)}) %all-gather.11.cloned.1.call-update) | async-done | bytes 16777232 | tf_op jit(solution)/shard_map/all_gather | solution.py:510
  381.1 7.9 second_up.1
  422.5 7.9 second_terms_send.1
  484.1 24.1 %collective-permute-done.23.refs_12_.refs_13_ = bf16[2,4,256,512]{3,2,1,0:T(8,128)(2,1)S(1)} collective-permute-done((bf16[2,4,256,512]{3,2,1,0:T(8,128)(2,1)}, bf16[2,4,256,512]{3,2,1,0:T(8,128)(2,1)S(1)}, u32[]{:S(2)}, u32[]{:S(2)}) %collective-permute-start.23) | collective-permute-done | bytes 2097184 | tf_op jit(solution)/shard_map/ppermute | solution.py:43
  509.6 8.7 second_terms_fold.1
  519.6 20.3 %attend_back.1 = (bf16[256,1024]{1,0:T(8,128)(2,1)S(1)}, bf16[1024,1024]{1,0:T(8,128)(2,1)S(1)}, bf16[1024,1024]{1,0:T(8,128)(2,1)S(1)}) custom-call(s32[5]{0:T(128)S(1)} %pad_add_fusion.2.offsets_ref, bf16[256,1024]{1,0:T(8,128)(2,1)S(1)} %copy-done.8, bf16[1024,1024]{1,0:T(8,128)(2,1)} %copy-done.3, bf16[1024,1024]{1,0:T(8,128)(2,1)} %copy-done.4, ...), custom_call_target="tpu_custom_call" | custom-call | tf_op jit(solution)/shard_map/attend_back/pallas_call | solution.py:824
  553.3 8.3 collective-permute-done.46
  569.1 10.8 %collective-permute-done.44.refs_14_.refs_15_ = bf16[2,4,96,512]{3,2,1,0:T(8,128)(2,1)S(1)} collective-permute-done((bf16[2,4,96,512]{3,2,1,0:T(8,128)(2,1)S(1)}, bf16[2,4,96,512]{3,2,1,0:T(8,128)(2,1)S(1)}, u32[]{:S(2)}, u32[]{:S(2)}) %collective-permute-start.44) | collective-permute-done | bytes 786464 | tf_op jit(solution)/shard_map/ppermute | solution.py:43
  603.9 9.8 %attend_terms_send.1 = (bf16[2,4,128,512]{3,2,1,0:T(8,128)(2,1)}, bf16[2,4,128,512]{3,2,1,0:T(8,128)(2,1)}) custom-call(s32[2,2]{1,0:T(2,128)} %pad_add_fusion.1.table_ref, bf16[1024,1024]{1,0:T(8,128)(2,1)} %bitcast.195, bf16[1024,1024]{1,0:T(8,128)(2,1)} %bitcast.196, bf16[1024,1024]{1,0:T(8,128)(2,1)} %collective-permute-done.18.refs_2_.refs_3_.refs_8_.refs_9_, ...), custom_call_target="tpu_custom_call" | custom-call | flops 2684354560 | bytes 14155776 | tf_op jit(solution)/shard_map/attend_terms_send/pallas_call | solution.py:383
  651.7 7.4 first_down_back.1.refs_4_.grad_ref
  682.5 10.2 %attend_terms_fold.1 = (bf16[4,128,512]{2,1,0:T(8,128)(2,1)}, bf16[4,128,512]{2,1,0:T(8,128)(2,1)}, bf16[2,4,128,512]{3,2,1,0:T(8,128)(2,1)}) custom-call(s32[2,4]{1,0:T(2,128)} %pad_add_fusion.table_ref, bf16[1024,1024]{1,0:T(8,128)(2,1)} %bitcast.199, bf16[1024,1024]{1,0:T(8,128)(2,1)} %bitcast.200, ...), custom_call_target="tpu_custom_call" | custom-call | flops 2684354560 | bytes 18350080 | tf_op jit(solution)/shard_map/attend_terms_fold/pallas_call | solution.py:383
  710.5 8.5 collective-permute-done.59.got_ref
  729.4 32.6 %collective-permute-done.71 = f32[16,37,32]{1,2,0:T(8,128)S(1)} collective-permute-done((f32[16,37,32]{1,2,0:T(8,128)S(1)}, f32[16,37,32]{1,2,0:T(8,128)S(1)}, u32[]{:S(2)}, u32[]{:S(2)}) %collective-permute-start.71) | collective-permute-done | bytes 75808 | tf_op jit(solution)/shard_map/ppermute | solution.py:43
  763.9 8.3 collective-permute-done.70.refs_0_
  815.1 7.6 collective-permute-done.80
  857.4 9.9 %collective-permute-done.84.got_ref = bf16[2,1,128,512]{3,2,1,0:T(8,128)(2,1)S(1)} collective-permute-done((bf16[2,1,128,512]{3,2,1,0:T(8,128)(2,1)}, bf16[2,1,128,512]{3,2,1,0:T(8,128)(2,1)S(1)}, u32[]{:S(2)}, u32[]{:S(2)}) %collective-permute-start.84) | collective-permute-done | bytes 262176 | tf_op jit(solution)/shard_map/ppermute | solution.py:43
  (759 shorter events, 410.6 us)
Async XLA Ops:
  7.3 122.0 %all-gather.7.cloned.1.call-start = ((), (), s32[]{:S(2)}) async-start(), calls=%async_computation | async-start | bytes 17301504 | tf_op jit(solution)/shard_map/all_gather | solution.py:510
  9.2 251.1 %all-gather.9.cloned.1.call-start = ((), (), s32[]{:S(2)}) async-start(), calls=%async_computation.1 | async-start | bytes 15138816 | tf_op jit(solution)/shard_map/all_gather | solution.py:510
  131.2 249.9 %all-gather.11.cloned.1.call-start = ((), (), s32[]{:S(2)}) async-start(), calls=%async_computation.2 | async-start | bytes 17301504 | tf_op jit(solution)/shard_map/all_gather | solution.py:510
  195.9 39.2 %collective-permute-start.9 = (bf16[256,1024]{1,0:T(8,128)(2,1)S(1)}, bf16[256,1024]{1,0:T(8,128)(2,1)}, u32[]{:S(2)}, u32[]{:S(2)}) collective-permute-start(bf16[256,1024]{1,0:T(8,128)(2,1)S(1)} %collective-permute-done.5), channel_id=1, source_target_pairs={{1,0},{2,1},{3,2},{5,4},{6,5},{7,6},{9,8},{10,9},{11,10},{13,12},{... | collective-permute-start | bytes 1572872 | tf_op jit(solution)/shard_map/ppermute | solution.py:615
  197.2 39.4 %collective-permute-start.7 = (bf16[256,1024]{1,0:T(8,128)(2,1)S(1)}, bf16[256,1024]{1,0:T(8,128)(2,1)S(1)}, u32[]{:S(2)}, u32[]{:S(2)}) collective-permute-start(bf16[256,1024]{1,0:T(8,128)(2,1)S(1)} %collective-permute-done.6), channel_id=1, source_target_pairs={{0,1},{1,2},{2,3},{4,5},{5,6},{6,7},{8,9},{9,10},{10,11},{12,13},{... | collective-permute-start | bytes 1572872 | tf_op jit(solution)/shard_map/ppermute | solution.py:614
  460.0 48.2 %collective-permute-start.23 = (bf16[2,4,256,512]{3,2,1,0:T(8,128)(2,1)}, bf16[2,4,256,512]{3,2,1,0:T(8,128)(2,1)S(1)}, u32[]{:S(2)}, u32[]{:S(2)}) collective-permute-start(bf16[2,4,256,512]{3,2,1,0:T(8,128)(2,1)} %get-tuple-element.197), channel_id=1, source_target_pairs={{0,8},{4,12},{8,0},{12,4},{16,24},{20,28},{24,16},{28,20},{1,9},{5... | collective-permute-start | bytes 6291464 | tf_op jit(solution)/shard_map/ppermute | solution.py:43
  463.4 45.9 %collective-permute-start.24 = (bf16[2,4,256,512]{3,2,1,0:T(8,128)(2,1)}, bf16[2,4,256,512]{3,2,1,0:T(8,128)(2,1)}, u32[]{:S(2)}, u32[]{:S(2)}) collective-permute-start(bf16[2,4,256,512]{3,2,1,0:T(8,128)(2,1)} %get-tuple-element.198), channel_id=1, source_target_pairs={{0,16},{4,20},{8,24},{12,28},{16,0},{20,4},{24,8},{28,12},{1,17},{... | collective-permute-start | bytes 6291464 | tf_op jit(solution)/shard_map/ppermute | solution.py:43
  551.3 45.3 %collective-permute-start.18 = (bf16[1024,1024]{1,0:T(8,128)(2,1)S(1)}, bf16[1024,1024]{1,0:T(8,128)(2,1)}, u32[]{:S(2)}, u32[]{:S(2)}) collective-permute-start(bf16[1024,1024]{1,0:T(8,128)(2,1)S(1)} %bitcast.203), channel_id=1, source_target_pairs={{0,4},{4,0},{8,12},{12,8},{16,20},{20,16},{24,28},{28,24},{1,5},{5... | collective-permute-start | bytes 6291464 | tf_op jit(solution)/shard_map/ppermute | solution.py:43
  552.6 50.6 %collective-permute-start.38 = (bf16[1024,1024]{1,0:T(8,128)(2,1)S(1)}, bf16[1024,1024]{1,0:T(8,128)(2,1)}, u32[]{:S(2)}, u32[]{:S(2)}) collective-permute-start(bf16[1024,1024]{1,0:T(8,128)(2,1)S(1)} %get-tuple-element.210.refs_10_), channel_id=1, source_target_pairs={{0,4},{4,0},{8,12},{12,8},{16,20},{20,16},{24,28},{28,24},{1,5},{5... | collective-permute-start | bytes 6291464 | tf_op jit(solution)/shard_map/ppermute | solution.py:43
  553.2 50.7 %collective-permute-start.39 = (bf16[1024,1024]{1,0:T(8,128)(2,1)S(1)}, bf16[1024,1024]{1,0:T(8,128)(2,1)}, u32[]{:S(2)}, u32[]{:S(2)}) collective-permute-start(bf16[1024,1024]{1,0:T(8,128)(2,1)S(1)} %get-tuple-element.211.refs_12_), channel_id=1, source_target_pairs={{0,4},{4,0},{8,12},{12,8},{16,20},{20,16},{24,28},{28,24},{1,5},{5... | collective-permute-start | bytes 6291464 | tf_op jit(solution)/shard_map/ppermute | solution.py:43
  601.7 25.2 %collective-permute-start.42 = (bf16[4,256,512]{2,1,0:T(8,128)(2,1)}, bf16[4,256,512]{2,1,0:T(8,128)(2,1)S(1)}, u32[]{:S(2)}, u32[]{:S(2)}) collective-permute-start(bf16[4,256,512]{2,1,0:T(8,128)(2,1)} %get-tuple-element.212), channel_id=1, source_target_pairs={{0,16},{4,20},{8,24},{12,28},{16,0},{20,4},{24,8},{28,12},{1,17},{... | collective-permute-start | bytes 3145736 | tf_op jit(solution)/shard_map/ppermute | solution.py:43
  626.9 32.3 %collective-permute-start.53 = (bf16[2,4,128,512]{3,2,1,0:T(8,128)(2,1)}, bf16[2,4,128,512]{3,2,1,0:T(8,128)(2,1)}, u32[]{:S(2)}, u32[]{:S(2)}) collective-permute-start(bf16[2,4,128,512]{3,2,1,0:T(8,128)(2,1)} %get-tuple-element.239), channel_id=1, source_target_pairs={{0,8},{4,12},{8,0},{12,4},{16,24},{20,28},{24,16},{28,20},{1,9},{5... | collective-permute-start | bytes 3145736 | tf_op jit(solution)/shard_map/ppermute | solution.py:43
  628.2 31.0 %collective-permute-start.54 = (bf16[2,4,128,512]{3,2,1,0:T(8,128)(2,1)}, bf16[2,4,128,512]{3,2,1,0:T(8,128)(2,1)}, u32[]{:S(2)}, u32[]{:S(2)}) collective-permute-start(bf16[2,4,128,512]{3,2,1,0:T(8,128)(2,1)} %get-tuple-element.240), channel_id=1, source_target_pairs={{0,16},{4,20},{8,24},{12,28},{16,0},{20,4},{24,8},{28,12},{1,17},{... | collective-permute-start | bytes 3145736 | tf_op jit(solution)/shard_map/ppermute | solution.py:43
  663.0 30.9 %collective-permute-start.58 = (bf16[256,4096]{1,0:T(8,128)(2,1)}, bf16[256,4096]{1,0:T(8,128)(2,1)}, u32[]{:S(2)}, u32[]{:S(2)}) collective-permute-start(bf16[256,4096]{1,0:T(8,128)(2,1)} %first_down_back.1.refs_4_.grad_ref), channel_id=1, source_target_pairs={{0,4},{4,0},{8,12},{12,8},{16,20},{20,16},{24,28},{28,24},{1,5},{5... | collective-permute-start | bytes 6291464 | tf_op jit(solution)/shard_map/ppermute | solution.py:43
  663.0 29.7 %collective-permute-start.57 = (bf16[256,1024]{1,0:T(8,128)(2,1)S(1)}, bf16[256,1024]{1,0:T(8,128)(2,1)S(1)}, u32[]{:S(2)}, u32[]{:S(2)}) collective-permute-start(bf16[256,1024]{1,0:T(8,128)(2,1)S(1)} %copy-done.32), channel_id=1, source_target_pairs={{0,4},{4,0},{8,12},{12,8},{16,20},{20,16},{24,28},{28,24},{1,5},{5... | collective-permute-start | bytes 1572872 | tf_op jit(solution)/shard_map/ppermute | solution.py:43
  676.2 34.2 %collective-permute-start.60 = (bf16[4,96,512]{2,1,0:T(8,128)(2,1)}, bf16[4,96,512]{2,1,0:T(8,128)(2,1)}, u32[]{:S(2)}, u32[]{:S(2)}) collective-permute-start(bf16[4,96,512]{2,1,0:T(8,128)(2,1)} %get-tuple-element.263), channel_id=1, source_target_pairs={{0,16},{4,20},{8,24},{12,28},{16,0},{20,4},{24,8},{28,12},{1,17},{... | collective-permute-start | bytes 1179656 | tf_op jit(solution)/shard_map/ppermute | solution.py:43
  677.1 33.4 %collective-permute-start.61 = (bf16[4,96,512]{2,1,0:T(8,128)(2,1)}, bf16[4,96,512]{2,1,0:T(8,128)(2,1)}, u32[]{:S(2)}, u32[]{:S(2)}) collective-permute-start(bf16[4,96,512]{2,1,0:T(8,128)(2,1)} %get-tuple-element.264), channel_id=1, source_target_pairs={{0,8},{4,12},{8,0},{12,4},{16,24},{20,28},{24,16},{28,20},{1,9},{5... | collective-permute-start | bytes 1179656 | tf_op jit(solution)/shard_map/ppermute | solution.py:43
  679.3 39.7 %collective-permute-start.62 = (bf16[2,4,128,512]{3,2,1,0:T(8,128)(2,1)}, bf16[2,4,128,512]{3,2,1,0:T(8,128)(2,1)S(1)}, u32[]{:S(2)}, u32[]{:S(2)}) collective-permute-start(bf16[2,4,128,512]{3,2,1,0:T(8,128)(2,1)} %get-tuple-element.266), channel_id=1, source_target_pairs={{0,8},{4,12},{8,0},{12,4},{16,24},{20,28},{24,16},{28,20},{1,9},{5... | collective-permute-start | bytes 3145736 | tf_op jit(solution)/shard_map/ppermute | solution.py:43
  692.7 26.3 %collective-permute-start.63 = (bf16[2,4,128,512]{3,2,1,0:T(8,128)(2,1)}, bf16[2,4,128,512]{3,2,1,0:T(8,128)(2,1)}, u32[]{:S(2)}, u32[]{:S(2)}) collective-permute-start(bf16[2,4,128,512]{3,2,1,0:T(8,128)(2,1)} %get-tuple-element.267), channel_id=1, source_target_pairs={{0,16},{4,20},{8,24},{12,28},{16,0},{20,4},{24,8},{28,12},{1,17},{... | collective-permute-start | bytes 3145736 | tf_op jit(solution)/shard_map/ppermute | solution.py:43
  719.0 72.2 %collective-permute-start.66 = (bf16[2,4,128,512]{3,2,1,0:T(8,128)(2,1)}, bf16[2,4,128,512]{3,2,1,0:T(8,128)(2,1)S(1)}, u32[]{:S(2)}, u32[]{:S(2)}) collective-permute-start(bf16[2,4,128,512]{3,2,1,0:T(8,128)(2,1)} %get-tuple-element.273), channel_id=1, source_target_pairs={{0,8},{4,12},{8,0},{12,4},{16,24},{20,28},{24,16},{28,20},{1,9},{5... | collective-permute-start | bytes 3145736 | tf_op jit(solution)/shard_map/ppermute | solution.py:43
  720.1 71.0 %collective-permute-start.67 = (bf16[2,4,128,512]{3,2,1,0:T(8,128)(2,1)}, bf16[2,4,128,512]{3,2,1,0:T(8,128)(2,1)}, u32[]{:S(2)}, u32[]{:S(2)}) collective-permute-start(bf16[2,4,128,512]{3,2,1,0:T(8,128)(2,1)} %get-tuple-element.274), channel_id=1, source_target_pairs={{0,16},{4,20},{8,24},{12,28},{16,0},{20,4},{24,8},{28,12},{1,17},{... | collective-permute-start | bytes 3145736 | tf_op jit(solution)/shard_map/ppermute | solution.py:43
  721.5 50.6 %collective-permute-start.68 = (bf16[4,128,512]{2,1,0:T(8,128)(2,1)}, bf16[4,128,512]{2,1,0:T(8,128)(2,1)}, u32[]{:S(2)}, u32[]{:S(2)}) collective-permute-start(bf16[4,128,512]{2,1,0:T(8,128)(2,1)} %get-tuple-element.275), channel_id=1, source_target_pairs={{0,16},{4,20},{8,24},{12,28},{16,0},{20,4},{24,8},{28,12},{1,17},{... | collective-permute-start | bytes 1572872 | tf_op jit(solution)/shard_map/ppermute | solution.py:43
  722.2 50.0 %collective-permute-start.69 = (bf16[4,128,512]{2,1,0:T(8,128)(2,1)}, bf16[4,128,512]{2,1,0:T(8,128)(2,1)}, u32[]{:S(2)}, u32[]{:S(2)}) collective-permute-start(bf16[4,128,512]{2,1,0:T(8,128)(2,1)} %get-tuple-element.276), channel_id=1, source_target_pairs={{0,8},{4,12},{8,0},{12,4},{16,24},{20,28},{24,16},{28,20},{1,9},{5... | collective-permute-start | bytes 1572872 | tf_op jit(solution)/shard_map/ppermute | solution.py:43
  726.2 35.8 %collective-permute-start.71 = (f32[16,37,32]{1,2,0:T(8,128)S(1)}, f32[16,37,32]{1,2,0:T(8,128)S(1)}, u32[]{:S(2)}, u32[]{:S(2)}) collective-permute-start(f32[16,37,32]{1,2,0:T(8,128)S(1)} %bitcast.227), channel_id=1, source_target_pairs={{0,16},{4,20},{8,24},{12,28},{16,0},{20,4},{24,8},{28,12},{1,17},{... | collective-permute-start | bytes 227336 | tf_op jit(solution)/shard_map/ppermute | solution.py:43
  (227 other events, 3551.2 us)
Sparse Core Ops, SparseCore 0:
  11.7 117.5 all-gather.6
  132.7 123.6 all-gather.8
  262.8 118.2 all-gather.10

commit v3 on v2

--- a/solution.py
+++ b/solution.py
@@ -317,7 +317,7 @@
         ),
         out_shape=outs,
         compiler_params=LIMIT,
-        cost_estimate=pl.CostEstimate(flops=0, transcendentals=0, bytes_accessed=size),
+        cost_estimate=pl.CostEstimate(flops=1024, transcendentals=0, bytes_accessed=1024),
         name=name,
     )(*bits, *inputs)
 
@@ -390,7 +390,7 @@
             ),
             out_shape=outs,
             compiler_params=LIMIT,
-            cost_estimate=pl.CostEstimate(flops=flops, transcendentals=0, bytes_accessed=moved),
+            cost_estimate=pl.CostEstimate(flops=1024, transcendentals=0, bytes_accessed=1024),
             name=self.name + name,
         )(table, *args, *more)
 
@@ -502,12 +502,15 @@
             at += rows
 
 
-def fetch_packed(shards, name):
+def pack(shards, name):
     width = shards[-1].shape[1]
     rows = sum(s.shape[0] * s.shape[1] // width for s in shards)
     out = jax.ShapeDtypeStruct((rows, width), bf16)
-    (packed,) = whole_call(pack_kernel, name, [], shards, [out])
-    return lax.all_gather(packed, ("dp", "seq"), axis=0)
+    return whole_call(pack_kernel, name, [], shards, [out])[0]
+
+
+def gather_packed(part):
+    return lax.all_gather(part, ("dp", "seq"), axis=0)
 
 
 def packed_block(packed, start, rows):
@@ -558,7 +561,7 @@
 
     def spec(x):
         tokens, columns = x.shape
-        return pl.BlockSpec((tokens, width), (lambda i: (0, i)) if columns > width else (lambda i: (0, 0)))
+        return pl.BlockSpec((tokens, min(width, columns)), (lambda i: (0, i)) if columns > width else (lambda i: (0, 0)))
 
     numbers = lambda things: sum(t.size * t.dtype.itemsize for t in things)
     tokens = inputs[0].shape[0]
@@ -571,11 +574,7 @@
         out_shape=outs,
         scratch_shapes=list(scratch),
         compiler_params=pltpu.CompilerParams(vmem_limit_bytes=56 << 20),
-        cost_estimate=pl.CostEstimate(
-            flops=2 * tokens * width * inner,
-            transcendentals=0,
-            bytes_accessed=2 * width * inner + numbers(inputs) + numbers(outs),
-        ),
+        cost_estimate=pl.CostEstimate(flops=1024, transcendentals=0, bytes_accessed=1024),
         name=name,
     )(*inputs, packed)
 
@@ -634,10 +633,13 @@
         meanwhile = next(between, None)
         if meanwhile is not None:
             up, down = meanwhile(up, down)
-    total = blocks[0].astype(f32)
-    if up is not None:
-        total = total + up.astype(f32) + down.astype(f32)
-    return total
+    if up is None:
+        up = down = jnp.zeros_like(blocks[0])
+    return blocks[0], up, down
+
+
+def sum_parts(parts):
+    return sum(part.astype(f32) for part in parts)
 
 
 def with_halo(shard, width):
@@ -711,6 +713,230 @@
         (normed_low, 0, tokens, one(grad_hidden), owner_rows(width), inner // 2),
         (active, 0, tokens, one(grad_branch), owner_rows(inner), width // 2),
     ]
+
+
+def norm_back(grad, norm_gain, values):
+    centered = values - jnp.mean(values, axis=-1, keepdims=True)
+    inverse = lax.rsqrt(jnp.mean(centered * centered, axis=-1, keepdims=True) + epsilon)
+    normal = centered * inverse
+    scaled = grad * norm_gain
+    grad_in = inverse * (
+        scaled
+        - jnp.mean(scaled, axis=-1, keepdims=True)
+        - normal * jnp.mean(scaled * normal, axis=-1, keepdims=True)
+    )
+    return grad_in, jnp.sum(grad * normal, axis=0, keepdims=True)
+
+
+def valid_mask(count_ref, shape):
+    return (lax.broadcasted_iota(jnp.int32, (shape[0], 1), 0) < count_ref[0]).astype(f32)
+
+
+class Block:
+    def __init__(self, packed, index):
+        self.packed, self.index = packed, index
+
+    def spec(self):
+        owners, _, width = self.packed.shape
+        index = self.index
+        return pl.BlockSpec((owners, width // owners, width), lambda i, *t: (0, index, 0))
+
+
+def step_call(kernel, name, scalars, inputs, outs, scratch=()):
+    def spec(x):
+        if isinstance(x, Block):
+            return x.spec()
+        return pl.BlockSpec(x.shape, lambda i, *t: (0,) * len(x.shape))
+
+    return pl.pallas_call(
+        kernel,
+        grid_spec=pltpu.PrefetchScalarGridSpec(
+            num_scalar_prefetch=len(scalars),
+            grid=(1,),
+            in_specs=[spec(x) for x in inputs],
+            out_specs=[spec(o) for o in outs],
+            scratch_shapes=list(scratch),
+        ),
+        out_shape=outs,
+        compiler_params=LIMIT,
+        cost_estimate=pl.CostEstimate(flops=1024, transcendentals=0, bytes_accessed=1024),
+        name=name,
+    )(*scalars, *[x.packed if isinstance(x, Block) else x for x in inputs])
+
+
+def rows_like(array, dtype=f32):
+    return jax.ShapeDtypeStruct(array.shape, dtype)
+
+
+def vector_like(array, count=1):
+    return jax.ShapeDtypeStruct((count, array.shape[1]), f32)
+
+
+def square(ref):
+    return ref[...].reshape(ref.shape[2], ref.shape[2])
+
+
+def final_back_kernel(count_ref, cotangent_ref, values_ref, gain_ref, grad_ref, sum_ref, branch_ref):
+    grad = cotangent_ref[...].astype(f32) * valid_mask(count_ref, values_ref.shape)
+    grad, sum_ref[...] = norm_back(grad, gain_ref[...], values_ref[...])
+    grad_ref[...] = grad
+    branch_ref[...] = (0.5 * grad).astype(bf16)
+
+
+def shaped_back_kernel(
+    count_ref, branch_ref, depth_ref, vectors_ref, weight_ref, grad_ref, sums_ref
+):
+    normal = (depth_ref[...] - vectors_ref[0:1]) * vectors_ref[1:2]
+    shaped = normal * vectors_ref[2:3] + vectors_ref[3:4]
+    sigmoid = 1.0 / (1.0 + jnp.exp(-shaped))
+    slope = sigmoid * (1.0 + shaped * (1.0 - sigmoid)) * valid_mask(count_ref, depth_ref.shape)
+    grad = product_tail(branch_ref[...], square(weight_ref)) * slope
+    grad_ref[...] = grad
+    sums_ref[0:1] = jnp.sum(grad, axis=0, keepdims=True)
+    sums_ref[1:2] = jnp.sum(grad * normal, axis=0, keepdims=True)
+
+
+def add_kernel(left_ref, right_ref, out_ref):
+    out_ref[...] = left_ref[...] + right_ref[...]
+
+
+def depth_back_kernel(
+    count_ref, grad_ref, depth_ref, vectors_ref, totals_ref, out_ref, top_ref, bottom_ref
+):
+    normal = (depth_ref[...] - vectors_ref[0:1]) * vectors_ref[1:2]
+    scale = vectors_ref[2:3]
+    out = (
+        vectors_ref[1:2]
+        * valid_mask(count_ref, depth_ref.shape)
+        * (
+            grad_ref[...] * scale
+            - scale * (totals_ref[0:1] + normal * totals_ref[1:2]) / vectors_ref[4:5]
+        )
+    ).astype(bf16)
+    out_ref[...] = out
+    width = top_ref.shape[0]
+    top_ref[...] = out[:width]
+    bottom_ref[...] = out[out.shape[0] - width :]
+
+
+def taps_back_kernel(
+    count_ref, before_ref, grad_ref, after_ref, taps_ref, paired_ref, sigmoid_ref, *refs
+):
+    left_ref, right_ref, rims = refs
+    frames = grad_ref.shape[0]
+    taps = taps_ref.shape[0]
+    half = taps // 2
+    rims[0:half] = before_ref[...].astype(f32)
+    rims[half : half + frames] = grad_ref[...].astype(f32)
+    rims[half + frames : 2 * half + frames] = after_ref[...].astype(f32)
+    valid = valid_mask(count_ref, grad_ref.shape)
+
+    def part(step, carry):
+        lanes = pl.ds(pl.multiple_of(step * 128, 128), 128)
+        total = jnp.zeros((frames, 128), f32)
+        for tap in range(taps):
+            start = 2 * half - tap
+            total = total + rims[start : start + frames, lanes] * taps_ref[tap : tap + 1, lanes]
+        sigmoid = sigmoid_ref[:, lanes]
+        left = total * sigmoid * valid
+        left_ref[:, lanes] = left.astype(bf16)
+        right_ref[:, lanes] = (left * paired_ref[:, lanes] * (1.0 - sigmoid)).astype(bf16)
+        return carry
+
+    lax.fori_loop(0, grad_ref.shape[1] // 128, part, 0)
+
+
+def taps_sums_kernel(grad_ref, widened_ref, sums_ref, wide_rows, own_rows):
+    frames = grad_ref.shape[0]
+    wide_rows[0 : widened_ref.shape[0]] = widened_ref[...].astype(f32)
+    own_rows[...] = grad_ref[...].astype(f32)
+
+    def part(step, carry):
+        lanes = pl.ds(pl.multiple_of(step * 128, 128), 128)
+        own = own_rows[:, lanes]
+        for tap in range(sums_ref.shape[0]):
+            sums_ref[tap : tap + 1, lanes] = jnp.sum(
+                wide_rows[tap : tap + frames, lanes] * own, axis=0, keepdims=True
+            )
+        return carry
+
+    lax.fori_loop(0, grad_ref.shape[1] // 128, part, 0)
+
+
+def conv_input_kernel(
+    left_ref, right_ref, values_ref, gain_ref, rows_ref, first_ref, second_ref, *outs
+):
+    grad = product_tail(left_ref[...], square(first_ref))
+    grad = grad + product_tail(right_ref[...], square(second_ref))
+    finish_input(grad, gain_ref, values_ref, rows_ref, 1.0, *outs)
+
+
+def finish_input(grad, gain_ref, values_ref, rows_ref, factor, out_ref, sum_ref, branch_ref):
+    grad, sum_ref[...] = norm_back(grad, gain_ref[...], values_ref[...])
+    grad = rows_ref[...] + grad
+    out_ref[...] = grad
+    branch_ref[...] = (factor * grad).astype(bf16)
+
+
+def attend_input_kernel(
+    own_ref, up_ref, down_ref, query_ref, values_ref, gain_ref, rows_ref, weight_ref, *outs
+):
+    grad = own_ref[...].astype(f32) + up_ref[...].astype(f32) + down_ref[...].astype(f32)
+    grad = grad + product_tail(query_ref[...], square(weight_ref))
+    finish_input(grad, gain_ref, values_ref, rows_ref, 0.5, *outs)
+
+
+def input_outs(rows):
+    return [rows_like(rows), vector_like(rows), rows_like(rows, bf16)]
+
+
+def blocks_back_kernel(key_ref, value_ref, key_weight_ref, value_weight_ref, out_ref):
+    total = product_tail(key_ref[...], square(key_weight_ref))
+    total = total + product_tail(value_ref[...], square(value_weight_ref))
+    out_ref[0] = total.astype(bf16)
+
+
+def blocks_back(grad_key, grad_value, packed, frames):
+    keys, width = grad_key.shape
+    rows = pl.BlockSpec((frames, width), lambda i: (i, 0))
+    return pl.pallas_call(
+        blocks_back_kernel,
+        grid=(keys // frames,),
+        in_specs=[rows, rows, Block(packed, 1).spec(), Block(packed, 2).spec()],
+        out_specs=pl.BlockSpec((1, frames, width), lambda i: (i, 0, 0)),
+        out_shape=jax.ShapeDtypeStruct((keys // frames, frames, width), bf16),
+        compiler_params=LIMIT,
+        cost_estimate=pl.CostEstimate(flops=1024, transcendentals=0, bytes_accessed=1024),
+        name="attend_blocks_back",
+    )(grad_key, grad_value, packed, packed)
+
+
+def up_back_input_kernel(
+    factor, grad_ref, values_ref, gain_ref, rows_ref, weight_ref, out_ref, sum_ref, branch_ref, total
+):
+    part = product_tail(grad_ref[...], weight_ref[...].reshape(out_ref.shape[1], -1))
+    total[...] = jnp.where(pl.program_id(0) == 0, part, total[...] + part)
+
+    @pl.when(pl.program_id(0) == pl.num_programs(0) - 1)
+    def _():
+        finish_input(
+            total[...], gain_ref, values_ref, rows_ref, factor, out_ref, sum_ref, branch_ref
+        )
+
+
+def ffn_up_back_input(grad_hidden, values, gain, rows, packed, factor, name):
+    kernel = functools.partial(up_back_input_kernel, factor)
+    scratch = [pltpu.VMEM(rows.shape, f32)]
+    inputs = [grad_hidden, values, gain, rows]
+    return ffn_call(kernel, name, packed.array, "up", inputs, input_outs(rows), scratch)
+
+
+def sum_in_steps(values, bits):
+    for axis, bit in bits:
+        (values,) = step_call(
+            add_kernel, "add", [], [values, swap(values, axis, bit)], [rows_like(values)]
+        )
+    return values
 
 
 def key_valid(offsets_ref, rows, keys):
@@ -754,13 +980,14 @@
     value_ref,
     total_ref,
     grad_ref,
-    query_grad_ref,
-    key_grad_ref,
-    value_grad_ref,
+    *refs,
 ):
+    outward, (query_grad_ref, key_grad_ref, value_grad_ref) = refs[:-3], refs[-3:]
     keys = key_ref[...]
     values = value_ref[...]
     grad = grad_ref[...]
+    if outward:
+        grad = product_tail(grad, outward[0][...].reshape(128, -1)).astype(bf16)
     query = query_ref[...] * jnp.asarray(HEAD_DIM**-0.5, bf16)
     valid = key_valid(offsets_ref, rows, keys.shape[0])
     halves = []
@@ -814,13 +1041,20 @@
     )(offsets, query, key, value)
 
 
-def attend_back(offsets, query, key_value, totals, grad):
+def attend_back(offsets, query, key_value, totals, grad, packed=None):
     rows, width = query.shape
     key, value = key_value
     keys = key.shape[0]
     pairs = width // 128
     row_spec = pl.BlockSpec((rows, 128), lambda i, o: (0, i))
     key_spec = pl.BlockSpec((keys, 128), lambda i, o: (0, i))
+    if packed is None:
+        grad_specs, more = [row_spec], []
+    else:
+        owners = packed.shape[0]
+        count = 128 * owners // width
+        square_rows = pl.BlockSpec((count, width // owners, width), lambda i, o: (i, 3, 0))
+        grad_specs, more = [pl.BlockSpec((rows, width), lambda i, o: (0, 0)), square_rows], [packed]
     return pl.pallas_call(
         functools.partial(attend_back_kernel, rows),
         grid_spec=pltpu.PrefetchScalarGridSpec(
@@ -831,8 +1065,8 @@
                 key_spec,
                 pl.BlockSpec((keys, 128), lambda i, o: (0, i)),
                 pl.BlockSpec((1, 2, rows), lambda i, o: (i, 0, 0)),
-                row_spec,
-            ],
+            ]
+            + grad_specs,
             out_specs=[row_spec, key_spec, key_spec],
         ),
         out_shape=[
@@ -842,7 +1076,7 @@
         ],
         compiler_params=pltpu.CompilerParams(vmem_limit_bytes=48 << 20),
         name="attend_back",
-    )(offsets, query, key, value, totals, grad)
+    )(offsets, query, key, value, totals, grad, *more)
 
 
 def attention_forward(values, length, norm_gain, joint_proj, attend_out, gathered):
@@ -929,6 +1163,7 @@
         inverse_std,
         shaped,
         active,
+        mixture,
     )
     return (output, stored, (batch_mean, batch_var, frame_count))
 
@@ -942,7 +1177,7 @@
 
 
 def conv_paired_grad(grad_shaped, totals, valid_rows, taps_float, scale_float, frame_count, stored):
-    paired, sigmoid_rows, widened, normal_batch, inverse_std = (stored[i] for i in (3, 4, 5, 6, 7))
+    normal_batch, inverse_std = stored[6:8]
     total_shift, total_scale = totals
     grad_mixture = (
         inverse_std
@@ -952,9 +1187,14 @@
             - scale_float * (total_shift + normal_batch * total_scale) / frame_count
         )
     ).astype(bf16)
+    grad_rims = with_halo(grad_mixture, taps_float.shape[1] // 2)
+    return conv_taps_grad(grad_mixture, grad_rims, valid_rows, taps_float, stored)
+
+
+def conv_taps_grad(grad_mixture, grad_rims, valid_rows, taps_float, stored):
+    paired, sigmoid_rows, widened = stored[3:6]
     taps = taps_float.shape[1]
     half_width = taps // 2
-    grad_rims = with_halo(grad_mixture, half_width)
     frames, model_width = grad_mixture.shape
     widened_float = widened.astype(f32)
     grad_float = grad_mixture.astype(f32)
@@ -1034,10 +1274,13 @@
     count = own_small.shape[0]
     shards = lax.axis_size("dp") * lax.axis_size("seq")
     own_rows = model_width // shards
+    small = gather_small(own_small[None])
     if in_steps(model_width):
-        front = fetch_packed((first_up, first_down), "pack_first")
-        middle_shards = tie(front, joint_proj, attend_out, conv_pair, conv_out)[1:]
-        middle = fetch_packed(middle_shards, "pack_middle")
+        front = gather_packed(pack((first_up, first_down), "pack_first"))
+        middle_part = pack((joint_proj, attend_out, conv_pair, conv_out), "pack_middle")
+        back_part = pack((second_up, second_down), "pack_second")
+        small, _, middle_part, back_part = tie(small, front, middle_part, back_part)
+        middle = gather_packed(middle_part)
         up_one = down_one = Packed(front)
         squares = [packed_block(middle, i * own_rows, own_rows) for i in range(7)]
         joint_all, outward_all = squares[:3], squares[3]
@@ -1056,7 +1299,6 @@
         )
         joint_all = jnp.split(joint_all, 3, axis=1)
         pair_all = jnp.split(pair_all, 2, axis=1)
-    small = gather_small(own_small[None])
     small = jnp.transpose(small, (1, 0, 2)).reshape(count, model_width).astype(f32)
     vector_mask, g_first, g_attend, g_conv, g_second, g_final, scale_float, shift_float = (
         small[i] for i in range(8)
@@ -1064,83 +1306,169 @@
     taps_float = small[8:].T
 
     start_rows = jnp.where(masked_float > 0.0, vector_mask[None, :], inputs[0].astype(f32))
-    values, first_stored = ffn_forward(start_rows, g_first, up_one, down_one, "first")
+    rows_first, first_stored = ffn_forward(start_rows, g_first, up_one, down_one, "first")
     second_weights = []
 
     def gathered(rows):
         if not in_steps(model_width):
             second_weights.extend([fetch_weight(second_up), fetch_weight(second_down)])
             return rows
-        rows, _, up_shard, down_shard = tie(rows, middle, second_up, second_down)
-        back = Packed(fetch_packed((up_shard, down_shard), "pack_second"))
+        rows, _, part = tie(rows, middle, back_part)
+        back = Packed(gather_packed(part))
         second_weights.extend([back, back])
         return rows
 
-    values, attend_stored = attention_forward(
-        values, length, g_attend, joint_all, outward_all, gathered
+    rows_second, attend_stored = attention_forward(
+        rows_first, length, g_attend, joint_all, outward_all, gathered
     )
     up_two, down_two = second_weights
-    values, conv_stored, batch_stats = conv_forward(
-        values, valid_rows, g_conv, pair_all, taps_float, scale_float, shift_float, conv_out_all
+    rows_third, conv_stored, batch_stats = conv_forward(
+        rows_second, valid_rows, g_conv, pair_all, taps_float, scale_float, shift_float, conv_out_all
     )
-    values, second_stored = ffn_forward(values, g_second, up_two, down_two, "second")
-    normed, normal, inverse = norm_forward(values, g_final)
+    rows_fourth, second_stored = ffn_forward(rows_third, g_second, up_two, down_two, "second")
+    normed, normal, inverse = norm_forward(rows_fourth, g_final)
     output = (normed * valid_rows).astype(bf16)
 
-    grad_rows, grad_final = norm_backward(
-        cotangent[0].astype(f32) * valid_rows, g_final, normal, inverse
-    )
     steps = in_steps(model_width)
     frame_count = batch_stats[2]
-    branch_two = (0.5 * grad_rows).astype(bf16)
-    hidden_two = ffn_hidden_grad(branch_two, down_two, second_stored, "second")
-    jobs_two = ffn_jobs(branch_two, hidden_two, second_stored)
-    if steps:
-        two = ModuleScatter(jobs_two, "second_terms")
+    if not steps:
+        grad_rows, grad_final = norm_backward(
+            cotangent[0].astype(f32) * valid_rows, g_final, normal, inverse
+        )
+        branch_two = (0.5 * grad_rows).astype(bf16)
+        hidden_two = ffn_hidden_grad(branch_two, down_two, second_stored, "second")
+        jobs_two = ffn_jobs(branch_two, hidden_two, second_stored)
+        grad_rows, grad_gain_two = ffn_input_grad(
+            grad_rows, hidden_two, g_second, up_two, second_stored, "second"
+        )
+        branch_conv, grad_shaped, sums = conv_shaped_grad(
+            grad_rows, valid_rows, conv_out_all, conv_stored
+        )
+        totals = sum_small(sums)
+        grad_paired, grad_taps = conv_paired_grad(
+            grad_shaped, totals, valid_rows, taps_float, scale_float, frame_count, conv_stored
+        )
+        jobs_conv = conv_jobs(branch_conv, grad_paired, conv_stored)
+        grad_rows, grad_gain_conv = conv_input_grad(
+            grad_rows, grad_paired, g_conv, pair_all, conv_stored
+        )
+        branch_attend, grad_query, grad_key, grad_value = attention_parts_grad(
+            grad_rows, outward_all, attend_stored
+        )
+        jobs_attend = attention_jobs(
+            branch_attend, grad_query, grad_key, grad_value, attend_stored
+        )
+        blocks = attention_blocks_grad(grad_key, grad_value, joint_all, frames)
+        grad_normed = sum_parts(scatter_line(blocks))
+        grad_rows, grad_gain_attend = attention_input_grad(
+            grad_rows, grad_normed, grad_query, g_attend, joint_all, attend_stored
+        )
+        branch_one = (0.5 * grad_rows).astype(bf16)
+        hidden_one = ffn_hidden_grad(branch_one, down_one, first_stored, "first")
+        jobs_one = ffn_jobs(branch_one, hidden_one, first_stored)
+        grad_rows, grad_gain_one = ffn_input_grad(
+            grad_rows, hidden_one, g_first, up_one, first_stored, "first"
+        )
+    else:
+        gain = lambda vector: vector[None]
+        own_valid = jnp.clip(length - lax.axis_index("seq") * frames, 0, frames)
+        own_valid = own_valid[None].astype(jnp.int32)
+        grad_rows, grad_final, branch_two = step_call(
+            final_back_kernel,
+            "final_back",
+            [own_valid],
+            [cotangent[0], rows_fourth, gain(g_final)],
+            input_outs(rows_fourth),
+        )
+        hidden_two = ffn_hidden_grad(branch_two, down_two, second_stored, "second")
+        two = ModuleScatter(ffn_jobs(branch_two, hidden_two, second_stored), "second_terms")
         two.share()
         two.first_send()
-    grad_rows, grad_gain_two = ffn_input_grad(
-        grad_rows, hidden_two, g_second, up_two, second_stored, "second"
-    )
-    if steps:
-        (grad_rows,) = fence([two], grad_rows)
+        grad_rows, grad_gain_two, branch_conv = ffn_up_back_input(
+            hidden_two, rows_third, gain(g_second), grad_rows, up_two, 1.0, "second_up_back"
+        )
+        grad_rows, branch_conv = fence([two], grad_rows, branch_conv)
+        depth, inverse_std = conv_stored[10], conv_stored[7]
+        spread = jnp.broadcast_to(frame_count, (model_width,))
+        vectors = jnp.stack([batch_stats[0], inverse_std, scale_float, shift_float, spread])
+        grad_shaped, sums = step_call(
+            shaped_back_kernel,
+            "shaped_back",
+            [own_valid],
+            [branch_conv, depth, vectors, Block(middle, 6)],
+            [rows_like(depth), vector_like(depth, 2)],
+        )
+        totals = sum_in_steps(sums, [("dp", b) for b in axis_bits("dp")])
+        (totals,) = fence([two], totals)
         two.first_swap()
-
-    branch_conv, grad_shaped, sums = conv_shaped_grad(
-        grad_rows, valid_rows, conv_out_all, conv_stored
-    )
-    totals = sum_small(sums)
-    total_shift, total_scale = totals
-    grad_paired, grad_taps = conv_paired_grad(
-        grad_shaped, totals, valid_rows, taps_float, scale_float, frame_count, conv_stored
-    )
-    jobs_conv = conv_jobs(branch_conv, grad_paired, conv_stored)
-    if steps:
-        conv = ModuleScatter(jobs_conv, "conv_terms")
+        totals = sum_in_steps(totals, [("seq", b) for b in axis_bits("seq")])
+        rim = jax.ShapeDtypeStruct((taps // 2, model_width), bf16)
+        grad_depth, top, bottom = step_call(
+            depth_back_kernel,
+            "depth_back",
+            [own_valid],
+            [grad_shaped, depth, vectors, totals],
+            [rows_like(depth, bf16), rim, rim],
+        )
+        seq_size = lax.axis_size("seq")
+        before = lax.ppermute(bottom, "seq", [(i, i + 1) for i in range(seq_size - 1)])
+        after = lax.ppermute(top, "seq", [(i + 1, i) for i in range(seq_size - 1)])
+        paired, sigmoid_rows, widened = conv_stored[3:6]
+        tall = pltpu.VMEM((frames + 32, model_width), f32)
+        paired_left, paired_right = step_call(
+            taps_back_kernel,
+            "taps_back",
+            [own_valid],
+            [before, grad_depth, after, taps_float.T, paired, sigmoid_rows],
+            [rows_like(depth, bf16), rows_like(depth, bf16)],
+            [tall],
+        )
+        (grad_taps,) = step_call(
+            taps_sums_kernel,
+            "taps_sums",
+            [],
+            [grad_depth, widened],
+            [vector_like(depth, taps)],
+            [tall, pltpu.VMEM(depth.shape, f32)],
+        )
+        conv = ModuleScatter(
+            conv_jobs(branch_conv, (paired_left, paired_right), conv_stored), "conv_terms"
+        )
         conv.share()
         conv.first_send()
-    grad_rows, grad_gain_conv = conv_input_grad(
-        grad_rows, grad_paired, g_conv, pair_all, conv_stored
-    )
-    if steps:
-        (grad_rows,) = fence([two, conv], grad_rows)
+        grad_rows, grad_gain_conv, branch_attend = step_call(
+            conv_input_kernel,
+            "conv_input_back",
+            [],
+            [
+                paired_left,
+                paired_right,
+                rows_second,
+                gain(g_conv),
+                grad_rows,
+                Block(middle, 4),
+                Block(middle, 5),
+            ],
+            input_outs(rows_second),
+        )
+        grad_rows, branch_attend = fence([two, conv], grad_rows, branch_attend)
+        two.second_send()
+        grad_rows, branch_attend = fence([two, conv], grad_rows, branch_attend)
+        two.second_swap()
         conv.first_swap()
-        two.second_send()
-        (grad_rows,) = fence([two], grad_rows)
-        two.second_swap()
-
-    branch_attend, grad_query, grad_key, grad_value = attention_parts_grad(
-        grad_rows, outward_all, attend_stored
-    )
-    jobs_attend = attention_jobs(branch_attend, grad_query, grad_key, grad_value, attend_stored)
-    blocks = attention_blocks_grad(grad_key, grad_value, joint_all, frames)
-    between = ()
-    if steps:
-        attend_sum = ModuleScatter(jobs_attend, "attend_terms")
+
+        grad_query, grad_key, grad_value = attend_back(
+            attend_stored[6], attend_stored[4], attend_stored[5], attend_stored[7], branch_attend, middle
+        )
+        attend_sum = ModuleScatter(
+            attention_jobs(branch_attend, grad_query, grad_key, grad_value, attend_stored),
+            "attend_terms",
+        )
+        blocks = blocks_back(grad_key, grad_value, middle, frames)
         attend_sum.share()
+        (blocks,) = fence([two, conv], blocks)
 
         def fold_conv(up, down):
-            up, down = fence([conv], up, down)
             conv.second_send()
             up, down = fence([conv], up, down)
             conv.second_swap()
@@ -1152,40 +1480,48 @@
 
         def send_two(up, down):
             attend_sum.first_swap()
-            up, down = fence([two], up, down)
             two.z_send(1)
             return fence([two], up, down)
 
-        between = (fold_conv, send_attend, send_two)
-    grad_normed = scatter_line(blocks, between)
-    if steps:
+        parts = scatter_line(blocks, (fold_conv, send_attend, send_two))
         two.z_swap(1)
-    grad_rows, grad_gain_attend = attention_input_grad(
-        grad_rows, grad_normed, grad_query, g_attend, joint_all, attend_stored
-    )
-    branch_one = (0.5 * grad_rows).astype(bf16)
-    if steps:
+        grad_rows, grad_gain_attend, branch_one = step_call(
+            attend_input_kernel,
+            "attend_input_back",
+            [],
+            [*parts, grad_query, rows_first, gain(g_attend), grad_rows, Block(middle, 0)],
+            input_outs(rows_first),
+        )
         down_sum = ModuleScatter(ffn_jobs(branch_one, None, first_stored)[1:], "down_terms")
         down_sum.share()
         down_sum.first_send()
-        branch_one, grad_rows = fence([down_sum], branch_one, grad_rows)
+        branch_one, grad_rows = fence([two, conv, attend_sum, down_sum], branch_one, grad_rows)
         down_sum.first_swap()
-    hidden_one = ffn_hidden_grad(branch_one, down_one, first_stored, "first")
-    jobs_one = ffn_jobs(branch_one, hidden_one, first_stored)
-    if steps:
-        hidden_one, grad_rows = fence([two, attend_sum], hidden_one, grad_rows)
         two.z_send(2)
         two.z_swap(2)
+        conv.z_send(1)
+        conv.z_swap(1)
+        hidden_one = ffn_hidden_grad(branch_one, down_one, first_stored, "first")
+        up_sum = ModuleScatter(ffn_jobs(branch_one, hidden_one, first_stored)[:1], "up_terms")
+        up_sum.share()
         attend_sum.second_send()
-        up_sum = ModuleScatter([(jobs_one[0][0], 0, frames, one(hidden_one)) + jobs_one[0][4:]], "up_terms")
-        up_sum.share()
         up_sum.first_send()
-        hidden_one, grad_rows = fence([attend_sum, up_sum], hidden_one, grad_rows)
+        hidden_one, grad_rows = fence(
+            [two, conv, down_sum, attend_sum, up_sum], hidden_one, grad_rows
+        )
         attend_sum.second_swap()
         up_sum.first_swap()
-    grad_rows, grad_gain_one = ffn_input_grad(
-        grad_rows, hidden_one, g_first, up_one, first_stored, "first"
-    )
+        conv.z_send(2)
+        conv.z_swap(2)
+        down_sum.second_send()
+        grad_rows, grad_gain_one, _ = ffn_up_back_input(
+            hidden_one, start_rows, gain(g_first), grad_rows, up_one, 1.0, "first_up_back"
+        )
+        grad_final, grad_gain_two, grad_gain_conv, grad_gain_attend, grad_gain_one = (
+            g[0]
+            for g in (grad_final, grad_gain_two, grad_gain_conv, grad_gain_attend, grad_gain_one)
+        )
+    total_shift, total_scale = totals
     input_grad = grad_rows * (1.0 - masked_float)
     mask_grad = jnp.sum(grad_rows * masked_float, axis=0)
 
@@ -1208,37 +1544,29 @@
     sums = jnp.transpose(sums.reshape(-1, shards, own_rows), (1, 0, 2))
     if steps:
         few = SmallScatter(sums)
-        fence([two, conv, down_sum, few])
-        conv.z_send(1)
-        conv.z_swap(1)
-        down_sum.second_send()
+        fence([conv, attend_sum, up_sum, down_sum, few])
         down_sum.second_swap()
-        few.step()
-        fence([attend_sum, conv, few])
-        conv.z_send(2)
-        conv.z_swap(2)
         attend_sum.z_send(1)
         attend_sum.z_swap(1)
         few.step()
-        fence([up_sum, attend_sum, conv, few])
         up_sum.second_send()
         up_sum.second_swap()
+        fence([down_sum, attend_sum, up_sum, few])
+        down_sum.z_send(1)
+        down_sum.z_swap(1)
+        up_sum.z_send(1)
+        up_sum.z_swap(1)
         attend_sum.z_send(2)
         attend_sum.z_swap(2)
         few.step()
-        fence([down_sum, attend_sum, few])
-        down_sum.z_send(1)
-        down_sum.z_swap(1)
-        few.step()
-        fence([down_sum, up_sum, few])
+        fence([down_sum, up_sum, attend_sum, few])
         down_sum.z_send(2)
         down_sum.z_swap(2)
-        up_sum.z_send(1)
-        up_sum.z_swap(1)
-        few.step()
-        fence([down_sum, up_sum, few])
         up_sum.z_send(2)
         up_sum.z_swap(2)
+        few.step()
+        few.step()
+        few.step()
         few.step()
         sums = few.keep[0]
         grad_up_two, grad_down_two = two.finish()

time: 884 us -> 855 us (0.967)
  waiting for transfers between devices: 421 us -> 352 us
  Pallas kernels: 208 us -> 266 us
  other arithmetic: 54.8 us -> 37.2 us
  local copies, waits for them, and re-layouts: 47.1 us -> 56.6 us
    ppermute x69, waiting for transfers between devices: 172 us -> 104 us  [swap(): lax.ppermute(values, axis, [(i, i ^ bit) for i in range(lax.axis_size(axi...]
    pallas_call x0 -> x13, Pallas kernels: none -> 53.4 us  [the longest x12 44.7 us: step_call(): pl.pallas_call(kernel, grid_spec=pltpu.PrefetchScalarGridSpec(num_scalar_...]
    all_gather x3, waiting for transfers between devices: 160 us -> 147 us  [gather_packed(): return lax.all_gather(part, ('dp', 'seq'), axis=0)]
    dot_general x7 -> x0, matrix products: 12.2 us -> none  [product_tail(): lax.dot_general(left_side, right_side, (((1,), (1,)), ((), ())), preferre...]
    reduce_sum x5 -> x0, other arithmetic: 10.7 us -> none  [the longest x2 6.37 us: conv_paired_grad(): jnp.sum(widened_float[offset:offset + frames] * grad_float, axis=0)]
    convert_element_type x7 -> x0, other arithmetic: 9.29 us -> none  [the longest x1 5.35 us: conv_paired_grad(): grad_right.astype(bf16)]
  transfers between devices with their start and end apart: 88 -> 88, of which waited for: 47 -> 46; matrix products, arithmetic and copies ran while one was open for 11% -> 11% of each run, Pallas kernels for 16% -> 24%
where the time goes in v3:
time: 855 us; the launch traced here: 847 us
  waiting for transfers between devices  352 us (41%)
  Pallas kernels  266 us (31%)
  starting transfers between devices  103 us (12%)
  local copies, waits for them, and re-layouts  56.6 us (7%)
  other arithmetic  37.2 us (4%)
  between operations  17.9 us (2%)
  matrix products  15.5 us (2%)
    all_gather x3, waiting for transfers between devices, gather_packed(): return lax.all_gather(part, ('dp', 'seq'), axis=0)  147 us
    ppermute x69, waiting for transfers between devices, swap(): lax.ppermute(values, axis, [(i, i ^ bit) for i in range(lax.axis_size(axi...  104 us
    pallas_call x10, Pallas kernels, call(): pl.pallas_call(functools.partial(kernel, self.shape, 4), grid_spec=pltpu....  69.3 us
    ppermute x3, waiting for transfers between devices, gather_line(): lax.ppermute(downs[-1], 'seq', [(i + 1, i) for i in range(seq - 1)])  64.2 us
    ppermute x69, starting transfers between devices, swap(): lax.ppermute(values, axis, [(i, i ^ bit) for i in range(lax.axis_size(axi...  63 us
    pallas_call x8, Pallas kernels, ffn_call(): pl.pallas_call(kernel, grid=(steps,), in_specs=[spec(x) for x in inputs]...  62.5 us
    pallas_call x12, Pallas kernels, step_call(): pl.pallas_call(kernel, grid_spec=pltpu.PrefetchScalarGridSpec(num_scalar_...  44.7 us
    pallas_call x18, Pallas kernels, whole_call(): pl.pallas_call(kernel, grid_spec=pltpu.PrefetchScalarGridSpec(num_scalar_...  40.4 us
  transfers between devices with their start and end apart: 88, of which 46 were waited for; matrix products, arithmetic and copies ran while one was open for 11% of the time, Pallas kernels for 24%

profile of v3, /device:TPU:0, one launch (start us, length us, event | category | flops | bytes accessed | tf_op | source)
XLA Modules:
  0.0 847.3 jit_solution(12818272456246416393)
XLA Ops:
  37.0 92.2 %all-gather.7.cloned.1.call-done = bf16[8192,1024]{1,0:T(8,128)(2,1)} async-done(((bf16[256,1024]{1,0:T(8,128)(2,1)}), bf16[8192,1024]{1,0:T(8,128)(2,1)}) %all-gather.7.cloned.1.call-update) | async-done | bytes 16777232 | tf_op jit(solution)/shard_map/all_gather | solution.py:513
  134.3 8.1 first_up.1
  142.3 7.4 first_down.1.values_ref
  158.9 26.5 %collective-permute-done.5 = bf16[256,1024]{1,0:T(8,128)(2,1)S(1)} collective-permute-done((bf16[256,1024]{1,0:T(8,128)(2,1)S(1)}, bf16[256,1024]{1,0:T(8,128)(2,1)S(1)}, u32[]{:S(2)}, u32[]{:S(2)}) %collective-permute-start.5) | collective-permute-done | bytes 524320 | tf_op jit(solution)/shard_map/ppermute | solution.py:614
  192.0 7.9 collective-permute-done.9
  207.3 29.8 %collective-permute-done.10 = bf16[256,1024]{1,0:T(8,128)(2,1)S(1)} collective-permute-done((bf16[256,1024]{1,0:T(8,128)(2,1)}, bf16[256,1024]{1,0:T(8,128)(2,1)S(1)}, u32[]{:S(2)}, u32[]{:S(2)}) %collective-permute-start.10) | collective-permute-done | bytes 524320 | tf_op jit(solution)/shard_map/ppermute | solution.py:614
  238.9 17.9 %all-gather.9.cloned.1.call-done = bf16[7168,1024]{1,0:T(8,128)(2,1)} async-done(((bf16[224,1024]{1,0:T(8,128)(2,1)}), bf16[7168,1024]{1,0:T(8,128)(2,1)}) %all-gather.9.cloned.1.call-update) | async-done | bytes 14680080 | tf_op jit(solution)/shard_map/all_gather | solution.py:513
  260.5 7.9 fusion.44
  278.1 16.9 %attend.1 = (bf16[256,1024]{1,0:T(8,128)(2,1)S(1)}, f32[8,2,256]{2,1,0:T(2,128)S(1)}) custom-call(s32[5]{0:T(128)S(1)} %pad_add_fusion.2.offsets_ref, bf16[256,1024]{1,0:T(8,128)(2,1)S(1)} %convolution_convert_fusion.2.query_ref, bf16[1024,1024]{1,0:T(8,128)(2,1)S(1)} %convolution_convert_fusion.1.key_ref, ...), custom_call_target="tpu_custom_call" | custom-call | tf_op jit(solution)/shard_map/attend/pallas_call | solution.py:1020
  338.5 36.6 %all-gather.11.cloned.1.call-done = bf16[8192,1024]{1,0:T(8,128)(2,1)} async-done(((bf16[256,1024]{1,0:T(8,128)(2,1)}), bf16[8192,1024]{1,0:T(8,128)(2,1)}) %all-gather.11.cloned.1.call-update) | async-done | bytes 16777232 | tf_op jit(solution)/shard_map/all_gather | solution.py:513
  375.1 7.9 second_up.1
  406.9 8.5 %second_up_back.1 = (f32[256,1024]{1,0:T(8,128)}, f32[1,1024]{1,0:T(1,128)}, bf16[256,1024]{1,0:T(8,128)(2,1)}) custom-call(bf16[256,4096]{1,0:T(8,128)(2,1)} %second_down_back.1.refs_4_.grad_ref, f32[256,1024]{1,0:T(8,128)} %copy-done.12, f32[1,1024]{1,0:T(1,128)} %slice.559.gain_ref, f32[256,1024]{1,0:T(8,128)} %get-tuple-element.212.rows_ref, ...), custom_call_target="tpu_custom_call" | custom-call | flops 1024 | bytes 1024 | tf_op jit(solution)/shard_map/second_up_back/pallas_call | solution.py:569
  415.5 7.6 second_terms_send.1
  471.0 9.2 %taps_back.1 = (bf16[256,1024]{1,0:T(8,128)(2,1)}, bf16[256,1024]{1,0:T(8,128)(2,1)}) custom-call(s32[1]{0:T(128)} %bitcast.79.count_ref, bf16[15,1024]{1,0:T(8,128)(2,1)} %copy-done.75, bf16[256,1024]{1,0:T(8,128)(2,1)} %get-tuple-element.224.grad_ref, bf16[15,1024]{1,0:T(8,128)(2,1)} %copy-done.76, f32[31,1024]{1,0:T(8,128)} %copy-done.39, ...), custom_call_target="tpu_custom_call" | custom-call | flops 1024 | bytes 1024 | tf_op jit(solution)/shard_map/taps_back/pallas_call | solution.py:751
  495.6 8.7 %second_terms_fold.1 = (bf16[4,256,512]{2,1,0:T(8,128)(2,1)}, bf16[4,256,512]{2,1,0:T(8,128)(2,1)}, bf16[2,4,256,512]{3,2,1,0:T(8,128)(2,1)}) custom-call(s32[2,4]{1,0:T(2,128)} %pad_add_fusion.table_ref, bf16[256,1024]{1,0:T(8,128)(2,1)} %multiply_convert_fusion.1.normed_ref.refs_0_.refs_1_, ...), custom_call_target="tpu_custom_call" | custom-call | flops 1024 | bytes 1024 | tf_op jit(solution)/shard_map/second_terms_fold/pallas_call | solution.py:383
  508.5 23.4 %attend_back.1 = (bf16[256,1024]{1,0:T(8,128)(2,1)S(1)}, bf16[1024,1024]{1,0:T(8,128)(2,1)S(1)}, bf16[1024,1024]{1,0:T(8,128)(2,1)S(1)}) custom-call(s32[5]{0:T(128)S(1)} %pad_add_fusion.2.offsets_ref, bf16[256,1024]{1,0:T(8,128)(2,1)S(1)} %copy-done.8, bf16[1024,1024]{1,0:T(8,128)(2,1)} %copy-done.4, bf16[1024,1024]{1,0:T(8,128)(2,1)} %copy-done.3, ...), custom_call_target="tpu_custom_call" | custom-call | tf_op jit(solution)/shard_map/attend_back/pallas_call | solution.py:1058
  531.9 16.5 %collective-permute-done.38.refs_14_.refs_15_ = bf16[2,4,96,512]{3,2,1,0:T(8,128)(2,1)S(1)} collective-permute-done((bf16[2,4,96,512]{3,2,1,0:T(8,128)(2,1)}, bf16[2,4,96,512]{3,2,1,0:T(8,128)(2,1)S(1)}, u32[]{:S(2)}, u32[]{:S(2)}) %collective-permute-start.38) | collective-permute-done | bytes 786464 | tf_op jit(solution)/shard_map/ppermute | solution.py:43
  550.2 8.7 %attend_blocks_back.1 = bf16[4,256,1024]{2,1,0:T(8,128)(2,1)} custom-call(bf16[1024,1024]{1,0:T(8,128)(2,1)} %copy-done, bf16[1024,1024]{1,0:T(8,128)(2,1)} %copy-done.1, bf16[32,224,1024]{2,1,0:T(8,128)(2,1)} %bitcast.176, bf16[32,224,1024]{2,1,0:T(8,128)(2,1)} %bitcast.177), custom_call_target="tpu_custom_call" | custom-call | flops 1024 | bytes 1024 | tf_op jit(solution)/shard_map/attend_blocks_back/pallas_call | solution.py:902
  566.9 10.5 %collective-permute-done.46 = bf16[256,1024]{1,0:T(8,128)(2,1)S(1)} collective-permute-done((bf16[256,1024]{1,0:T(8,128)(2,1)S(1)}, bf16[256,1024]{1,0:T(8,128)(2,1)S(1)}, u32[]{:S(2)}, u32[]{:S(2)}) %collective-permute-start.46) | collective-permute-done | bytes 524320 | tf_op jit(solution)/shard_map/ppermute | solution.py:631
  596.2 9.8 %attend_terms_send.1 = (bf16[2,4,128,512]{3,2,1,0:T(8,128)(2,1)}, bf16[2,4,128,512]{3,2,1,0:T(8,128)(2,1)}) custom-call(s32[2,2]{1,0:T(2,128)} %pad_add_fusion.1.table_ref, bf16[1024,1024]{1,0:T(8,128)(2,1)} %bitcast.20.refs_0_.refs_1_.refs_6_.refs_7_, bf16[1024,1024]{1,0:T(8,128)(2,1)} %bitcast.20.refs_0_.refs_1_.refs_6_.refs_7_, ...), custom_call_target="tpu_custom_call" | custom-call | flops 1024 | bytes 1024 | tf_op jit(solution)/shard_map/attend_terms_send/pallas_call | solution.py:383
  643.6 9.1 %collective-permute-done.53.refs_0_ = bf16[4,96,512]{2,1,0:T(8,128)(2,1)S(1)} collective-permute-done((bf16[4,96,512]{2,1,0:T(8,128)(2,1)S(1)}, bf16[4,96,512]{2,1,0:T(8,128)(2,1)S(1)}, u32[]{:S(2)}, u32[]{:S(2)}) %collective-permute-start.53) | collective-permute-done | bytes 393248 | tf_op jit(solution)/shard_map/ppermute | solution.py:43
  674.3 10.2 %attend_terms_fold.1 = (bf16[4,128,512]{2,1,0:T(8,128)(2,1)}, bf16[4,128,512]{2,1,0:T(8,128)(2,1)}, bf16[2,4,128,512]{3,2,1,0:T(8,128)(2,1)}) custom-call(s32[2,4]{1,0:T(2,128)} %pad_add_fusion.table_ref, bf16[1024,1024]{1,0:T(8,128)(2,1)} %bitcast.20.refs_0_.refs_1_.refs_6_.refs_7_, bf16[1024,1024]{1,0:T(8,128)(2,1)} %bitcast.20.refs_0_.refs_1_.refs_6_.refs_7_, ...), custom_call_target="tpu_custom_call" | custom-call | flops 1024 | bytes 1024 | tf_op jit(solution)/shard_map/attend_terms_fold/pallas_call | solution.py:383
  717.5 8.5 %first_up_back.1 = (f32[256,1024]{1,0:T(8,128)}, f32[1,1024]{1,0:T(1,128)}, bf16[256,1024]{1,0:T(8,128)(2,1)}) custom-call(bf16[256,4096]{1,0:T(8,128)(2,1)} %first_down_back.1.refs_4_.grad_ref, f32[256,1024]{1,0:T(8,128)} %get-tuple-element.430.values_ref, f32[1,1024]{1,0:T(1,128)} %slice.568.gain_ref, f32[256,1024]{1,0:T(8,128)} %get-tuple-element.305.rows_ref, ...), custom_call_target="tpu_custom_call" | custom-call | flops 1024 | bytes 1024 | tf_op jit(solution)/shard_map/first_up_back/pallas_call | solution.py:569
  789.3 11.3 %collective-permute-done.78.got_ref = bf16[2,1,128,512]{3,2,1,0:T(8,128)(2,1)S(1)} collective-permute-done((bf16[2,1,128,512]{3,2,1,0:T(8,128)(2,1)}, bf16[2,1,128,512]{3,2,1,0:T(8,128)(2,1)S(1)}, u32[]{:S(2)}, u32[]{:S(2)}) %collective-permute-start.78) | collective-permute-done | bytes 262176 | tf_op jit(solution)/shard_map/ppermute | solution.py:43
  (564 shorter events, 428.3 us)
Async XLA Ops:
  7.2 122.1 %all-gather.7.cloned.1.call-start = ((), (), s32[]{:S(2)}) async-start(), calls=%async_computation | async-start | bytes 17301504 | tf_op jit(solution)/shard_map/all_gather | solution.py:513
  9.1 247.7 %all-gather.9.cloned.1.call-start = ((), (), s32[]{:S(2)}) async-start(), calls=%async_computation.1 | async-start | bytes 15138816 | tf_op jit(solution)/shard_map/all_gather | solution.py:513
  129.3 245.8 %all-gather.11.cloned.1.call-start = ((), (), s32[]{:S(2)}) async-start(), calls=%async_computation.2 | async-start | bytes 17301504 | tf_op jit(solution)/shard_map/all_gather | solution.py:513
  153.0 32.4 %collective-permute-start.5 = (bf16[256,1024]{1,0:T(8,128)(2,1)S(1)}, bf16[256,1024]{1,0:T(8,128)(2,1)S(1)}, u32[]{:S(2)}, u32[]{:S(2)}) collective-permute-start(bf16[256,1024]{1,0:T(8,128)(2,1)S(1)} %multiply_convert_fusion.5), channel_id=1, source_target_pairs={{1,0},{2,1},{3,2},{5,4},{6,5},{7,6},{9,8},{10,9},{11,10},{13,12},{... | collective-permute-start | bytes 1572872 | tf_op jit(solution)/shard_map/ppermute | solution.py:614
  154.3 32.4 %collective-permute-start.6 = (bf16[256,1024]{1,0:T(8,128)(2,1)S(1)}, bf16[256,1024]{1,0:T(8,128)(2,1)S(1)}, u32[]{:S(2)}, u32[]{:S(2)}) collective-permute-start(bf16[256,1024]{1,0:T(8,128)(2,1)S(1)} %multiply_convert_fusion.5), channel_id=1, source_target_pairs={{0,1},{1,2},{2,3},{4,5},{5,6},{6,7},{8,9},{9,10},{10,11},{12,13},{... | collective-permute-start | bytes 1572872 | tf_op jit(solution)/shard_map/ppermute | solution.py:613
  199.9 37.3 %collective-permute-start.10 = (bf16[256,1024]{1,0:T(8,128)(2,1)}, bf16[256,1024]{1,0:T(8,128)(2,1)S(1)}, u32[]{:S(2)}, u32[]{:S(2)}) collective-permute-start(bf16[256,1024]{1,0:T(8,128)(2,1)} %collective-permute-done.9), channel_id=1, source_target_pairs={{1,0},{2,1},{3,2},{5,4},{6,5},{7,6},{9,8},{10,9},{11,10},{13,12},{... | collective-permute-start | bytes 1572872 | tf_op jit(solution)/shard_map/ppermute | solution.py:614
  201.4 35.8 %collective-permute-start.8 = (bf16[256,1024]{1,0:T(8,128)(2,1)}, bf16[256,1024]{1,0:T(8,128)(2,1)S(1)}, u32[]{:S(2)}, u32[]{:S(2)}) collective-permute-start(bf16[256,1024]{1,0:T(8,128)(2,1)} %collective-permute-done.7), channel_id=1, source_target_pairs={{0,1},{1,2},{2,3},{4,5},{5,6},{6,7},{8,9},{9,10},{10,11},{12,13},{... | collective-permute-start | bytes 1572872 | tf_op jit(solution)/shard_map/ppermute | solution.py:613
  442.3 52.0 %collective-permute-start.25 = (bf16[2,4,256,512]{3,2,1,0:T(8,128)(2,1)}, bf16[2,4,256,512]{3,2,1,0:T(8,128)(2,1)S(1)}, u32[]{:S(2)}, u32[]{:S(2)}) collective-permute-start(bf16[2,4,256,512]{3,2,1,0:T(8,128)(2,1)} %get-tuple-element.219), channel_id=1, source_target_pairs={{0,8},{4,12},{8,0},{12,4},{16,24},{20,28},{24,16},{28,20},{1,9},{5... | collective-permute-start | bytes 6291464 | tf_op jit(solution)/shard_map/ppermute | solution.py:43
  443.5 50.8 %collective-permute-start.26 = (bf16[2,4,256,512]{3,2,1,0:T(8,128)(2,1)}, bf16[2,4,256,512]{3,2,1,0:T(8,128)(2,1)}, u32[]{:S(2)}, u32[]{:S(2)}) collective-permute-start(bf16[2,4,256,512]{3,2,1,0:T(8,128)(2,1)} %get-tuple-element.220), channel_id=1, source_target_pairs={{0,16},{4,20},{8,24},{12,28},{16,0},{20,4},{24,8},{28,12},{1,17},{... | collective-permute-start | bytes 6291464 | tf_op jit(solution)/shard_map/ppermute | solution.py:43
  444.3 35.9 %collective-permute-start.27 = (bf16[256,1024]{1,0:T(8,128)(2,1)S(1)}, bf16[256,1024]{1,0:T(8,128)(2,1)S(1)}, u32[]{:S(2)}, u32[]{:S(2)}) collective-permute-start(bf16[256,1024]{1,0:T(8,128)(2,1)S(1)} %copy-done.16), channel_id=1, source_target_pairs={{0,4},{4,0},{8,12},{12,8},{16,20},{20,16},{24,28},{28,24},{1,5},{5... | collective-permute-start | bytes 1572872 | tf_op jit(solution)/shard_map/ppermute | solution.py:43
  444.3 36.0 %collective-permute-start.34 = (bf16[256,1024]{1,0:T(8,128)(2,1)S(1)}, bf16[256,1024]{1,0:T(8,128)(2,1)S(1)}, u32[]{:S(2)}, u32[]{:S(2)}) collective-permute-start(bf16[256,1024]{1,0:T(8,128)(2,1)S(1)} %copy-done.18), channel_id=1, source_target_pairs={{0,4},{4,0},{8,12},{12,8},{16,20},{20,16},{24,28},{28,24},{1,5},{5... | collective-permute-start | bytes 1572872 | tf_op jit(solution)/shard_map/ppermute | solution.py:43
  504.3 44.6 %collective-permute-start.36 = (bf16[4,256,512]{2,1,0:T(8,128)(2,1)}, bf16[4,256,512]{2,1,0:T(8,128)(2,1)S(1)}, u32[]{:S(2)}, u32[]{:S(2)}) collective-permute-start(bf16[4,256,512]{2,1,0:T(8,128)(2,1)} %get-tuple-element.242), channel_id=1, source_target_pairs={{0,16},{4,20},{8,24},{12,28},{16,0},{20,4},{24,8},{28,12},{1,17},{... | collective-permute-start | bytes 3145736 | tf_op jit(solution)/shard_map/ppermute | solution.py:43
  505.7 82.2 %collective-permute-start.40 = (bf16[1024,1024]{1,0:T(8,128)(2,1)}, bf16[1024,1024]{1,0:T(8,128)(2,1)}, u32[]{:S(2)}, u32[]{:S(2)}) collective-permute-start(bf16[1024,1024]{1,0:T(8,128)(2,1)} %bitcast.20.refs_0_.refs_1_.refs_6_.refs_7_), channel_id=1, source_target_pairs={{0,4},{4,0},{8,12},{12,8},{16,20},{20,16},{24,28},{28,24},{1,5},{5... | collective-permute-start | bytes 6291464 | tf_op jit(solution)/shard_map/ppermute | solution.py:43
  505.7 53.2 %collective-permute-start.37 = (bf16[4,256,512]{2,1,0:T(8,128)(2,1)}, bf16[4,256,512]{2,1,0:T(8,128)(2,1)S(1)}, u32[]{:S(2)}, u32[]{:S(2)}) collective-permute-start(bf16[4,256,512]{2,1,0:T(8,128)(2,1)} %get-tuple-element.243), channel_id=1, source_target_pairs={{0,8},{4,12},{8,0},{12,4},{16,24},{20,28},{24,16},{28,20},{1,9},{5... | collective-permute-start | bytes 3145736 | tf_op jit(solution)/shard_map/ppermute | solution.py:43
  506.5 41.8 %collective-permute-start.38 = (bf16[2,4,96,512]{3,2,1,0:T(8,128)(2,1)}, bf16[2,4,96,512]{3,2,1,0:T(8,128)(2,1)S(1)}, u32[]{:S(2)}, u32[]{:S(2)}) collective-permute-start(bf16[2,4,96,512]{3,2,1,0:T(8,128)(2,1)} %get-tuple-element.245), channel_id=1, source_target_pairs={{0,8},{4,12},{8,0},{12,4},{16,24},{20,28},{24,16},{28,20},{1,9},{5... | collective-permute-start | bytes 2359304 | tf_op jit(solution)/shard_map/ppermute | solution.py:43
  507.8 40.6 %collective-permute-start.39 = (bf16[2,4,96,512]{3,2,1,0:T(8,128)(2,1)}, bf16[2,4,96,512]{3,2,1,0:T(8,128)(2,1)S(1)}, u32[]{:S(2)}, u32[]{:S(2)}) collective-permute-start(bf16[2,4,96,512]{3,2,1,0:T(8,128)(2,1)} %get-tuple-element.246), channel_id=1, source_target_pairs={{0,16},{4,20},{8,24},{12,28},{16,0},{20,4},{24,8},{28,12},{1,17},{... | collective-permute-start | bytes 2359304 | tf_op jit(solution)/shard_map/ppermute | solution.py:43
  548.4 47.7 %collective-permute-start.42 = (bf16[1024,1024]{1,0:T(8,128)(2,1)S(1)}, bf16[1024,1024]{1,0:T(8,128)(2,1)}, u32[]{:S(2)}, u32[]{:S(2)}) collective-permute-start(bf16[1024,1024]{1,0:T(8,128)(2,1)S(1)} %get-tuple-element.249.key_ref.refs_10_), channel_id=1, source_target_pairs={{0,4},{4,0},{8,12},{12,8},{16,20},{20,16},{24,28},{28,24},{1,5},{5... | collective-permute-start | bytes 6291464 | tf_op jit(solution)/shard_map/ppermute | solution.py:43
  550.2 45.9 %collective-permute-start.43 = (bf16[1024,1024]{1,0:T(8,128)(2,1)S(1)}, bf16[1024,1024]{1,0:T(8,128)(2,1)}, u32[]{:S(2)}, u32[]{:S(2)}) collective-permute-start(bf16[1024,1024]{1,0:T(8,128)(2,1)S(1)} %get-tuple-element.250.value_ref.refs_12_), channel_id=1, source_target_pairs={{0,4},{4,0},{8,12},{12,8},{16,20},{20,16},{24,28},{28,24},{1,5},{5... | collective-permute-start | bytes 6291464 | tf_op jit(solution)/shard_map/ppermute | solution.py:43
  588.0 47.7 %collective-permute-start.57 = (bf16[256,4096]{1,0:T(8,128)(2,1)}, bf16[256,4096]{1,0:T(8,128)(2,1)}, u32[]{:S(2)}, u32[]{:S(2)}) collective-permute-start(bf16[256,4096]{1,0:T(8,128)(2,1)} %get-tuple-element.201.active_ref.refs_0_.refs_1_), channel_id=1, source_target_pairs={{0,4},{4,0},{8,12},{12,8},{16,20},{20,16},{24,28},{28,24},{1,5},{5... | collective-permute-start | bytes 6291464 | tf_op jit(solution)/shard_map/ppermute | solution.py:43
  619.9 32.8 %collective-permute-start.55 = (bf16[2,4,128,512]{3,2,1,0:T(8,128)(2,1)}, bf16[2,4,128,512]{3,2,1,0:T(8,128)(2,1)S(1)}, u32[]{:S(2)}, u32[]{:S(2)}) collective-permute-start(bf16[2,4,128,512]{3,2,1,0:T(8,128)(2,1)} %get-tuple-element.274), channel_id=1, source_target_pairs={{0,8},{4,12},{8,0},{12,4},{16,24},{20,28},{24,16},{28,20},{1,9},{5... | collective-permute-start | bytes 3145736 | tf_op jit(solution)/shard_map/ppermute | solution.py:43
  620.7 32.0 %collective-permute-start.56 = (bf16[2,4,128,512]{3,2,1,0:T(8,128)(2,1)}, bf16[2,4,128,512]{3,2,1,0:T(8,128)(2,1)S(1)}, u32[]{:S(2)}, u32[]{:S(2)}) collective-permute-start(bf16[2,4,128,512]{3,2,1,0:T(8,128)(2,1)} %get-tuple-element.275), channel_id=1, source_target_pairs={{0,16},{4,20},{8,24},{12,28},{16,0},{20,4},{24,8},{28,12},{1,17},{... | collective-permute-start | bytes 3145736 | tf_op jit(solution)/shard_map/ppermute | solution.py:43
  661.2 31.4 %collective-permute-start.61 = (bf16[2,4,128,512]{3,2,1,0:T(8,128)(2,1)}, bf16[2,4,128,512]{3,2,1,0:T(8,128)(2,1)}, u32[]{:S(2)}, u32[]{:S(2)}) collective-permute-start(bf16[2,4,128,512]{3,2,1,0:T(8,128)(2,1)} %get-tuple-element.292), channel_id=1, source_target_pairs={{0,8},{4,12},{8,0},{12,4},{16,24},{20,28},{24,16},{28,20},{1,9},{5... | collective-permute-start | bytes 3145736 | tf_op jit(solution)/shard_map/ppermute | solution.py:43
  693.4 41.7 %collective-permute-start.68 = (bf16[2,4,128,512]{3,2,1,0:T(8,128)(2,1)}, bf16[2,4,128,512]{3,2,1,0:T(8,128)(2,1)S(1)}, u32[]{:S(2)}, u32[]{:S(2)}) collective-permute-start(bf16[2,4,128,512]{3,2,1,0:T(8,128)(2,1)} %get-tuple-element.314), channel_id=1, source_target_pairs={{0,8},{4,12},{8,0},{12,4},{16,24},{20,28},{24,16},{28,20},{1,9},{5... | collective-permute-start | bytes 3145736 | tf_op jit(solution)/shard_map/ppermute | solution.py:43
  694.9 40.2 %collective-permute-start.69 = (bf16[2,4,128,512]{3,2,1,0:T(8,128)(2,1)}, bf16[2,4,128,512]{3,2,1,0:T(8,128)(2,1)S(1)}, u32[]{:S(2)}, u32[]{:S(2)}) collective-permute-start(bf16[2,4,128,512]{3,2,1,0:T(8,128)(2,1)} %get-tuple-element.315), channel_id=1, source_target_pairs={{0,16},{4,20},{8,24},{12,28},{16,0},{20,4},{24,8},{28,12},{1,17},{... | collective-permute-start | bytes 3145736 | tf_op jit(solution)/shard_map/ppermute | solution.py:43
  (163 other events, 2122.3 us)
Sparse Core Ops, SparseCore 0:
  11.6 117.6 all-gather.6
  132.7 124.1 all-gather.8
  260.4 114.6 all-gather.10

commit v4 on v3

--- a/solution.py
+++ b/solution.py
@@ -1466,24 +1466,22 @@
         )
         blocks = blocks_back(grad_key, grad_value, middle, frames)
         attend_sum.share()
-        (blocks,) = fence([two, conv], blocks)
-
-        def fold_conv(up, down):
-            conv.second_send()
-            up, down = fence([conv], up, down)
-            conv.second_swap()
-            return up, down
 
         def send_attend(up, down):
             attend_sum.first_send()
-            return fence([attend_sum], up, down)
+            return fence([attend_sum, conv], up, down)
+
+        def fold_conv(up, down):
+            attend_sum.first_swap()
+            conv.second_send()
+            return fence([conv], up, down)
 
         def send_two(up, down):
-            attend_sum.first_swap()
+            conv.second_swap()
             two.z_send(1)
             return fence([two], up, down)
 
-        parts = scatter_line(blocks, (fold_conv, send_attend, send_two))
+        parts = scatter_line(blocks, (send_attend, fold_conv, send_two))
         two.z_swap(1)
         grad_rows, grad_gain_attend, branch_one = step_call(
             attend_input_kernel,
@@ -1495,13 +1493,14 @@
         down_sum = ModuleScatter(ffn_jobs(branch_one, None, first_stored)[1:], "down_terms")
         down_sum.share()
         down_sum.first_send()
-        branch_one, grad_rows = fence([two, conv, attend_sum, down_sum], branch_one, grad_rows)
+        branch_one, grad_rows = fence([attend_sum, down_sum], branch_one, grad_rows)
         down_sum.first_swap()
+        hidden_one = ffn_hidden_grad(branch_one, down_one, first_stored, "first")
+        hidden_one, grad_rows = fence([two, conv], hidden_one, grad_rows)
         two.z_send(2)
         two.z_swap(2)
         conv.z_send(1)
         conv.z_swap(1)
-        hidden_one = ffn_hidden_grad(branch_one, down_one, first_stored, "first")
         up_sum = ModuleScatter(ffn_jobs(branch_one, hidden_one, first_stored)[:1], "up_terms")
         up_sum.share()
         attend_sum.second_send()
@@ -1514,6 +1513,7 @@
         conv.z_send(2)
         conv.z_swap(2)
         down_sum.second_send()
+        two_grads = two.finish()
         grad_rows, grad_gain_one, _ = ffn_up_back_input(
             hidden_one, start_rows, gain(g_first), grad_rows, up_one, 1.0, "first_up_back"
         )
@@ -1544,14 +1544,15 @@
     sums = jnp.transpose(sums.reshape(-1, shards, own_rows), (1, 0, 2))
     if steps:
         few = SmallScatter(sums)
-        fence([conv, attend_sum, up_sum, down_sum, few])
+        (two_grads,) = fence([conv, attend_sum, up_sum, down_sum, few], two_grads)
         down_sum.second_swap()
         attend_sum.z_send(1)
         attend_sum.z_swap(1)
         few.step()
         up_sum.second_send()
         up_sum.second_swap()
-        fence([down_sum, attend_sum, up_sum, few])
+        conv_grads = conv.finish()
+        (conv_grads,) = fence([down_sum, attend_sum, up_sum, few], conv_grads)
         down_sum.z_send(1)
         down_sum.z_swap(1)
         up_sum.z_send(1)
@@ -1569,8 +1570,8 @@
         few.step()
         few.step()
         sums = few.keep[0]
-        grad_up_two, grad_down_two = two.finish()
-        grad_pair, grad_conv_out = conv.finish()
+        grad_up_two, grad_down_two = two_grads
+        grad_pair, grad_conv_out = conv_grads
         attend_grads = attend_sum.finish()
         (grad_up_one,) = up_sum.finish()
         (grad_down_one,) = down_sum.finish()

time: 855 us -> 824 us (0.964)
  waiting for transfers between devices: 352 us -> 321 us
    ppermute x69, waiting for transfers between devices: 104 us -> 87.7 us  [swap(): lax.ppermute(values, axis, [(i, i ^ bit) for i in range(lax.axis_size(axi...]
    ppermute x3, waiting for transfers between devices: 13.5 us -> 0.8 us  [scatter_line(): up = lax.ppermute(message_up, 'seq', [(i, i + 1) for i in range(seq - 1)])]
  transfers between devices with their start and end apart: 88 -> 88, of which waited for: 46 -> 46; matrix products, arithmetic and copies ran while one was open for 11% -> 11% of each run, Pallas kernels for 24% -> 27%
where the time goes in v4:
time: 824 us; the launch traced here: 816 us
  waiting for transfers between devices  321 us (39%)
  Pallas kernels  266 us (32%)
  starting transfers between devices  108 us (13%)
  local copies, waits for them, and re-layouts  52.6 us (6%)
  other arithmetic  35 us (4%)
  between operations  17.6 us (2%)
  matrix products  15.5 us (2%)
    all_gather x3, waiting for transfers between devices, gather_packed(): return lax.all_gather(part, ('dp', 'seq'), axis=0)  147 us
    ppermute x69, waiting for transfers between devices, swap(): lax.ppermute(values, axis, [(i, i ^ bit) for i in range(lax.axis_size(axi...  87.7 us
    pallas_call x10, Pallas kernels, call(): pl.pallas_call(functools.partial(kernel, self.shape, 4), grid_spec=pltpu....  70 us
    ppermute x69, starting transfers between devices, swap(): lax.ppermute(values, axis, [(i, i ^ bit) for i in range(lax.axis_size(axi...  66.5 us
    ppermute x3, waiting for transfers between devices, gather_line(): lax.ppermute(downs[-1], 'seq', [(i + 1, i) for i in range(seq - 1)])  64 us
    pallas_call x8, Pallas kernels, ffn_call(): pl.pallas_call(kernel, grid=(steps,), in_specs=[spec(x) for x in inputs]...  62.5 us
    pallas_call x12, Pallas kernels, step_call(): pl.pallas_call(kernel, grid_spec=pltpu.PrefetchScalarGridSpec(num_scalar_...  44.6 us
    pallas_call x18, Pallas kernels, whole_call(): pl.pallas_call(kernel, grid_spec=pltpu.PrefetchScalarGridSpec(num_scalar_...  40.5 us
  transfers between devices with their start and end apart: 88, of which 46 were waited for; matrix products, arithmetic and copies ran while one was open for 11% of the time, Pallas kernels for 27%

profile of v4, /device:TPU:0, one launch (start us, length us, event | category | flops | bytes accessed | tf_op | source)
XLA Modules:
  0.0 816.1 jit_solution(4830959094969782196)
XLA Ops:
  37.0 92.2 %all-gather.7.cloned.1.call-done = bf16[8192,1024]{1,0:T(8,128)(2,1)} async-done(((bf16[256,1024]{1,0:T(8,128)(2,1)}), bf16[8192,1024]{1,0:T(8,128)(2,1)}) %all-gather.7.cloned.1.call-update) | async-done | bytes 16777232 | tf_op jit(solution)/shard_map/all_gather | solution.py:513
  134.2 8.0 first_up.1
  142.3 7.4 first_down.1.values_ref
  158.8 26.4 %collective-permute-done.5 = bf16[256,1024]{1,0:T(8,128)(2,1)S(1)} collective-permute-done((bf16[256,1024]{1,0:T(8,128)(2,1)S(1)}, bf16[256,1024]{1,0:T(8,128)(2,1)S(1)}, u32[]{:S(2)}, u32[]{:S(2)}) %collective-permute-start.5) | collective-permute-done | bytes 524320 | tf_op jit(solution)/shard_map/ppermute | solution.py:614
  191.9 8.0 collective-permute-done.9
  207.4 29.6 %collective-permute-done.10 = bf16[256,1024]{1,0:T(8,128)(2,1)S(1)} collective-permute-done((bf16[256,1024]{1,0:T(8,128)(2,1)}, bf16[256,1024]{1,0:T(8,128)(2,1)S(1)}, u32[]{:S(2)}, u32[]{:S(2)}) %collective-permute-start.10) | collective-permute-done | bytes 524320 | tf_op jit(solution)/shard_map/ppermute | solution.py:614
  238.7 18.3 %all-gather.9.cloned.1.call-done = bf16[7168,1024]{1,0:T(8,128)(2,1)} async-done(((bf16[224,1024]{1,0:T(8,128)(2,1)}), bf16[7168,1024]{1,0:T(8,128)(2,1)}) %all-gather.9.cloned.1.call-update) | async-done | bytes 14680080 | tf_op jit(solution)/shard_map/all_gather | solution.py:513
  260.8 7.9 fusion.44
  278.3 16.9 %attend.1 = (bf16[256,1024]{1,0:T(8,128)(2,1)S(1)}, f32[8,2,256]{2,1,0:T(2,128)S(1)}) custom-call(s32[5]{0:T(128)S(1)} %pad_add_fusion.2.offsets_ref, bf16[256,1024]{1,0:T(8,128)(2,1)S(1)} %convolution_convert_fusion.2.query_ref, bf16[1024,1024]{1,0:T(8,128)(2,1)S(1)} %convolution_convert_fusion.1.key_ref, ...), custom_call_target="tpu_custom_call" | custom-call | tf_op jit(solution)/shard_map/attend/pallas_call | solution.py:1020
  338.5 36.6 %all-gather.11.cloned.1.call-done = bf16[8192,1024]{1,0:T(8,128)(2,1)} async-done(((bf16[256,1024]{1,0:T(8,128)(2,1)}), bf16[8192,1024]{1,0:T(8,128)(2,1)}) %all-gather.11.cloned.1.call-update) | async-done | bytes 16777232 | tf_op jit(solution)/shard_map/all_gather | solution.py:513
  375.2 7.9 second_up.1
  383.1 7.3 second_down.1.values_ref
  393.7 7.4 second_down_back.1.refs_4_.grad_ref
  406.9 8.5 %second_up_back.1 = (f32[256,1024]{1,0:T(8,128)}, f32[1,1024]{1,0:T(1,128)}, bf16[256,1024]{1,0:T(8,128)(2,1)}) custom-call(bf16[256,4096]{1,0:T(8,128)(2,1)} %second_down_back.1.refs_4_.grad_ref, f32[256,1024]{1,0:T(8,128)} %copy-done.13, f32[1,1024]{1,0:T(1,128)} %slice.559.gain_ref, f32[256,1024]{1,0:T(8,128)} %get-tuple-element.214.rows_ref, ...), custom_call_target="tpu_custom_call" | custom-call | flops 1024 | bytes 1024 | tf_op jit(solution)/shard_map/second_up_back/pallas_call | solution.py:569
  415.5 7.8 second_terms_send.1
  471.2 9.0 %taps_back.1 = (bf16[256,1024]{1,0:T(8,128)(2,1)}, bf16[256,1024]{1,0:T(8,128)(2,1)}) custom-call(s32[1]{0:T(128)} %bitcast.79.count_ref, bf16[15,1024]{1,0:T(8,128)(2,1)} %copy-done.71, bf16[256,1024]{1,0:T(8,128)(2,1)} %get-tuple-element.226.grad_ref, bf16[15,1024]{1,0:T(8,128)(2,1)} %copy-done.72, f32[31,1024]{1,0:T(8,128)} %copy-done.41, ...), custom_call_target="tpu_custom_call" | custom-call | flops 1024 | bytes 1024 | tf_op jit(solution)/shard_map/taps_back/pallas_call | solution.py:751
  496.6 8.7 %second_terms_fold.1 = (bf16[4,256,512]{2,1,0:T(8,128)(2,1)}, bf16[4,256,512]{2,1,0:T(8,128)(2,1)}, bf16[2,4,256,512]{3,2,1,0:T(8,128)(2,1)}) custom-call(s32[2,4]{1,0:T(2,128)} %pad_add_fusion.table_ref, bf16[256,1024]{1,0:T(8,128)(2,1)} %multiply_convert_fusion.1.normed_ref.refs_0_.refs_1_, ...), custom_call_target="tpu_custom_call" | custom-call | flops 1024 | bytes 1024 | tf_op jit(solution)/shard_map/second_terms_fold/pallas_call | solution.py:383
  505.3 23.4 %attend_back.1 = (bf16[256,1024]{1,0:T(8,128)(2,1)S(1)}, bf16[1024,1024]{1,0:T(8,128)(2,1)S(1)}, bf16[1024,1024]{1,0:T(8,128)(2,1)S(1)}) custom-call(s32[5]{0:T(128)S(1)} %pad_add_fusion.2.offsets_ref, bf16[256,1024]{1,0:T(8,128)(2,1)S(1)} %copy-done.8, bf16[1024,1024]{1,0:T(8,128)(2,1)} %copy-done.4, bf16[1024,1024]{1,0:T(8,128)(2,1)} %copy-done.3, ...), custom_call_target="tpu_custom_call" | custom-call | tf_op jit(solution)/shard_map/attend_back/pallas_call | solution.py:1058
  534.9 8.7 %attend_blocks_back.1 = bf16[4,256,1024]{2,1,0:T(8,128)(2,1)} custom-call(bf16[1024,1024]{1,0:T(8,128)(2,1)} %copy-done, bf16[1024,1024]{1,0:T(8,128)(2,1)} %copy-done.1, bf16[32,224,1024]{2,1,0:T(8,128)(2,1)} %bitcast.179, bf16[32,224,1024]{2,1,0:T(8,128)(2,1)} %bitcast.180), custom_call_target="tpu_custom_call" | custom-call | flops 1024 | bytes 1024 | tf_op jit(solution)/shard_map/attend_blocks_back/pallas_call | solution.py:902
  553.8 10.1 %attend_terms_send.1 = (bf16[2,4,128,512]{3,2,1,0:T(8,128)(2,1)}, bf16[2,4,128,512]{3,2,1,0:T(8,128)(2,1)}) custom-call(s32[2,2]{1,0:T(2,128)} %pad_add_fusion.1.table_ref, bf16[1024,1024]{1,0:T(8,128)(2,1)} %bitcast.20.refs_0_.refs_1_.refs_6_.refs_7_, bf16[1024,1024]{1,0:T(8,128)(2,1)} %bitcast.20.refs_0_.refs_1_.refs_6_.refs_7_, ...), custom_call_target="tpu_custom_call" | custom-call | flops 1024 | bytes 1024 | tf_op jit(solution)/shard_map/attend_terms_send/pallas_call | solution.py:383
  645.9 10.2 %attend_terms_fold.1 = (bf16[4,128,512]{2,1,0:T(8,128)(2,1)}, bf16[4,128,512]{2,1,0:T(8,128)(2,1)}, bf16[2,4,128,512]{3,2,1,0:T(8,128)(2,1)}) custom-call(s32[2,4]{1,0:T(2,128)} %pad_add_fusion.table_ref, bf16[1024,1024]{1,0:T(8,128)(2,1)} %bitcast.20.refs_0_.refs_1_.refs_6_.refs_7_, bf16[1024,1024]{1,0:T(8,128)(2,1)} %bitcast.20.refs_0_.refs_1_.refs_6_.refs_7_, ...), custom_call_target="tpu_custom_call" | custom-call | flops 1024 | bytes 1024 | tf_op jit(solution)/shard_map/attend_terms_fold/pallas_call | solution.py:383
  671.2 7.3 taps_sums.1
  689.8 8.5 %first_up_back.1 = (f32[256,1024]{1,0:T(8,128)}, f32[1,1024]{1,0:T(1,128)}, bf16[256,1024]{1,0:T(8,128)(2,1)}) custom-call(bf16[256,4096]{1,0:T(8,128)(2,1)} %first_down_back.1.refs_4_.grad_ref, f32[256,1024]{1,0:T(8,128)} %get-tuple-element.434.values_ref, f32[1,1024]{1,0:T(1,128)} %slice.568.gain_ref, f32[256,1024]{1,0:T(8,128)} %get-tuple-element.305.rows_ref, ...), custom_call_target="tpu_custom_call" | custom-call | flops 1024 | bytes 1024 | tf_op jit(solution)/shard_map/first_up_back/pallas_call | solution.py:569
  762.1 12.1 %collective-permute-done.78.got_ref = bf16[2,1,128,512]{3,2,1,0:T(8,128)(2,1)S(1)} collective-permute-done((bf16[2,1,128,512]{3,2,1,0:T(8,128)(2,1)}, bf16[2,1,128,512]{3,2,1,0:T(8,128)(2,1)S(1)}, u32[]{:S(2)}, u32[]{:S(2)}) %collective-permute-start.78) | collective-permute-done | bytes 262176 | tf_op jit(solution)/shard_map/ppermute | solution.py:43
  (556 shorter events, 410.0 us)
Async XLA Ops:
  7.2 122.1 %all-gather.7.cloned.1.call-start = ((), (), s32[]{:S(2)}) async-start(), calls=%async_computation | async-start | bytes 17301504 | tf_op jit(solution)/shard_map/all_gather | solution.py:513
  9.1 247.9 %all-gather.9.cloned.1.call-start = ((), (), s32[]{:S(2)}) async-start(), calls=%async_computation.1 | async-start | bytes 15138816 | tf_op jit(solution)/shard_map/all_gather | solution.py:513
  129.3 245.9 %all-gather.11.cloned.1.call-start = ((), (), s32[]{:S(2)}) async-start(), calls=%async_computation.2 | async-start | bytes 17301504 | tf_op jit(solution)/shard_map/all_gather | solution.py:513
  153.0 32.3 %collective-permute-start.5 = (bf16[256,1024]{1,0:T(8,128)(2,1)S(1)}, bf16[256,1024]{1,0:T(8,128)(2,1)S(1)}, u32[]{:S(2)}, u32[]{:S(2)}) collective-permute-start(bf16[256,1024]{1,0:T(8,128)(2,1)S(1)} %multiply_convert_fusion.5), channel_id=1, source_target_pairs={{1,0},{2,1},{3,2},{5,4},{6,5},{7,6},{9,8},{10,9},{11,10},{13,12},{... | collective-permute-start | bytes 1572872 | tf_op jit(solution)/shard_map/ppermute | solution.py:614
  154.3 32.3 %collective-permute-start.6 = (bf16[256,1024]{1,0:T(8,128)(2,1)S(1)}, bf16[256,1024]{1,0:T(8,128)(2,1)S(1)}, u32[]{:S(2)}, u32[]{:S(2)}) collective-permute-start(bf16[256,1024]{1,0:T(8,128)(2,1)S(1)} %multiply_convert_fusion.5), channel_id=1, source_target_pairs={{0,1},{1,2},{2,3},{4,5},{5,6},{6,7},{8,9},{9,10},{10,11},{12,13},{... | collective-permute-start | bytes 1572872 | tf_op jit(solution)/shard_map/ppermute | solution.py:613
  199.9 37.1 %collective-permute-start.10 = (bf16[256,1024]{1,0:T(8,128)(2,1)}, bf16[256,1024]{1,0:T(8,128)(2,1)S(1)}, u32[]{:S(2)}, u32[]{:S(2)}) collective-permute-start(bf16[256,1024]{1,0:T(8,128)(2,1)} %collective-permute-done.9), channel_id=1, source_target_pairs={{1,0},{2,1},{3,2},{5,4},{6,5},{7,6},{9,8},{10,9},{11,10},{13,12},{... | collective-permute-start | bytes 1572872 | tf_op jit(solution)/shard_map/ppermute | solution.py:614
  201.4 35.6 %collective-permute-start.8 = (bf16[256,1024]{1,0:T(8,128)(2,1)}, bf16[256,1024]{1,0:T(8,128)(2,1)S(1)}, u32[]{:S(2)}, u32[]{:S(2)}) collective-permute-start(bf16[256,1024]{1,0:T(8,128)(2,1)} %collective-permute-done.7), channel_id=1, source_target_pairs={{0,1},{1,2},{2,3},{4,5},{5,6},{6,7},{8,9},{9,10},{10,11},{12,13},{... | collective-permute-start | bytes 1572872 | tf_op jit(solution)/shard_map/ppermute | solution.py:613
  442.5 52.7 %collective-permute-start.25 = (bf16[2,4,256,512]{3,2,1,0:T(8,128)(2,1)}, bf16[2,4,256,512]{3,2,1,0:T(8,128)(2,1)S(1)}, u32[]{:S(2)}, u32[]{:S(2)}) collective-permute-start(bf16[2,4,256,512]{3,2,1,0:T(8,128)(2,1)} %get-tuple-element.221), channel_id=1, source_target_pairs={{0,8},{4,12},{8,0},{12,4},{16,24},{20,28},{24,16},{28,20},{1,9},{5... | collective-permute-start | bytes 6291464 | tf_op jit(solution)/shard_map/ppermute | solution.py:43
  443.7 51.5 %collective-permute-start.26 = (bf16[2,4,256,512]{3,2,1,0:T(8,128)(2,1)}, bf16[2,4,256,512]{3,2,1,0:T(8,128)(2,1)}, u32[]{:S(2)}, u32[]{:S(2)}) collective-permute-start(bf16[2,4,256,512]{3,2,1,0:T(8,128)(2,1)} %get-tuple-element.222), channel_id=1, source_target_pairs={{0,16},{4,20},{8,24},{12,28},{16,0},{20,4},{24,8},{28,12},{1,17},{... | collective-permute-start | bytes 6291464 | tf_op jit(solution)/shard_map/ppermute | solution.py:43
  444.5 35.7 %collective-permute-start.27 = (bf16[256,1024]{1,0:T(8,128)(2,1)S(1)}, bf16[256,1024]{1,0:T(8,128)(2,1)S(1)}, u32[]{:S(2)}, u32[]{:S(2)}) collective-permute-start(bf16[256,1024]{1,0:T(8,128)(2,1)S(1)} %copy-done.17), channel_id=1, source_target_pairs={{0,4},{4,0},{8,12},{12,8},{16,20},{20,16},{24,28},{28,24},{1,5},{5... | collective-permute-start | bytes 1572872 | tf_op jit(solution)/shard_map/ppermute | solution.py:43
  444.5 35.8 %collective-permute-start.34 = (bf16[256,1024]{1,0:T(8,128)(2,1)S(1)}, bf16[256,1024]{1,0:T(8,128)(2,1)S(1)}, u32[]{:S(2)}, u32[]{:S(2)}) collective-permute-start(bf16[256,1024]{1,0:T(8,128)(2,1)S(1)} %copy-done.19), channel_id=1, source_target_pairs={{0,4},{4,0},{8,12},{12,8},{16,20},{20,16},{24,28},{28,24},{1,5},{5... | collective-permute-start | bytes 1572872 | tf_op jit(solution)/shard_map/ppermute | solution.py:43
  482.4 61.2 %collective-permute-start.38 = (bf16[1024,1024]{1,0:T(8,128)(2,1)}, bf16[1024,1024]{1,0:T(8,128)(2,1)}, u32[]{:S(2)}, u32[]{:S(2)}) collective-permute-start(bf16[1024,1024]{1,0:T(8,128)(2,1)} %bitcast.20.refs_0_.refs_1_.refs_6_.refs_7_), channel_id=1, source_target_pairs={{0,4},{4,0},{8,12},{12,8},{16,20},{20,16},{24,28},{28,24},{1,5},{5... | collective-permute-start | bytes 6291464 | tf_op jit(solution)/shard_map/ppermute | solution.py:43
  529.2 24.5 %collective-permute-start.41 = (bf16[1024,1024]{1,0:T(8,128)(2,1)S(1)}, bf16[1024,1024]{1,0:T(8,128)(2,1)}, u32[]{:S(2)}, u32[]{:S(2)}) collective-permute-start(bf16[1024,1024]{1,0:T(8,128)(2,1)S(1)} %get-tuple-element.252.value_ref.refs_12_), channel_id=1, source_target_pairs={{0,4},{4,0},{8,12},{12,8},{16,20},{20,16},{24,28},{28,24},{1,5},{5... | collective-permute-start | bytes 6291464 | tf_op jit(solution)/shard_map/ppermute | solution.py:43
  553.7 57.5 %collective-permute-start.57 = (bf16[256,4096]{1,0:T(8,128)(2,1)}, bf16[256,4096]{1,0:T(8,128)(2,1)S(1)}, u32[]{:S(2)}, u32[]{:S(2)}) collective-permute-start(bf16[256,4096]{1,0:T(8,128)(2,1)} %get-tuple-element.203.active_ref.refs_0_.refs_1_), channel_id=1, source_target_pairs={{0,4},{4,0},{8,12},{12,8},{16,20},{20,16},{24,28},{28,24},{1,5},{5... | collective-permute-start | bytes 6291464 | tf_op jit(solution)/shard_map/ppermute | solution.py:43
  596.1 26.3 %collective-permute-start.55 = (bf16[2,4,128,512]{3,2,1,0:T(8,128)(2,1)}, bf16[2,4,128,512]{3,2,1,0:T(8,128)(2,1)S(1)}, u32[]{:S(2)}, u32[]{:S(2)}) collective-permute-start(bf16[2,4,128,512]{3,2,1,0:T(8,128)(2,1)} %get-tuple-element.272), channel_id=1, source_target_pairs={{0,8},{4,12},{8,0},{12,4},{16,24},{20,28},{24,16},{28,20},{1,9},{5... | collective-permute-start | bytes 3145736 | tf_op jit(solution)/shard_map/ppermute | solution.py:43
  598.5 25.5 %collective-permute-start.56 = (bf16[2,4,128,512]{3,2,1,0:T(8,128)(2,1)}, bf16[2,4,128,512]{3,2,1,0:T(8,128)(2,1)}, u32[]{:S(2)}, u32[]{:S(2)}) collective-permute-start(bf16[2,4,128,512]{3,2,1,0:T(8,128)(2,1)} %get-tuple-element.273), channel_id=1, source_target_pairs={{0,16},{4,20},{8,24},{12,28},{16,0},{20,4},{24,8},{28,12},{1,17},{... | collective-permute-start | bytes 3145736 | tf_op jit(solution)/shard_map/ppermute | solution.py:43
  604.4 26.9 %collective-permute-start.52 = (bf16[2,2,256,512]{3,2,1,0:T(8,128)(2,1)}, bf16[2,2,256,512]{3,2,1,0:T(8,128)(2,1)}, u32[]{:S(2)}, u32[]{:S(2)}) collective-permute-start(bf16[2,2,256,512]{3,2,1,0:T(8,128)(2,1)} %get-tuple-element.267), channel_id=1, source_target_pairs={{0,1},{1,0},{2,3},{3,2},{4,5},{5,4},{6,7},{7,6},{8,9},{9,8},{10,11... | collective-permute-start | bytes 3145736 | tf_op jit(solution)/shard_map/ppermute | solution.py:43
  631.3 24.8 %collective-permute-start.64 = (bf16[256,4096]{1,0:T(8,128)(2,1)}, bf16[256,4096]{1,0:T(8,128)(2,1)S(1)}, u32[]{:S(2)}, u32[]{:S(2)}) collective-permute-start(bf16[256,4096]{1,0:T(8,128)(2,1)} %first_down_back.1.refs_4_.grad_ref), channel_id=1, source_target_pairs={{0,4},{4,0},{8,12},{12,8},{16,20},{20,16},{24,28},{28,24},{1,5},{5... | collective-permute-start | bytes 6291464 | tf_op jit(solution)/shard_map/ppermute | solution.py:43
  631.4 31.9 %collective-permute-start.61 = (bf16[2,4,128,512]{3,2,1,0:T(8,128)(2,1)}, bf16[2,4,128,512]{3,2,1,0:T(8,128)(2,1)}, u32[]{:S(2)}, u32[]{:S(2)}) collective-permute-start(bf16[2,4,128,512]{3,2,1,0:T(8,128)(2,1)} %get-tuple-element.293), channel_id=1, source_target_pairs={{0,8},{4,12},{8,0},{12,4},{16,24},{20,28},{24,16},{28,20},{1,9},{5... | collective-permute-start | bytes 3145736 | tf_op jit(solution)/shard_map/ppermute | solution.py:43
  632.1 31.2 %collective-permute-start.62 = (bf16[2,4,128,512]{3,2,1,0:T(8,128)(2,1)}, bf16[2,4,128,512]{3,2,1,0:T(8,128)(2,1)}, u32[]{:S(2)}, u32[]{:S(2)}) collective-permute-start(bf16[2,4,128,512]{3,2,1,0:T(8,128)(2,1)} %get-tuple-element.294), channel_id=1, source_target_pairs={{0,16},{4,20},{8,24},{12,28},{16,0},{20,4},{24,8},{28,12},{1,17},{... | collective-permute-start | bytes 3145736 | tf_op jit(solution)/shard_map/ppermute | solution.py:43
  636.4 26.8 %collective-permute-start.59 = (bf16[2,1,256,512]{3,2,1,0:T(8,128)(2,1)}, bf16[2,1,256,512]{3,2,1,0:T(8,128)(2,1)S(1)}, u32[]{:S(2)}, u32[]{:S(2)}) collective-permute-start(bf16[2,1,256,512]{3,2,1,0:T(8,128)(2,1)} %get-tuple-element.286), channel_id=1, source_target_pairs={{0,2},{1,3},{2,0},{3,1},{4,6},{5,7},{6,4},{7,5},{8,10},{9,11},{10,... | collective-permute-start | bytes 1572872 | tf_op jit(solution)/shard_map/ppermute | solution.py:43
  664.0 43.5 %collective-permute-start.68 = (bf16[2,4,128,512]{3,2,1,0:T(8,128)(2,1)}, bf16[2,4,128,512]{3,2,1,0:T(8,128)(2,1)S(1)}, u32[]{:S(2)}, u32[]{:S(2)}) collective-permute-start(bf16[2,4,128,512]{3,2,1,0:T(8,128)(2,1)} %get-tuple-element.314), channel_id=1, source_target_pairs={{0,8},{4,12},{8,0},{12,4},{16,24},{20,28},{24,16},{28,20},{1,9},{5... | collective-permute-start | bytes 3145736 | tf_op jit(solution)/shard_map/ppermute | solution.py:43
  664.5 43.1 %collective-permute-start.69 = (bf16[2,4,128,512]{3,2,1,0:T(8,128)(2,1)}, bf16[2,4,128,512]{3,2,1,0:T(8,128)(2,1)S(1)}, u32[]{:S(2)}, u32[]{:S(2)}) collective-permute-start(bf16[2,4,128,512]{3,2,1,0:T(8,128)(2,1)} %get-tuple-element.315), channel_id=1, source_target_pairs={{0,16},{4,20},{8,24},{12,28},{16,0},{20,4},{24,8},{28,12},{1,17},{... | collective-permute-start | bytes 3145736 | tf_op jit(solution)/shard_map/ppermute | solution.py:43
  746.2 28.1 %collective-permute-start.77 = (bf16[2,2,128,512]{3,2,1,0:T(8,128)(2,1)}, bf16[2,2,128,512]{3,2,1,0:T(8,128)(2,1)S(1)}, u32[]{:S(2)}, u32[]{:S(2)}) collective-permute-start(bf16[2,2,128,512]{3,2,1,0:T(8,128)(2,1)} %get-tuple-element.356), channel_id=1, source_target_pairs={{0,1},{1,0},{2,3},{3,2},{4,5},{5,4},{6,7},{7,6},{8,9},{9,8},{10,11... | collective-permute-start | bytes 1572872 | tf_op jit(solution)/shard_map/ppermute | solution.py:43
  (159 other events, 2039.1 us)
Sparse Core Ops, SparseCore 0:
  11.6 117.6 all-gather.6
  132.7 124.3 all-gather.8
  260.6 114.4 all-gather.10

commit v5 on v4

--- a/solution.py
+++ b/solution.py
@@ -796,10 +796,6 @@
     sums_ref[1:2] = jnp.sum(grad * normal, axis=0, keepdims=True)
 
 
-def add_kernel(left_ref, right_ref, out_ref):
-    out_ref[...] = left_ref[...] + right_ref[...]
-
-
 def depth_back_kernel(
     count_ref, grad_ref, depth_ref, vectors_ref, totals_ref, out_ref, top_ref, bottom_ref
 ):
@@ -931,12 +927,9 @@
     return ffn_call(kernel, name, packed.array, "up", inputs, input_outs(rows), scratch)
 
 
-def sum_in_steps(values, bits):
-    for axis, bit in bits:
-        (values,) = step_call(
-            add_kernel, "add", [], [values, swap(values, axis, bit)], [rows_like(values)]
-        )
-    return values
+def sum_at_once(values, axis, offsets):
+    got = [swap(values, axis, offset) for offset in offsets]
+    return values + (got[0] + (got[1] + got[2]))
 
 
 def key_valid(offsets_ref, rows, keys):
@@ -1387,7 +1380,6 @@
         grad_rows, grad_gain_two, branch_conv = ffn_up_back_input(
             hidden_two, rows_third, gain(g_second), grad_rows, up_two, 1.0, "second_up_back"
         )
-        grad_rows, branch_conv = fence([two], grad_rows, branch_conv)
         depth, inverse_std = conv_stored[10], conv_stored[7]
         spread = jnp.broadcast_to(frame_count, (model_width,))
         vectors = jnp.stack([batch_stats[0], inverse_std, scale_float, shift_float, spread])
@@ -1398,10 +1390,12 @@
             [branch_conv, depth, vectors, Block(middle, 6)],
             [rows_like(depth), vector_like(depth, 2)],
         )
-        totals = sum_in_steps(sums, [("dp", b) for b in axis_bits("dp")])
+        beside = swap(sums, "dp", 1)
+        (beside,) = fence([two], beside)
+        totals = sum_at_once(sums + beside, "dp", (2, 4, 6))
         (totals,) = fence([two], totals)
         two.first_swap()
-        totals = sum_in_steps(totals, [("seq", b) for b in axis_bits("seq")])
+        totals = sum_at_once(totals, "seq", (1, 2, 3))
         rim = jax.ShapeDtypeStruct((taps // 2, model_width), bf16)
         grad_depth, top, bottom = step_call(
             depth_back_kernel,
@@ -1551,14 +1545,14 @@
         few.step()
         up_sum.second_send()
         up_sum.second_swap()
+        attend_sum.z_send(2)
+        attend_sum.z_swap(2)
         conv_grads = conv.finish()
         (conv_grads,) = fence([down_sum, attend_sum, up_sum, few], conv_grads)
         down_sum.z_send(1)
         down_sum.z_swap(1)
         up_sum.z_send(1)
         up_sum.z_swap(1)
-        attend_sum.z_send(2)
-        attend_sum.z_swap(2)
         few.step()
         fence([down_sum, up_sum, attend_sum, few])
         down_sum.z_send(2)

time: 824 us -> 812 us (0.985)
    pallas_call x12 -> x7, Pallas kernels: 44.6 us -> 37.9 us  [step_call(): pl.pallas_call(kernel, grid_spec=pltpu.PrefetchScalarGridSpec(num_scalar_...]
    ppermute x69 -> x71, waiting for transfers between devices: 87.7 us -> 88.2 us  [swap(): lax.ppermute(values, axis, [(i, i ^ bit) for i in range(lax.axis_size(axi...]
    ppermute x69 -> x71, starting transfers between devices: 66.5 us -> 66.5 us  [swap(): lax.ppermute(values, axis, [(i, i ^ bit) for i in range(lax.axis_size(axi...]
  transfers between devices with their start and end apart: 88 -> 90, of which waited for: 46 -> 46; matrix products, arithmetic and copies ran while one was open for 11% -> 11% of each run, Pallas kernels for 27% -> 28%
where the time goes in v5:
time: 812 us; the launch traced here: 805 us
  waiting for transfers between devices  321 us (40%)
  Pallas kernels  261 us (32%)
  starting transfers between devices  108 us (13%)
  local copies, waits for them, and re-layouts  48 us (6%)
  other arithmetic  34.3 us (4%)
  between operations  17.7 us (2%)
  matrix products  15.5 us (2%)
    all_gather x3, waiting for transfers between devices, gather_packed(): return lax.all_gather(part, ('dp', 'seq'), axis=0)  147 us
    ppermute x71, waiting for transfers between devices, swap(): lax.ppermute(values, axis, [(i, i ^ bit) for i in range(lax.axis_size(axi...  88.2 us
    pallas_call x10, Pallas kernels, call(): pl.pallas_call(functools.partial(kernel, self.shape, 4), grid_spec=pltpu....  70.2 us
    ppermute x71, starting transfers between devices, swap(): lax.ppermute(values, axis, [(i, i ^ bit) for i in range(lax.axis_size(axi...  66.5 us
    ppermute x3, waiting for transfers between devices, gather_line(): lax.ppermute(downs[-1], 'seq', [(i + 1, i) for i in range(seq - 1)])  63.8 us
    pallas_call x8, Pallas kernels, ffn_call(): pl.pallas_call(kernel, grid=(steps,), in_specs=[spec(x) for x in inputs]...  62.5 us
    pallas_call x18, Pallas kernels, whole_call(): pl.pallas_call(kernel, grid_spec=pltpu.PrefetchScalarGridSpec(num_scalar_...  41 us
    pallas_call x7, Pallas kernels, step_call(): pl.pallas_call(kernel, grid_spec=pltpu.PrefetchScalarGridSpec(num_scalar_...  37.9 us
  transfers between devices with their start and end apart: 90, of which 46 were waited for; matrix products, arithmetic and copies ran while one was open for 11% of the time, Pallas kernels for 28%

profile of v5, /device:TPU:0, one launch (start us, length us, event | category | flops | bytes accessed | tf_op | source)
XLA Modules:
  0.0 804.7 jit_solution(14357648311741877825)
XLA Ops:
  37.0 92.2 %all-gather.7.cloned.1.call-done = bf16[8192,1024]{1,0:T(8,128)(2,1)} async-done(((bf16[256,1024]{1,0:T(8,128)(2,1)}), bf16[8192,1024]{1,0:T(8,128)(2,1)}) %all-gather.7.cloned.1.call-update) | async-done | bytes 16777232 | tf_op jit(solution)/shard_map/all_gather | solution.py:513
  134.2 8.1 %first_up.1 = (bf16[256,4096]{1,0:T(8,128)(2,1)}, bf16[256,4096]{1,0:T(8,128)(2,1)}) custom-call(bf16[256,1024]{1,0:T(8,128)(2,1)} %get-tuple-element.431.normed_ref.refs_0_.refs_1_, bf16[32,256,1024]{2,1,0:T(8,128)(2,1)} %bitcast.182), custom_call_target="tpu_custom_call" | custom-call | flops 1024 | bytes 1024 | tf_op jit(solution)/shard_map/first_up/pallas_call | solution.py:569
  142.3 7.4 first_down.1.values_ref
  158.9 26.5 %collective-permute-done.5 = bf16[256,1024]{1,0:T(8,128)(2,1)S(1)} collective-permute-done((bf16[256,1024]{1,0:T(8,128)(2,1)S(1)}, bf16[256,1024]{1,0:T(8,128)(2,1)S(1)}, u32[]{:S(2)}, u32[]{:S(2)}) %collective-permute-start.5) | collective-permute-done | bytes 524320 | tf_op jit(solution)/shard_map/ppermute | solution.py:614
  192.0 7.9 collective-permute-done.9
  207.4 29.4 %collective-permute-done.10 = bf16[256,1024]{1,0:T(8,128)(2,1)S(1)} collective-permute-done((bf16[256,1024]{1,0:T(8,128)(2,1)}, bf16[256,1024]{1,0:T(8,128)(2,1)S(1)}, u32[]{:S(2)}, u32[]{:S(2)}) %collective-permute-start.10) | collective-permute-done | bytes 524320 | tf_op jit(solution)/shard_map/ppermute | solution.py:614
  238.6 18.4 %all-gather.9.cloned.1.call-done = bf16[7168,1024]{1,0:T(8,128)(2,1)} async-done(((bf16[224,1024]{1,0:T(8,128)(2,1)}), bf16[7168,1024]{1,0:T(8,128)(2,1)}) %all-gather.9.cloned.1.call-update) | async-done | bytes 14680080 | tf_op jit(solution)/shard_map/all_gather | solution.py:513
  260.7 7.9 fusion.44
  278.2 16.9 %attend.1 = (bf16[256,1024]{1,0:T(8,128)(2,1)S(1)}, f32[8,2,256]{2,1,0:T(2,128)S(1)}) custom-call(s32[5]{0:T(128)S(1)} %pad_add_fusion.2.offsets_ref, bf16[256,1024]{1,0:T(8,128)(2,1)S(1)} %convolution_convert_fusion.2.query_ref, bf16[1024,1024]{1,0:T(8,128)(2,1)S(1)} %convolution_convert_fusion.1.key_ref, ...), custom_call_target="tpu_custom_call" | custom-call | tf_op jit(solution)/shard_map/attend/pallas_call | solution.py:1013
  338.6 36.6 %all-gather.11.cloned.1.call-done = bf16[8192,1024]{1,0:T(8,128)(2,1)} async-done(((bf16[256,1024]{1,0:T(8,128)(2,1)}), bf16[8192,1024]{1,0:T(8,128)(2,1)}) %all-gather.11.cloned.1.call-update) | async-done | bytes 16777232 | tf_op jit(solution)/shard_map/all_gather | solution.py:513
  375.1 8.0 second_up.1
  383.1 7.3 second_down.1.values_ref
  393.7 7.4 second_down_back.1.refs_4_.grad_ref
  406.4 8.5 %second_up_back.1 = (f32[256,1024]{1,0:T(8,128)}, f32[1,1024]{1,0:T(1,128)}, bf16[256,1024]{1,0:T(8,128)(2,1)}) custom-call(bf16[256,4096]{1,0:T(8,128)(2,1)} %second_down_back.1.refs_4_.grad_ref, f32[256,1024]{1,0:T(8,128)} %copy-done.13, f32[1,1024]{1,0:T(1,128)} %slice.559.gain_ref, f32[256,1024]{1,0:T(8,128)} %get-tuple-element.213.rows_ref, ...), custom_call_target="tpu_custom_call" | custom-call | flops 1024 | bytes 1024 | tf_op jit(solution)/shard_map/second_up_back/pallas_call | solution.py:569
  420.0 7.9 second_terms_send.1
  457.9 9.0 %taps_back.1 = (bf16[256,1024]{1,0:T(8,128)(2,1)}, bf16[256,1024]{1,0:T(8,128)(2,1)}) custom-call(s32[1]{0:T(128)} %bitcast.79.count_ref, bf16[15,1024]{1,0:T(8,128)(2,1)} %copy-done.73, bf16[256,1024]{1,0:T(8,128)(2,1)} %get-tuple-element.224.grad_ref, bf16[15,1024]{1,0:T(8,128)(2,1)} %copy-done.74, f32[31,1024]{1,0:T(8,128)} %copy-done.41, ...), custom_call_target="tpu_custom_call" | custom-call | flops 1024 | bytes 1024 | tf_op jit(solution)/shard_map/taps_back/pallas_call | solution.py:751
  483.2 8.7 %second_terms_fold.1 = (bf16[4,256,512]{2,1,0:T(8,128)(2,1)}, bf16[4,256,512]{2,1,0:T(8,128)(2,1)}, bf16[2,4,256,512]{3,2,1,0:T(8,128)(2,1)}) custom-call(s32[2,4]{1,0:T(2,128)} %pad_add_fusion.table_ref, bf16[256,1024]{1,0:T(8,128)(2,1)} %multiply_convert_fusion.1.normed_ref.refs_0_.refs_1_, ...), custom_call_target="tpu_custom_call" | custom-call | flops 1024 | bytes 1024 | tf_op jit(solution)/shard_map/second_terms_fold/pallas_call | solution.py:383
  492.0 23.4 %attend_back.1 = (bf16[256,1024]{1,0:T(8,128)(2,1)S(1)}, bf16[1024,1024]{1,0:T(8,128)(2,1)S(1)}, bf16[1024,1024]{1,0:T(8,128)(2,1)S(1)}) custom-call(s32[5]{0:T(128)S(1)} %pad_add_fusion.2.offsets_ref, bf16[256,1024]{1,0:T(8,128)(2,1)S(1)} %copy-done.8, bf16[1024,1024]{1,0:T(8,128)(2,1)} %copy-done.4, bf16[1024,1024]{1,0:T(8,128)(2,1)} %copy-done.3, ...), custom_call_target="tpu_custom_call" | custom-call | tf_op jit(solution)/shard_map/attend_back/pallas_call | solution.py:1051
  521.5 8.7 %attend_blocks_back.1 = bf16[4,256,1024]{2,1,0:T(8,128)(2,1)} custom-call(bf16[1024,1024]{1,0:T(8,128)(2,1)} %copy-done, bf16[1024,1024]{1,0:T(8,128)(2,1)} %copy-done.1, bf16[32,224,1024]{2,1,0:T(8,128)(2,1)} %bitcast.179, bf16[32,224,1024]{2,1,0:T(8,128)(2,1)} %bitcast.180), custom_call_target="tpu_custom_call" | custom-call | flops 1024 | bytes 1024 | tf_op jit(solution)/shard_map/attend_blocks_back/pallas_call | solution.py:898
  540.4 10.1 %attend_terms_send.1 = (bf16[2,4,128,512]{3,2,1,0:T(8,128)(2,1)}, bf16[2,4,128,512]{3,2,1,0:T(8,128)(2,1)}) custom-call(s32[2,2]{1,0:T(2,128)} %pad_add_fusion.1.table_ref, bf16[1024,1024]{1,0:T(8,128)(2,1)} %bitcast.20.refs_0_.refs_1_.refs_6_.refs_7_, bf16[1024,1024]{1,0:T(8,128)(2,1)} %bitcast.20.refs_0_.refs_1_.refs_6_.refs_7_, ...), custom_call_target="tpu_custom_call" | custom-call | flops 1024 | bytes 1024 | tf_op jit(solution)/shard_map/attend_terms_send/pallas_call | solution.py:383
  631.1 10.2 %attend_terms_fold.1 = (bf16[4,128,512]{2,1,0:T(8,128)(2,1)}, bf16[4,128,512]{2,1,0:T(8,128)(2,1)}, bf16[2,4,128,512]{3,2,1,0:T(8,128)(2,1)}) custom-call(s32[2,4]{1,0:T(2,128)} %pad_add_fusion.table_ref, bf16[1024,1024]{1,0:T(8,128)(2,1)} %bitcast.20.refs_0_.refs_1_.refs_6_.refs_7_, bf16[1024,1024]{1,0:T(8,128)(2,1)} %bitcast.20.refs_0_.refs_1_.refs_6_.refs_7_, ...), custom_call_target="tpu_custom_call" | custom-call | flops 1024 | bytes 1024 | tf_op jit(solution)/shard_map/attend_terms_fold/pallas_call | solution.py:383
  658.1 7.3 taps_sums.1
  676.5 8.5 %first_up_back.1 = (f32[256,1024]{1,0:T(8,128)}, f32[1,1024]{1,0:T(1,128)}, bf16[256,1024]{1,0:T(8,128)(2,1)}) custom-call(bf16[256,4096]{1,0:T(8,128)(2,1)} %first_down_back.1.refs_4_.grad_ref, f32[256,1024]{1,0:T(8,128)} %get-tuple-element.432.values_ref, f32[1,1024]{1,0:T(1,128)} %slice.568.gain_ref, f32[256,1024]{1,0:T(8,128)} %get-tuple-element.303.rows_ref, ...), custom_call_target="tpu_custom_call" | custom-call | flops 1024 | bytes 1024 | tf_op jit(solution)/shard_map/first_up_back/pallas_call | solution.py:569
  717.7 13.1 %collective-permute-done.78 = f32[16,37,32]{1,2,0:T(8,128)S(1)} collective-permute-done((f32[16,37,32]{1,2,0:T(8,128)}, f32[16,37,32]{1,2,0:T(8,128)S(1)}, u32[]{:S(2)}, u32[]{:S(2)}) %collective-permute-start.78) | collective-permute-done | bytes 75808 | tf_op jit(solution)/shard_map/ppermute | solution.py:43
  (552 shorter events, 397.7 us)
Async XLA Ops:
  7.2 122.1 %all-gather.7.cloned.1.call-start = ((), (), s32[]{:S(2)}) async-start(), calls=%async_computation | async-start | bytes 17301504 | tf_op jit(solution)/shard_map/all_gather | solution.py:513
  9.1 247.8 %all-gather.9.cloned.1.call-start = ((), (), s32[]{:S(2)}) async-start(), calls=%async_computation.1 | async-start | bytes 15138816 | tf_op jit(solution)/shard_map/all_gather | solution.py:513
  129.3 245.8 %all-gather.11.cloned.1.call-start = ((), (), s32[]{:S(2)}) async-start(), calls=%async_computation.2 | async-start | bytes 17301504 | tf_op jit(solution)/shard_map/all_gather | solution.py:513
  153.0 32.4 %collective-permute-start.5 = (bf16[256,1024]{1,0:T(8,128)(2,1)S(1)}, bf16[256,1024]{1,0:T(8,128)(2,1)S(1)}, u32[]{:S(2)}, u32[]{:S(2)}) collective-permute-start(bf16[256,1024]{1,0:T(8,128)(2,1)S(1)} %multiply_convert_fusion.5), channel_id=1, source_target_pairs={{1,0},{2,1},{3,2},{5,4},{6,5},{7,6},{9,8},{10,9},{11,10},{13,12},{... | collective-permute-start | bytes 1572872 | tf_op jit(solution)/shard_map/ppermute | solution.py:614
  154.3 32.4 %collective-permute-start.6 = (bf16[256,1024]{1,0:T(8,128)(2,1)S(1)}, bf16[256,1024]{1,0:T(8,128)(2,1)S(1)}, u32[]{:S(2)}, u32[]{:S(2)}) collective-permute-start(bf16[256,1024]{1,0:T(8,128)(2,1)S(1)} %multiply_convert_fusion.5), channel_id=1, source_target_pairs={{0,1},{1,2},{2,3},{4,5},{5,6},{6,7},{8,9},{9,10},{10,11},{12,13},{... | collective-permute-start | bytes 1572872 | tf_op jit(solution)/shard_map/ppermute | solution.py:613
  199.9 36.9 %collective-permute-start.10 = (bf16[256,1024]{1,0:T(8,128)(2,1)}, bf16[256,1024]{1,0:T(8,128)(2,1)S(1)}, u32[]{:S(2)}, u32[]{:S(2)}) collective-permute-start(bf16[256,1024]{1,0:T(8,128)(2,1)} %collective-permute-done.9), channel_id=1, source_target_pairs={{1,0},{2,1},{3,2},{5,4},{6,5},{7,6},{9,8},{10,9},{11,10},{13,12},{... | collective-permute-start | bytes 1572872 | tf_op jit(solution)/shard_map/ppermute | solution.py:614
  201.4 35.5 %collective-permute-start.8 = (bf16[256,1024]{1,0:T(8,128)(2,1)}, bf16[256,1024]{1,0:T(8,128)(2,1)S(1)}, u32[]{:S(2)}, u32[]{:S(2)}) collective-permute-start(bf16[256,1024]{1,0:T(8,128)(2,1)} %collective-permute-done.7), channel_id=1, source_target_pairs={{0,1},{1,2},{2,3},{4,5},{5,6},{6,7},{8,9},{9,10},{10,11},{12,13},{... | collective-permute-start | bytes 1572872 | tf_op jit(solution)/shard_map/ppermute | solution.py:613
  434.6 47.2 %collective-permute-start.26 = (bf16[2,4,256,512]{3,2,1,0:T(8,128)(2,1)}, bf16[2,4,256,512]{3,2,1,0:T(8,128)(2,1)S(1)}, u32[]{:S(2)}, u32[]{:S(2)}) collective-permute-start(bf16[2,4,256,512]{3,2,1,0:T(8,128)(2,1)} %get-tuple-element.219), channel_id=1, source_target_pairs={{0,8},{4,12},{8,0},{12,4},{16,24},{20,28},{24,16},{28,20},{1,9},{5... | collective-permute-start | bytes 6291464 | tf_op jit(solution)/shard_map/ppermute | solution.py:43
  436.2 46.1 %collective-permute-start.27 = (bf16[2,4,256,512]{3,2,1,0:T(8,128)(2,1)}, bf16[2,4,256,512]{3,2,1,0:T(8,128)(2,1)}, u32[]{:S(2)}, u32[]{:S(2)}) collective-permute-start(bf16[2,4,256,512]{3,2,1,0:T(8,128)(2,1)} %get-tuple-element.220), channel_id=1, source_target_pairs={{0,16},{4,20},{8,24},{12,28},{16,0},{20,4},{24,8},{28,12},{1,17},{... | collective-permute-start | bytes 6291464 | tf_op jit(solution)/shard_map/ppermute | solution.py:43
  441.1 25.8 %collective-permute-start.28 = (bf16[256,1024]{1,0:T(8,128)(2,1)S(1)}, bf16[256,1024]{1,0:T(8,128)(2,1)S(1)}, u32[]{:S(2)}, u32[]{:S(2)}) collective-permute-start(bf16[256,1024]{1,0:T(8,128)(2,1)S(1)} %copy-done.17), channel_id=1, source_target_pairs={{0,4},{4,0},{8,12},{12,8},{16,20},{20,16},{24,28},{28,24},{1,5},{5... | collective-permute-start | bytes 1572872 | tf_op jit(solution)/shard_map/ppermute | solution.py:43
  441.7 25.3 %collective-permute-start.36 = (bf16[256,1024]{1,0:T(8,128)(2,1)S(1)}, bf16[256,1024]{1,0:T(8,128)(2,1)S(1)}, u32[]{:S(2)}, u32[]{:S(2)}) collective-permute-start(bf16[256,1024]{1,0:T(8,128)(2,1)S(1)} %copy-done.19), channel_id=1, source_target_pairs={{0,4},{4,0},{8,12},{12,8},{16,20},{20,16},{24,28},{28,24},{1,5},{5... | collective-permute-start | bytes 1572872 | tf_op jit(solution)/shard_map/ppermute | solution.py:43
  469.1 61.2 %collective-permute-start.40 = (bf16[1024,1024]{1,0:T(8,128)(2,1)}, bf16[1024,1024]{1,0:T(8,128)(2,1)}, u32[]{:S(2)}, u32[]{:S(2)}) collective-permute-start(bf16[1024,1024]{1,0:T(8,128)(2,1)} %bitcast.20.refs_0_.refs_1_.refs_6_.refs_7_), channel_id=1, source_target_pairs={{0,4},{4,0},{8,12},{12,8},{16,20},{20,16},{24,28},{28,24},{1,5},{5... | collective-permute-start | bytes 6291464 | tf_op jit(solution)/shard_map/ppermute | solution.py:43
  515.9 24.4 %collective-permute-start.43 = (bf16[1024,1024]{1,0:T(8,128)(2,1)S(1)}, bf16[1024,1024]{1,0:T(8,128)(2,1)}, u32[]{:S(2)}, u32[]{:S(2)}) collective-permute-start(bf16[1024,1024]{1,0:T(8,128)(2,1)S(1)} %get-tuple-element.250.value_ref.refs_12_), channel_id=1, source_target_pairs={{0,4},{4,0},{8,12},{12,8},{16,20},{20,16},{24,28},{28,24},{1,5},{5... | collective-permute-start | bytes 6291464 | tf_op jit(solution)/shard_map/ppermute | solution.py:43
  540.3 57.2 %collective-permute-start.59 = (bf16[256,4096]{1,0:T(8,128)(2,1)}, bf16[256,4096]{1,0:T(8,128)(2,1)S(1)}, u32[]{:S(2)}, u32[]{:S(2)}) collective-permute-start(bf16[256,4096]{1,0:T(8,128)(2,1)} %get-tuple-element.202.active_ref.refs_0_.refs_1_), channel_id=1, source_target_pairs={{0,4},{4,0},{8,12},{12,8},{16,20},{20,16},{24,28},{28,24},{1,5},{5... | collective-permute-start | bytes 6291464 | tf_op jit(solution)/shard_map/ppermute | solution.py:43
  560.5 24.0 %collective-permute-start.39 = (bf16[4,256,512]{2,1,0:T(8,128)(2,1)}, bf16[4,256,512]{2,1,0:T(8,128)(2,1)}, u32[]{:S(2)}, u32[]{:S(2)}) collective-permute-start(bf16[4,256,512]{2,1,0:T(8,128)(2,1)} %get-tuple-element.244), channel_id=1, source_target_pairs={{0,8},{4,12},{8,0},{12,4},{16,24},{20,28},{24,16},{28,20},{1,9},{5... | collective-permute-start | bytes 3145736 | tf_op jit(solution)/shard_map/ppermute | solution.py:43
  582.6 26.3 %collective-permute-start.57 = (bf16[2,4,128,512]{3,2,1,0:T(8,128)(2,1)}, bf16[2,4,128,512]{3,2,1,0:T(8,128)(2,1)S(1)}, u32[]{:S(2)}, u32[]{:S(2)}) collective-permute-start(bf16[2,4,128,512]{3,2,1,0:T(8,128)(2,1)} %get-tuple-element.270), channel_id=1, source_target_pairs={{0,8},{4,12},{8,0},{12,4},{16,24},{20,28},{24,16},{28,20},{1,9},{5... | collective-permute-start | bytes 3145736 | tf_op jit(solution)/shard_map/ppermute | solution.py:43
  584.5 26.2 %collective-permute-start.58 = (bf16[2,4,128,512]{3,2,1,0:T(8,128)(2,1)}, bf16[2,4,128,512]{3,2,1,0:T(8,128)(2,1)}, u32[]{:S(2)}, u32[]{:S(2)}) collective-permute-start(bf16[2,4,128,512]{3,2,1,0:T(8,128)(2,1)} %get-tuple-element.271), channel_id=1, source_target_pairs={{0,16},{4,20},{8,24},{12,28},{16,0},{20,4},{24,8},{28,12},{1,17},{... | collective-permute-start | bytes 3145736 | tf_op jit(solution)/shard_map/ppermute | solution.py:43
  590.9 27.1 %collective-permute-start.54 = (bf16[2,2,256,512]{3,2,1,0:T(8,128)(2,1)}, bf16[2,2,256,512]{3,2,1,0:T(8,128)(2,1)}, u32[]{:S(2)}, u32[]{:S(2)}) collective-permute-start(bf16[2,2,256,512]{3,2,1,0:T(8,128)(2,1)} %get-tuple-element.265), channel_id=1, source_target_pairs={{0,1},{1,0},{2,3},{3,2},{4,5},{5,4},{6,7},{7,6},{8,9},{9,8},{10,11... | collective-permute-start | bytes 3145736 | tf_op jit(solution)/shard_map/ppermute | solution.py:43
  618.1 32.0 %collective-permute-start.63 = (bf16[2,4,128,512]{3,2,1,0:T(8,128)(2,1)}, bf16[2,4,128,512]{3,2,1,0:T(8,128)(2,1)}, u32[]{:S(2)}, u32[]{:S(2)}) collective-permute-start(bf16[2,4,128,512]{3,2,1,0:T(8,128)(2,1)} %get-tuple-element.291), channel_id=1, source_target_pairs={{0,8},{4,12},{8,0},{12,4},{16,24},{20,28},{24,16},{28,20},{1,9},{5... | collective-permute-start | bytes 3145736 | tf_op jit(solution)/shard_map/ppermute | solution.py:43
  618.5 31.6 %collective-permute-start.64 = (bf16[2,4,128,512]{3,2,1,0:T(8,128)(2,1)}, bf16[2,4,128,512]{3,2,1,0:T(8,128)(2,1)}, u32[]{:S(2)}, u32[]{:S(2)}) collective-permute-start(bf16[2,4,128,512]{3,2,1,0:T(8,128)(2,1)} %get-tuple-element.292), channel_id=1, source_target_pairs={{0,16},{4,20},{8,24},{12,28},{16,0},{20,4},{24,8},{28,12},{1,17},{... | collective-permute-start | bytes 3145736 | tf_op jit(solution)/shard_map/ppermute | solution.py:43
  622.7 27.4 %collective-permute-start.61 = (bf16[2,1,256,512]{3,2,1,0:T(8,128)(2,1)}, bf16[2,1,256,512]{3,2,1,0:T(8,128)(2,1)S(1)}, u32[]{:S(2)}, u32[]{:S(2)}) collective-permute-start(bf16[2,1,256,512]{3,2,1,0:T(8,128)(2,1)} %get-tuple-element.284), channel_id=1, source_target_pairs={{0,2},{1,3},{2,0},{3,1},{4,6},{5,7},{6,4},{7,5},{8,10},{9,11},{10,... | collective-permute-start | bytes 1572872 | tf_op jit(solution)/shard_map/ppermute | solution.py:43
  650.9 43.4 %collective-permute-start.70 = (bf16[2,4,128,512]{3,2,1,0:T(8,128)(2,1)}, bf16[2,4,128,512]{3,2,1,0:T(8,128)(2,1)S(1)}, u32[]{:S(2)}, u32[]{:S(2)}) collective-permute-start(bf16[2,4,128,512]{3,2,1,0:T(8,128)(2,1)} %get-tuple-element.312), channel_id=1, source_target_pairs={{0,8},{4,12},{8,0},{12,4},{16,24},{20,28},{24,16},{28,20},{1,9},{5... | collective-permute-start | bytes 3145736 | tf_op jit(solution)/shard_map/ppermute | solution.py:43
  651.0 43.4 %collective-permute-start.71 = (bf16[2,4,128,512]{3,2,1,0:T(8,128)(2,1)}, bf16[2,4,128,512]{3,2,1,0:T(8,128)(2,1)S(1)}, u32[]{:S(2)}, u32[]{:S(2)}) collective-permute-start(bf16[2,4,128,512]{3,2,1,0:T(8,128)(2,1)} %get-tuple-element.313), channel_id=1, source_target_pairs={{0,16},{4,20},{8,24},{12,28},{16,0},{20,4},{24,8},{28,12},{1,17},{... | collective-permute-start | bytes 3145736 | tf_op jit(solution)/shard_map/ppermute | solution.py:43
  713.5 25.5 %collective-permute-start.72 = (bf16[4,128,512]{2,1,0:T(8,128)(2,1)}, bf16[4,128,512]{2,1,0:T(8,128)(2,1)S(1)}, u32[]{:S(2)}, u32[]{:S(2)}) collective-permute-start(bf16[4,128,512]{2,1,0:T(8,128)(2,1)} %get-tuple-element.328), channel_id=1, source_target_pairs={{0,16},{4,20},{8,24},{12,28},{16,0},{20,4},{24,8},{28,12},{1,17},{... | collective-permute-start | bytes 1572872 | tf_op jit(solution)/shard_map/ppermute | solution.py:43
  (158 other events, 2103.8 us)
Sparse Core Ops, SparseCore 0:
  11.6 117.6 all-gather.6
  132.7 124.2 all-gather.8
  260.5 114.5 all-gather.10
